TPU v7x, 32 devices: a whole 2x2x4 slice. The times are simulated.
32 devices in a mesh: dp: 8 (over y, x, core), tensor: 4 (over z).
Axes of the slice: x: 2, y: 2, z: 4, core: 2. Of those that a mesh axis runs over, the one named last changes fastest.
Arguments:
- tokens: bfloat16 [20480, 768], P(('dp', 'tensor')), may hold values from -6 to 6
- visible_counts: int32 [256], P('dp'), may hold values from 20 to 78, as said below
- norm_one_gain: float32 [768], replicated, may hold values from 0.1 to 1.9
- norm_one_shift: float32 [768], replicated, may hold values from -1.8 to 1.8
- input_weight: bfloat16 [768, 3, 768], P(None, None, 'tensor'), may hold values from -0.21875 to 0.21875
- input_bias: bfloat16 [2, 768], P(None, 'tensor'), may hold values from -1.796875 to 1.796875
- mixer_weight: bfloat16 [768, 768], P('tensor'), may hold values from -1.25 to 1.25
- mixer_bias: float32 [768], replicated, may hold values from -1.8 to 1.8
- norm_two_gain: float32 [768], replicated, may hold values from 0.1 to 1.9
- norm_two_shift: float32 [768], replicated, may hold values from -1.8 to 1.8
- up_weight: bfloat16 [768, 3072], P(None, 'tensor'), may hold values from -0.21875 to 0.21875
- up_bias: bfloat16 [3072], P('tensor'), may hold values from -1.796875 to 1.796875
- down_weight: bfloat16 [3072, 768], P('tensor'), may hold values from -0.109375 to 0.109375
- down_bias: float32 [768], replicated, may hold values from -1.8 to 1.8
- output_grad: bfloat16 [20480, 768], P(('dp', 'tensor')), may hold values from -6 to 6
Outputs:
- block_output: bfloat16 [20480, 768], P(('dp', 'tensor'))
- grad_tokens: float32 [20480, 768], P(('dp', 'tensor'))
- grad_norm_one_gain: float32 [768], replicated
- grad_norm_one_shift: float32 [768], replicated
- grad_input_weight: float32 [768, 3, 768], P(None, None, 'tensor')
- grad_input_bias: float32 [2, 768], P(None, 'tensor')
- grad_mixer_weight: float32 [768, 768], P('tensor')
- grad_mixer_bias: float32 [768], replicated
- grad_norm_two_gain: float32 [768], replicated
- grad_norm_two_shift: float32 [768], replicated
- grad_up_weight: float32 [768, 3072], P(None, 'tensor')
- grad_up_bias: float32 [3072], P('tensor')
- grad_down_weight: float32 [3072, 768], P('tensor')
- grad_down_bias: float32 [768], replicated
Inputs may be any that keep to these rules, and one draw needn't show every extreme that they name: `visible_counts`: each image has 20 to 78 visible patches; some image has exactly 78 and some exactly 20.
All inputs are finite; a program needn't handle non-finite values.
Results may differ from a plain program's by a relative error of at most 0.014.
Values may be sent and summed in bfloat16 or wider, within the bound.
No kernel may reach another device: no remote copies, remote signals or barrier semaphores. Data moves between devices by JAX's collectives and lax.ppermute only.
A program may use at most 128 MiB of HBM per device.

v0:
```python
import functools

import jax
import jax.numpy as jnp
import numpy as np
from jax import lax
from jax.experimental import pallas as pl
from jax.experimental.pallas import tpu as pltpu
from jax.sharding import PartitionSpec as P

HD = 64
SLOTS = 80
LANES = 128
TILE_IMAGES = 4
MASKED = -1000000000.0
EPS = 1e-06
F32 = jnp.float32
BF16 = jnp.bfloat16

ANY = pl.BlockSpec(memory_space=pl.ANY)
SMEM = pl.BlockSpec(memory_space=pltpu.SMEM)
VMEM = pl.BlockSpec(memory_space=pltpu.VMEM)


def shape(dims, kind):
    return jax.ShapeDtypeStruct(tuple(dims), kind)


def kept(dims, kind):
    return pltpu.HBM(tuple(dims), kind)


def from_hbm(*arrays):
    return tuple(pltpu.with_memory_space_constraint(a, pltpu.HBM) for a in arrays)


def params(megabytes, grid_dims=0):
    semantics = ("arbitrary",) * grid_dims if grid_dims else None
    return pltpu.CompilerParams(
        vmem_limit_bytes=megabytes * 1024 * 1024, dimension_semantics=semantics
    )


def cost(flops, moved):
    return pl.CostEstimate(flops=int(flops), bytes_accessed=int(moved), transcendentals=0)


def dot(left, right):
    return lax.dot_general(left, right, (((1,), (0,)), ((), ())), preferred_element_type=F32)


def dot_rows(left, right):
    return lax.dot_general(left, right, (((1,), (1,)), ((), ())), preferred_element_type=F32)


def dot_columns(left, right):
    return lax.dot_general(left, right, (((0,), (0,)), ((), ())), preferred_element_type=F32)


def centred(rows):
    center = rows - jnp.mean(rows, axis=-1, keepdims=True)
    spread = jnp.mean(center * center, axis=-1, keepdims=True)
    return center, lax.rsqrt(spread + EPS)


def norm_back(rows, gain, grad):
    center, rstd = centred(rows)
    xhat = center * rstd
    e = grad * gain
    back = rstd * (
        e - jnp.mean(e, axis=-1, keepdims=True) - xhat * jnp.mean(e * xhat, axis=-1, keepdims=True)
    )
    return (
        back,
        jnp.sum(grad * xhat, axis=0, keepdims=True),
        jnp.sum(grad, axis=0, keepdims=True),
    )


def norm_one_kernel(images, chunk, place, counts, tokens, gain, shift, out):
    rows = tokens.shape[0]

    @pl.loop(0, rows // chunk)
    def _(step):
        at = pl.ds(pl.multiple_of(step * chunk, chunk), chunk)
        center, rstd = centred(tokens[at, :].astype(F32))
        out[at, :] = (
            center * rstd * gain[...].reshape(1, -1) + shift[...].reshape(1, -1)
        ).astype(BF16)

    extra = out.shape[0] - rows
    row = lax.broadcasted_iota(jnp.int32, (extra, out.shape[1]), 0)
    table = jnp.zeros((extra, out.shape[1]), F32)
    first = place[2] * images
    for image in range(images):
        table = jnp.where(row == image, counts[first + image].astype(F32), table)
    out[rows:, :] = table.astype(BF16)


def norm_one(place, counts, tokens, gain, shift):
    rows, width = tokens.shape
    images = rows // SLOTS
    return pl.pallas_call(
        functools.partial(norm_one_kernel, images, SLOTS),
        out_shape=shape((rows + 16, width), BF16),
        in_specs=[SMEM, SMEM, VMEM, VMEM, VMEM],
        out_specs=VMEM,
        compiler_params=params(16),
        cost_estimate=cost(rows * width * 10, rows * width * 4),
    )(place, counts, tokens, gain, shift)


def norm_two_kernel(tokens, mine, received, bias, gain, shift, first_sum, normed):
    total = tokens[...].astype(F32) + (mine[...] + received[...].astype(F32)) + bias[...]
    first_sum[...] = total
    center, rstd = centred(total)
    normed[...] = (center * rstd * gain[...] + shift[...]).astype(BF16)


def rows_spec(tile, width):
    return pl.BlockSpec((tile, width), lambda i: (i, 0))


def fixed_spec(*dims):
    return pl.BlockSpec(dims, lambda i: (0,) * len(dims))


def norm_two(tokens, mine, received, bias, gain, shift):
    rows, width = tokens.shape
    tile = 2 * SLOTS
    row = rows_spec(tile, width)
    vector = fixed_spec(1, width)
    return pl.pallas_call(
        norm_two_kernel,
        grid=(rows // tile,),
        out_shape=(kept((rows, width), F32), shape((rows, width), BF16)),
        in_specs=[row, row, row, vector, vector, vector],
        out_specs=(row, row),
        compiler_params=params(16, 1),
        cost_estimate=cost(rows * width * 12, rows * width * 14),
    )(*from_hbm(tokens), mine, received, bias, gain, shift)


def added(*refs):
    total = refs[0][...].astype(F32)
    for ref in refs[1:]:
        total = total + ref[...].astype(F32)
    return total


def norm_two_back_kernel(
    part0, part1, part2, part3, first_sum, gain, output_grad, low, sums
):
    grad = added(part0, part1, part2, part3)
    back, grad_gain, grad_shift = norm_back(first_sum[...], gain[...], grad)
    out_grad = output_grad[...].astype(F32)
    total = out_grad + back
    low[...] = total.astype(BF16)

    @pl.when(pl.program_id(0) == 0)
    def _():
        sums[...] = jnp.zeros_like(sums)

    sums[0:1, :] += grad_gain
    sums[1:2, :] += grad_shift
    sums[2:3, :] += jnp.sum(total, axis=0, keepdims=True)
    sums[3:4, :] += jnp.sum(out_grad, axis=0, keepdims=True)


def norm_two_back(parts, first_sum, gain, output_grad):
    rows, width = parts[0].shape
    tile = 2 * SLOTS
    row = rows_spec(tile, width)
    return pl.pallas_call(
        norm_two_back_kernel,
        grid=(rows // tile,),
        out_shape=(shape((rows, width), BF16), shape((8, width), F32)),
        in_specs=[row] * 5 + [fixed_spec(1, width), row],
        out_specs=(row, fixed_spec(8, width)),
        compiler_params=params(16, 1),
        cost_estimate=cost(rows * width * 25, rows * width * 18),
    )(*parts, *from_hbm(first_sum), gain, *from_hbm(output_grad))


def norm_one_back_kernel(
    groups,
    place,
    part0,
    part1,
    part2,
    part3,
    tokens,
    gain,
    grad_first,
    sums_two,
    bias_near,
    bias_far,
    input_near,
    input_far,
    grad_tokens,
    vectors,
):
    grad = added(part0, part1, part2, part3)
    back, grad_gain, grad_shift = norm_back(tokens[...].astype(F32), gain[...], grad)
    grad_tokens[...] = grad_first[...].astype(F32) + back

    @pl.when(pl.program_id(0) == 0)
    def _():
        near = lax.rem(place[2] - 1 - place[1] + groups, groups)
        far = lax.rem(place[2] - 3 * place[1] + groups, groups)
        row = lax.broadcasted_iota(jnp.int32, vectors.shape, 0)
        table = jnp.zeros(vectors.shape, F32)
        for index in range(4):
            table = jnp.where(row == 2 + index, sums_two[index : index + 1, :], table)
        table = jnp.where(row == 6 + near, bias_near[0:1, :], table)
        vectors[...] = jnp.where(row == 6 + far, bias_far[0:1, :], table)
        columns = input_near.shape[1]
        few = lax.broadcasted_iota(jnp.int32, (vectors.shape[0], columns), 0)
        for index in range(2):
            table = jnp.where(
                few == 6 + groups + near, input_near[index : index + 1, :], 0.0
            ) + jnp.where(few == 6 + groups + far, input_far[index : index + 1, :], 0.0)
            vectors[:, index * columns : (index + 1) * columns] += table

    vectors[0:1, :] += grad_gain
    vectors[1:2, :] += grad_shift


def norm_one_back(groups, place, parts, tokens, gain, grad_first, *small):
    rows, width = parts[0].shape
    tile = 2 * SLOTS
    row = rows_spec(tile, width)
    return pl.pallas_call(
        functools.partial(norm_one_back_kernel, groups),
        grid=(rows // tile,),
        out_shape=(kept((rows, width), F32), shape((16, width), F32)),
        in_specs=[SMEM] + [row] * 5 + [fixed_spec(1, width), row]
        + [fixed_spec(*array.shape) for array in small],
        out_specs=(row, fixed_spec(16, width)),
        compiler_params=params(16, 1),
        cost_estimate=cost(rows * width * 25, rows * width * 16),
    )(place, *parts, *from_hbm(tokens), gain, *from_hbm(grad_first), *small)


def pack_attention_kernel(place, projection, mixer, bias, up_bias, out, tail, sem, tail_sem):
    quarter = place[0]
    tail_copy = pltpu.make_async_copy(mixer, tail.at[pl.ds(0, mixer.shape[0])], tail_sem)
    tail_copy.start()
    size = out.shape[0] - 16
    feature_rows = projection.shape[0]
    first = pl.multiple_of(quarter * size, 16)
    from_projection = quarter * size < feature_rows

    @pl.when(from_projection)
    def _():
        copy = pltpu.make_async_copy(
            projection.at[pl.ds(first, size)], out.at[pl.ds(0, size)], sem
        )
        copy.start()
        copy.wait()

    @pl.when(jnp.logical_not(from_projection))
    def _():
        copy = pltpu.make_async_copy(mixer, out.at[pl.ds(0, size)], sem)
        copy.start()
        copy.wait()

    columns = bias.shape[1]
    row = lax.broadcasted_iota(jnp.int32, (16, columns), 0)
    both = bias[...].astype(F32)
    rows = jnp.where(row == 0, both[0:1, :], jnp.where(row == 1, both[1:2, :], 0.0))
    row_all = lax.broadcasted_iota(jnp.int32, (16, out.shape[1]), 0)
    out[size:, :] = jnp.where(row_all == 2, up_bias[...].astype(F32), 0.0).astype(BF16)
    row_two = jnp.where(row == 2, up_bias[:, 0:columns].astype(F32), rows)
    out[size:, 0:columns] = row_two.astype(BF16)
    tail[size:, :] = out[size:, :]
    tail_copy.wait()


def pack_attention(place, projection, mixer, bias, up_bias):
    size, width = mixer.shape
    return pl.pallas_call(
        pack_attention_kernel,
        out_shape=(shape((size + 16, width), BF16),) * 2,
        in_specs=[SMEM, ANY, ANY, VMEM, VMEM],
        out_specs=(VMEM, VMEM),
        scratch_shapes=[pltpu.SemaphoreType.DMA(()), pltpu.SemaphoreType.DMA(())],
        compiler_params=params(16),
        cost_estimate=cost(0, 2 * size * width),
    )(place, *from_hbm(projection, mixer), bias, up_bias)


def pack_hidden_kernel(place, up, down, out, sems):
    size = out.shape[0] // 2
    first = pl.multiple_of(place[0] * size, 16)
    copies = [
        pltpu.make_async_copy(
            source.at[pl.ds(first, size)], out.at[pl.ds(index * size, size)], sems.at[index]
        )
        for index, source in enumerate((up, down))
    ]
    run_copies(copies)


def pack_hidden(place, up, down):
    size, width = up.shape[0] // 4, up.shape[1]
    return pl.pallas_call(
        pack_hidden_kernel,
        out_shape=shape((2 * size, width), BF16),
        in_specs=[SMEM, ANY, ANY],
        out_specs=VMEM,
        scratch_shapes=[pltpu.SemaphoreType.DMA((2,))],
        compiler_params=params(16),
        cost_estimate=cost(0, 4 * size * width),
    )(place, *from_hbm(up, down))


def run_copies(copies):
    for copy in copies:
        copy.start()
    for copy in copies:
        copy.wait()


def make_copies(copies, sems):
    return [
        pltpu.make_async_copy(source, to, sems.at[index])
        for index, (source, to) in enumerate(copies)
    ]


def piece_copies(place, pieces, target, sems):
    size = pieces[0].shape[0] - 16
    copies = []
    for flip, piece in enumerate(pieces):
        to = pl.multiple_of(lax.bitwise_xor(place[0], flip) * size, 16)
        copies.append((piece.at[pl.ds(0, size)], target.at[pl.ds(to, size)]))
    copies.append((pieces[0].at[pl.ds(size, 16)], target.at[pl.ds(4 * size, 16)]))
    return make_copies(copies, sems)


def hidden_copies(place, pieces, bias_piece, target, sems):
    size = pieces[0].shape[0] // 2
    copies = []
    for flip in range(4):
        quarter = lax.bitwise_xor(place[0], flip)
        for matrix in range(2):
            to = pl.multiple_of((4 * matrix + quarter) * size, 16)
            source = pieces[3 + matrix] if flip == 3 else pieces[flip].at[pl.ds(matrix * size, size)]
            copies.append((source, target.at[pl.ds(to, size)]))
    first = bias_piece.shape[0] - 16
    copies.append((bias_piece.at[pl.ds(first, 16)], target.at[pl.ds(8 * size, 16)]))
    return make_copies(copies, sems)


def head_lanes(rows, width):
    return lax.broadcasted_iota(jnp.int32, (rows, width), 1) // HD


def spread_heads(block, lanes, heads):
    gap = jnp.zeros((LANES - SLOTS, block.shape[1]), block.dtype)
    parts = []
    for head in range(heads):
        parts.append(jnp.where(lanes == head, block, jnp.zeros_like(block)))
        parts.append(gap)
    return jnp.concatenate(parts, axis=0)


def gather_heads(product, lanes, heads):
    total = product[0:SLOTS]
    for head in range(1, heads):
        total = jnp.where(lanes == head, product[head * LANES : head * LANES + SLOTS], total)
    return total


def start_on_core(place, own, far, cut, sems):
    copies = [make_copies(cut(parts), sems) for parts in (own, far)]
    for core, some in enumerate(copies):

        @pl.when(place[1] == core)
        def _():
            for copy in some:
                copy.start()

    return copies[0]


def start_far(place, own, far, target, sems):
    def cut(parts):
        size = parts[0].shape[0]
        return [
            (parts[0], target.at[pl.ds(0, size)]),
            (parts[1], target.at[pl.ds(size, parts[1].shape[0])]),
        ]

    return start_on_core(place, own, far, cut, sems)


def start_matrices(place, own, far, target, sems):
    def cut(parts):
        size = parts[0].shape[0]
        bias = parts[2].at[pl.ds(parts[2].shape[0] - 16, 16)]
        return [
            (parts[0], target.at[pl.ds(0, size)]),
            (parts[1], target.at[pl.ds(size, size)]),
            (bias, target.at[pl.ds(2 * size, 16)]),
        ]

    return start_on_core(place, own, far, cut, sems)


def attention_kernel(
    heads,
    place,
    projection,
    tail,
    near0,
    near1,
    near2,
    near3,
    far0,
    far1,
    normed,
    counts,
    *rest,
):
    saved, soft, part, weights, table, sems = rest[-6:]

    @pl.when(pl.program_id(0) == 0)
    def _():
        copies = piece_copies(place, (near0, near1, near2, near3), weights.at[1], sems)
        for copy in copies:
            copy.start()
        far_sems = sems.at[pl.ds(8, 8)]
        copies += start_far(place, (projection, tail), (far0, far1), weights.at[0], far_sems)
        for copy in copies:
            copy.wait()

    cols = heads * HD
    visible_rows = counts[:, 0:LANES].astype(F32)
    for image in range(visible_rows.shape[0]):
        table[image, :, :] = visible_rows[image : image + 1, :]
    rows = normed[...]
    for slot in range(2):
        for index in range(3):
            value = dot_rows(rows, weights[slot, index * cols : (index + 1) * cols, :])
            if index != 1:
                bias_row = 0 if index == 0 else 1
                bias = weights[slot, 4 * cols : 4 * cols + 16, 0:cols].astype(F32)
                value = value + bias[bias_row : bias_row + 1, :]
            saved[4 * slot + index, :, :] = value.astype(BF16)

    lanes = head_lanes(SLOTS, cols)
    key_index = lax.broadcasted_iota(jnp.int32, (SLOTS, LANES), 1).astype(F32)
    first = pl.program_id(0) * TILE_IMAGES

    def one_image(image, carry):
        at = pl.ds(pl.multiple_of(image * SLOTS, 16), SLOTS)
        visible = key_index < table[first + image]
        for slot in range(2):
            queries = saved[4 * slot, at, :]
            keys = spread_heads(saved[4 * slot + 1, at, :], lanes, heads)
            values = spread_heads(saved[4 * slot + 2, at, :], lanes, heads)
            scores = dot_rows(queries, keys) * (HD**-0.5)
            lows = []
            for head in range(heads):
                one = jnp.where(visible, scores[:, head * LANES : (head + 1) * LANES], MASKED)
                exponent = jnp.exp(one - jnp.max(one, axis=-1, keepdims=True))
                total = jnp.sum(exponent, axis=-1, keepdims=True)
                lows.append((exponent / total).astype(BF16))
            low = jnp.concatenate(lows, axis=1)
            soft[at, slot * heads * LANES : (slot + 1) * heads * LANES] = low
            saved[4 * slot + 3, at, :] = dot(low, values).astype(BF16)
        return carry

    lax.fori_loop(0, TILE_IMAGES, one_image, 0, unroll=True)
    total = dot(saved[3, :, :], weights[0, 3 * cols : 4 * cols, :])
    total = total + dot(saved[7, :, :], weights[1, 3 * cols : 4 * cols, :])
    part[...] = total.astype(part.dtype)


def attention(place, own, near, far, normed, before, kind):
    projection, tail = own
    cols, width = projection.shape[0] // 3, projection.shape[1]
    heads = cols // HD
    rows = normed.shape[0] - 16
    tile = TILE_IMAGES * SLOTS
    tiles = rows // tile
    base = tiles if before is None else 0
    extra = () if before is None else from_hbm(*before)
    args = (place, projection, tail, *near, *far, normed, normed, *extra)
    return pl.pallas_call(
        functools.partial(attention_kernel, heads),
        grid=(tiles,),
        out_shape=(
            kept((8, 2 * rows, cols), BF16),
            kept((2 * rows, 2 * heads * LANES), BF16),
            shape((rows, width), kind),
        ),
        in_specs=[SMEM]
        + [ANY] * 8
        + [
            pl.BlockSpec((tile, width), lambda i: (i, 0)),
            pl.BlockSpec((16, width), lambda i: (rows // 16, 0)),
        ]
        + [ANY] * len(extra),
        out_specs=(
            pl.BlockSpec((8, tile, cols), lambda i: (0, base + i, 0)),
            pl.BlockSpec((tile, 2 * heads * LANES), lambda i: (base + i, 0)),
            pl.BlockSpec((tile, width), lambda i: (i, 0)),
        ),
        scratch_shapes=[
            pltpu.VMEM((2, 4 * cols + 16, width), BF16),
            pltpu.VMEM((16, 1, LANES), F32),
            pltpu.SemaphoreType.DMA((16,)),
        ],
        input_output_aliases={11: 0, 12: 1} if extra else {},
        compiler_params=params(20, 1),
        cost_estimate=cost(rows * width * cols * 16 + rows * 400000, rows * width * 10 + 5e6),
    )(*args)


def attention_back_kernel(heads, far, place, *rest):
    count = 4
    pieces, rest = rest[:count], rest[count:]
    normed_mine, normed_other, grad_mine, grad_other, saved, soft = rest[:6]
    rest = rest[6:]
    keep, send_x, send_y, send_xy, bias_sums = rest[:5]
    rest = rest[5:]
    back_mine, back_other, weights, sums, grads, sems = rest
    step = pl.program_id(0)
    steps = pl.num_programs(0)
    cols = heads * HD
    mine = step < steps // 2

    @pl.when(step == 0)
    def _():
        if far:
            copies = start_far(place, pieces[:2], pieces[2:], weights, sems)
        else:
            copies = piece_copies(place, pieces, weights, sems)
            for copy in copies:
                copy.start()
        for copy in copies:
            copy.wait()
        sums[...] = jnp.zeros_like(sums)
        bias_sums[...] = jnp.zeros_like(bias_sums)

    normed = jnp.where(mine, normed_mine[...], normed_other[...])
    grad = jnp.where(mine, grad_mine[...], grad_other[...])
    grads[3, :, :] = dot_rows(grad, weights[3 * cols : 4 * cols, :]).astype(BF16)
    lanes = head_lanes(SLOTS, cols)

    def one_image(image, carry):
        at = pl.ds(pl.multiple_of(image * SLOTS, 16), SLOTS)
        queries = saved[0, at, :]
        keys = spread_heads(saved[1, at, :], lanes, heads)
        values = spread_heads(saved[2, at, :], lanes, heads)
        grad_mixed = grads[3, at, :]
        low = soft[at, :]
        grad_soft = dot_rows(grad_mixed, values)
        lows = []
        for head in range(heads):
            one = low[:, head * LANES : (head + 1) * LANES].astype(F32)
            grad_one = grad_soft[:, head * LANES : (head + 1) * LANES]
            inner = jnp.sum(grad_one * one, axis=-1, keepdims=True)
            lows.append((one * (grad_one - inner) * (HD**-0.5)).astype(BF16))
        grad_scores = jnp.concatenate(lows, axis=1)
        grad_queries = dot(grad_scores, keys)
        grad_values = gather_heads(dot_columns(low, grad_mixed), lanes, heads)
        grad_keys = gather_heads(dot_columns(grad_scores, queries), lanes, heads)
        bias_sums[0:1, :] += jnp.sum(grad_queries, axis=0, keepdims=True)
        bias_sums[1:2, :] += jnp.sum(grad_values, axis=0, keepdims=True)
        grads[0, at, :] = grad_queries.astype(BF16)
        grads[1, at, :] = grad_keys.astype(BF16)
        grads[2, at, :] = grad_values.astype(BF16)
        return carry

    lax.fori_loop(0, TILE_IMAGES, one_image, 0, unroll=True)
    back = None
    for index in range(3):
        at = slice(index * cols, (index + 1) * cols)
        value = grads[index, :, :]
        term = dot(value, weights[at, :])
        back = term if back is None else back + term
        sums[at, :] += dot_columns(value, normed)
    sums[3 * cols : 4 * cols, :] += dot_columns(saved[3, :, :], grad)

    @pl.when(mine)
    def _():
        back_mine[...] = back.astype(BF16)

    @pl.when(jnp.logical_not(mine))
    def _():
        back_other[...] = back.astype(BF16)

    @pl.when(step == steps - 1)
    def _():
        size = keep.shape[2]
        for flip, ref in enumerate((keep, send_x, send_y, send_xy)):
            quarter = lax.bitwise_xor(place[0], flip)
            for half in range(2):
                at = pl.ds(pl.multiple_of((2 * quarter + half) * size, 16), size)
                ref[half, 0, :, :] = sums[at, :].astype(BF16)


def half_spec(tile, width, tiles, second):
    if second:
        return pl.BlockSpec((tile, width), lambda i: (jnp.maximum(i - tiles, 0), 0))
    return pl.BlockSpec((tile, width), lambda i: (jnp.minimum(i, tiles - 1), 0))


def attention_back(place, slot, own, pieces, normed, grads, saved, soft):
    rows, width = grads[0].shape
    cols = saved.shape[2]
    heads = cols // HD
    tile = TILE_IMAGES * SLOTS
    tiles = rows // tile
    far = own is not None
    mine, other = half_spec(tile, width, tiles, False), half_spec(tile, width, tiles, True)
    dims = (2, 1, cols // 2, width)
    weights = (*own, *pieces) if far else pieces
    return pl.pallas_call(
        functools.partial(attention_back_kernel, heads, far),
        grid=(2 * tiles,),
        out_shape=(
            *(shape(dims, BF16),) * 4,
            shape((8, cols), F32),
            shape((rows, width), BF16),
            shape((rows, width), BF16),
        ),
        in_specs=[SMEM]
        + [ANY] * 4
        + [
            mine,
            other,
            mine,
            other,
            pl.BlockSpec((4, tile, cols), lambda i: (slot, i, 0)),
            pl.BlockSpec((tile, heads * LANES), lambda i: (i, slot)),
        ],
        out_specs=(*(fixed_spec(*dims),) * 4, fixed_spec(8, cols), mine, other),
        scratch_shapes=[
            pltpu.VMEM((4 * cols + 16, width), BF16),
            pltpu.VMEM((4 * cols, width), F32),
            pltpu.VMEM((4, tile, cols), BF16),
            pltpu.SemaphoreType.DMA((16,)),
        ],
        compiler_params=params(24, 1),
        cost_estimate=cost(rows * width * cols * 30 + rows * 6e5, rows * width * 20 + 4e6),
    )(place, *weights, *normed, *grads, *from_hbm(saved, soft))


def hidden_kernel(last, place, *rest):
    pieces, rest = rest[:6], rest[6:]
    normed_parts, grad_parts, rest = rest[:2], rest[2:4], rest[4:]
    if last:
        whole_grads, rest = rest[0], rest[1:]
    else:
        (send_x, send_y, keep_x, keep_y), rest = rest[:4], rest[4:]
    bias_sums, out_mine, out_other, back_mine, back_other = rest[:5]
    rest = rest[5:]
    weights, normed, grad, active, grad_low, sums_up, sums_down, summed = rest[:8]
    piece_sems, sems, out_sems = rest[8:]
    rows, width = normed.shape
    half = rows // 2

    def load(first, parts, target):
        return [
            pltpu.make_async_copy(part, target.at[pl.ds(index * half, half)], sems.at[first + index])
            for index, part in enumerate(parts)
        ]

    normed_copies, grad_copies = load(0, normed_parts, normed), load(2, grad_parts, grad)
    for copy in normed_copies:
        copy.start()
    if last:
        starts = start_matrices(place, pieces[:3], pieces[3:], weights, piece_sems)
        first_needed, then_needed = [starts[0], starts[2]], [starts[1]]
    else:
        starts = hidden_copies(place, pieces[:5], pieces[5], weights, piece_sems)
        first_needed, then_needed = starts[0:8:2] + [starts[8]], starts[1:8:2]
        for copy in first_needed + then_needed:
            copy.start()
    for copy in grad_copies:
        copy.start()
    for copy in normed_copies + first_needed:
        copy.wait()

    bias = weights[2 * width : 2 * width + 16, :].astype(F32)[2:3, :]
    chunk = 256
    chunks = [slice(first, first + chunk) for first in range(0, width, chunk)]

    def weight_sums(at):
        sums_up[:, at] = dot_columns(normed[...], grad_low[:, at]).astype(BF16)
        sums_down[at, :] = dot_columns(active[:, at], grad[...]).astype(BF16)

    for index, at in enumerate(chunks):
        hidden = dot(normed[...], weights[0:width, at]) + bias[:, at]
        if index == 0:
            for copy in grad_copies + then_needed:
                copy.wait()
        phi = 0.5 + 0.5 * lax.erf(hidden * (0.5**0.5))
        slope = phi + hidden * (jnp.exp(-0.5 * hidden * hidden) * ((2.0 * np.pi) ** -0.5))
        active[:, at] = (hidden * phi).astype(BF16)
        down_rows = weights[width + at.start : width + at.stop, :]
        grad_pre = dot_rows(grad[...], down_rows) * slope
        bias_sums[0:1, at] = jnp.sum(grad_pre, axis=0, keepdims=True)
        grad_low[:, at] = grad_pre.astype(BF16)
        if index:
            weight_sums(chunks[index - 1])
    weight_sums(chunks[-1])

    size = sums_up.shape[0] // 8
    copies = []
    for flip in range(4):
        quarter = lax.bitwise_xor(place[0], flip)
        for part in range(2):
            at = pl.ds(pl.multiple_of((2 * quarter + part) * size, 16), size)
            for matrix, source in enumerate((sums_up, sums_down)):
                if last:
                    target = whole_grads.at[part, flip, matrix]
                elif part == 0:
                    target = (keep_x if flip % 2 == 0 else send_x).at[flip // 2, matrix]
                else:
                    target = (keep_y if flip < 2 else send_y).at[flip % 2, matrix]
                sem = piece_sems.at[len(copies)]
                copies.append(pltpu.make_async_copy(source.at[at], target, sem))
    for copy in copies:
        copy.start()
    targets = ((out_mine, out_other), (back_mine, back_other))

    def out_copy(index, part, first, sem):
        target = targets[index][part]
        source = summed.at[index, pl.ds(part * half, target.shape[0]), pl.ds(first, chunk)]
        return pltpu.make_async_copy(source, target.at[:, pl.ds(first, chunk)], sem)

    def finish_chunk(step, carry):
        first = pl.multiple_of(step * chunk, chunk)
        at = pl.ds(first, chunk)
        back = dot_rows(grad_low[...], weights[at, :])
        out = dot(active[...], weights[width : 2 * width, at])
        for index, value in enumerate((out, back)):
            summed[index, :, at] = value.astype(BF16)
            for part in range(2):
                out_copy(index, part, first, out_sems.at[step, index, part]).start()
        return carry

    lax.fori_loop(0, len(chunks), finish_chunk, 0)
    for step in range(len(chunks)):
        for index in range(2):
            for part in range(2):
                out_copy(index, part, step * chunk, out_sems.at[step, index, part]).wait()
    for copy in copies:
        copy.wait()


def hidden_block(place, pieces, normed, grads, last):
    rows, width = normed[0].shape
    size = width // 8
    if last:
        grad_shapes = (kept((2, 4, 2, size, width), BF16),)
    else:
        grad_shapes = (kept((2, 2, size, width), BF16),) * 4
    return pl.pallas_call(
        functools.partial(hidden_kernel, last),
        out_shape=(
            *grad_shapes,
            shape((8, width), F32),
            kept((rows, width), BF16),
            kept((rows, width), BF16),
            kept((rows, width), BF16),
            kept((rows, width), BF16),
        ),
        in_specs=[SMEM] + [ANY] * 10,
        out_specs=(ANY,) * len(grad_shapes) + (VMEM,) + (ANY,) * 4,
        scratch_shapes=[
            pltpu.VMEM((2 * width + 16, width), BF16),
            pltpu.VMEM((2 * rows, width), BF16),
            pltpu.VMEM((2 * rows, width), BF16),
            pltpu.VMEM((2 * rows, width), BF16),
            pltpu.VMEM((2 * rows, width), BF16),
            pltpu.VMEM((width, width), BF16),
            pltpu.VMEM((width, width), BF16),
            pltpu.VMEM((2, 2 * rows, width), BF16),
            pltpu.SemaphoreType.DMA((16,)),
            pltpu.SemaphoreType.DMA((4,)),
            pltpu.SemaphoreType.DMA((width // 256, 2, 2)),
        ],
        compiler_params=params(44),
        cost_estimate=cost(rows * width * width * 24, rows * width * 24 + 8e6),
    )(place, *pieces, *from_hbm(*normed, *grads))


def first_sums_kernel(keep_x, keep_y, got_x, got_y, send_y, send_x, base):
    add = lambda u, v: u.astype(F32) + v.astype(F32)
    base[0] = add(keep_x[0], got_x[0])
    base[1] = add(keep_y[0], got_y[0])
    send_y[...] = add(keep_x[1], got_x[1]).astype(BF16)
    send_x[...] = add(keep_y[1], got_y[1]).astype(BF16)


def plane_sums_kernel(base, next_y, next_x, plane):
    plane[0] = (base[0] + next_y[...].astype(F32)).astype(BF16)
    plane[1] = (base[1] + next_x[...].astype(F32)).astype(BF16)


def depth_sums_kernel(core, local_far, far, near, keep, send):
    halves = []
    for half in range(2):
        first = jnp.where(core == 0, local_far[half], far[half])
        halves.append(first.astype(F32) + near[half].astype(F32))
    keep[...] = jnp.where(core == 0, halves[0], halves[1])
    send[...] = jnp.where(core == 0, halves[1], halves[0]).astype(BF16)


def pair_send_kernel(core, own, got, send):
    send[...] = jnp.where(core == 0, own[1], got[0])


def pair_sums_kernel(core, own, got, received, keep, send_x, send_y, send_xy):
    for flip, ref in enumerate((keep, send_x, send_y, send_xy)):
        half = jnp.where(core == 0, own[0, flip], got[1, flip])
        ref[...] = (half.astype(F32) + received[flip].astype(F32)).astype(BF16)


def half_split_kernel(core, both, keep, send):
    keep[...] = jnp.where(core == 0, both[0], both[1])
    send[...] = jnp.where(core == 0, both[1], both[0])


def last_sums_kernel(keep, received, *rest):
    total = rest[-1]
    total[0:1] = (keep[...] + received[...].astype(F32)).astype(BF16)
    both = rest[0][...].astype(F32)
    for ref in rest[1:-1]:
        both = both + ref[...].astype(F32)
    total[1:3] = both.astype(BF16)


def total_kernel(*refs):
    total = refs[0][...].astype(F32)
    for ref in refs[1:-1]:
        total = total + ref[...].astype(F32)
    refs[-1][...] = total.astype(refs[-1].dtype)


def sums_kernel(parts, place, *refs):
    ins = sum(count for _, count, _ in parts)
    in_refs, out_refs = refs[:ins], refs[ins:]
    for body, count, outs in parts:
        mine, in_refs = in_refs[:count], in_refs[count:]
        results, out_refs = out_refs[:outs], out_refs[outs:]
        with_core = (depth_sums_kernel, pair_send_kernel, pair_sums_kernel, half_split_kernel)
        lead = (place[1],) if body in with_core else ()
        rows = mine[0].shape[-2]
        chunk = 32 if rows % 32 == 0 else 16

        @pl.loop(0, rows // chunk)
        def _(step):
            at = pl.ds(pl.multiple_of(step * chunk, chunk), chunk)
            views = [
                ref.at[(slice(None),) * (len(ref.shape) - 2) + (at, slice(None))]
                for ref in (*mine, *results)
            ]
            body(*lead, *views)


def sums(place, *work):
    parts, args, out_shapes = [], [], []
    for body, arrays in work:
        like = arrays[0].shape
        if body is first_sums_kernel:
            outs = [shape(like[1:], BF16), shape(like[1:], BF16), shape(like, F32)]
        elif body is plane_sums_kernel:
            outs = [shape(like, BF16)]
        elif body is pair_send_kernel:
            outs = [shape(like[1:], BF16)]
        elif body is pair_sums_kernel:
            outs = [shape(like[2:], BF16)] * 4
        elif body is half_split_kernel:
            outs = [shape(like[1:], BF16)] * 2
        elif body is depth_sums_kernel:
            outs = [shape(like[1:], F32), shape(like[1:], BF16)]
        else:
            dims = (3, *like[1:]) if body is last_sums_kernel else like
            outs = [shape(dims, arrays[0].dtype if body is total_kernel else BF16)]
        parts.append((body, len(arrays), len(outs)))
        args += arrays
        out_shapes += outs
    moved = sum(4 * np.prod(o.shape) for o in out_shapes)
    results = pl.pallas_call(
        functools.partial(sums_kernel, tuple(parts)),
        out_shape=tuple(out_shapes),
        in_specs=[SMEM] + [VMEM] * len(args),
        out_specs=(VMEM,) * len(out_shapes),
        compiler_params=params(16),
        cost_estimate=cost(0, moved),
    )(place, *args)
    grouped = []
    for _, _, count in parts:
        grouped.append(tuple(results[:count]))
        results = results[count:]
    return grouped


def finish_kernel(side, place, *refs):
    parts, outs, wide, sems = refs[:4], refs[-6:-2], refs[-2], refs[-1]
    matrices, half = parts[0].shape[:2]
    grad_input, grad_mixer = outs[:2]
    part = place[1] if side == 0 else 1 - place[1]
    copies = []
    for flip in range(4):
        quarter = lax.bitwise_xor(place[0], flip)
        at = pl.ds(pl.multiple_of((2 * quarter + part) * half, 8), half)
        for matrix in range(matrices):
            source, sem = wide.at[flip, matrix], sems.at[flip, matrix]

            @pl.loop(0, half // 16)
            def _(step):
                rows = pl.ds(pl.multiple_of(step * 16, 16), 16)
                wide[flip, matrix, rows, :] = parts[flip][matrix, rows, :].astype(F32)

            if matrix:
                copies.append(pltpu.make_async_copy(source, outs[1 + matrix].at[at], sem))
                copies[-1].start()
                continue
            rows = pl.ds(pl.multiple_of(part * half, 8), half)
            copies.append(pltpu.make_async_copy(source, grad_mixer.at[rows], sem))

            @pl.when(quarter < 3)
            def _():
                pltpu.make_async_copy(source, grad_input.at[at], sem).start()

            @pl.when(quarter == 3)
            def _():
                copies[-1].start()

    for copy in copies:
        copy.wait()


def finish(place, parts, side, before):
    matrices, half, width = parts[0].shape
    extra = before or ()
    return pl.pallas_call(
        functools.partial(finish_kernel, side),
        out_shape=tuple(kept((count * half, width), F32) for count in (6, 2, 8, 8)),
        in_specs=[SMEM] + [VMEM] * 4 + [ANY] * len(extra),
        out_specs=(ANY,) * 4,
        scratch_shapes=[
            pltpu.VMEM((4, matrices, half, width), F32),
            pltpu.SemaphoreType.DMA((4, matrices)),
        ],
        input_output_aliases={5 + index: index for index in range(len(extra))},
        compiler_params=params(12),
        cost_estimate=cost(0, half * width * 72),
    )(place, *parts, *extra)


def local(
    tokens,
    visible_counts,
    norm_one_gain,
    norm_one_shift,
    input_weight,
    input_bias,
    mixer_weight,
    mixer_bias,
    norm_two_gain,
    norm_two_shift,
    up_weight,
    up_bias,
    down_weight,
    down_bias,
    output_grad,
    groups,
    outer,
):
    width = tokens.shape[1]
    rows = tokens.shape[0]
    cols = mixer_weight.shape[0]
    t = lax.axis_index("t")
    core = lax.axis_index("c")
    place = jnp.stack([2 * lax.axis_index("a") + lax.axis_index("b"), core, t]).astype(jnp.int32)
    one_row = lambda v: v.reshape(1, -1)

    swap = [(0, 1), (1, 0)]
    cross = [(0, 3), (1, 2), (2, 1), (3, 0)]
    to_near = [(z, (z + 1) % groups) for z in range(groups)] + [
        (groups + z, groups + (z + 2) % groups) for z in range(groups)
    ]
    to_far = [(groups + z, groups + (z + 3) % groups) for z in range(groups)]
    home_near = [(j, i) for i, j in to_near]
    home_far = [(j, i) for i, j in to_far]

    def spread(piece):
        return (
            piece,
            lax.ppermute(piece, "b", swap),
            lax.ppermute(piece, "a", swap),
            lax.ppermute(piece, ("a", "b"), cross),
        )

    def together(*groups):
        return lax.optimization_barrier(groups)

    def after(value, *others):
        return lax.optimization_barrier((value, *others))[0]

    def first_exchange(send_x, send_y, keep_x, keep_y):
        got_x = lax.ppermute(send_x, "b", swap)
        got_y = lax.ppermute(send_y, "a", swap)
        return keep_x, keep_y, got_x, got_y

    def second_exchange(send_y, send_x, base):
        return base, lax.ppermute(send_y, "a", swap), lax.ppermute(send_x, "b", swap)

    def direct(keep, send_x, send_y, send_xy):
        return (
            keep,
            lax.ppermute(send_x, "b", swap),
            lax.ppermute(send_y, "a", swap),
            lax.ppermute(send_xy, ("a", "b"), cross),
        )

    def over_outer(value):
        return lax.psum(value.astype(F32), "o").astype(BF16) if outer > 1 else value

    projection = input_weight.transpose(1, 2, 0).reshape(3 * cols, width)
    normed_one = norm_one(
        place,
        visible_counts,
        tokens,
        norm_one_gain,
        norm_one_shift,
    )
    piece_one, tail_one = pack_attention(
        place, projection, mixer_weight, after(input_bias, normed_one), one_row(up_bias)
    )
    depth_near_one = lax.ppermute(piece_one, ("c", "t"), to_near)
    normed_other = lax.ppermute(normed_one, "c", swap)
    piece_two = pack_hidden(place, up_weight, down_weight)
    depth_near_one, normed_other, piece_two = together(depth_near_one, normed_other, piece_two)
    near_one = spread(depth_near_one)
    far_projection = lax.ppermute(after(projection, depth_near_one), ("c", "t"), to_far)
    far_mixer = lax.ppermute(after(tail_one, depth_near_one), ("c", "t"), to_far)
    near_two = lax.ppermute(after(piece_two, far_mixer, *near_one), ("c", "t"), to_near)

    own_one = (projection, tail_one)
    far_one = (far_projection, far_mixer)
    saved, soft, part = attention(place, own_one, near_one, far_one, normed_other, None, BF16)
    saved, soft, part, near_two = together(saved, soft, part, near_two)
    grad_other = lax.ppermute(after(output_grad, part), "c", swap)
    part_received = lax.ppermute(part, "c", swap)
    near_x = lax.ppermute(near_two, "b", swap)
    near_y = lax.ppermute(near_two, "a", swap)
    far_up = lax.ppermute(after(up_weight, near_two), ("c", "t"), to_far)
    saved, soft, part = attention(
        place, own_one, near_one, far_one, normed_one, (saved, soft), F32
    )
    part, part_received, near_x, near_y, far_up, grad_other = together(
        part, part_received, near_x, near_y, far_up, grad_other
    )
    quarter = near_two.shape[0] // 2
    near_up = lax.ppermute(near_y[:quarter], "b", swap)
    near_down = lax.ppermute(near_x[quarter:], "a", swap)
    first_sum, normed_two = norm_two(
        tokens,
        part,
        part_received,
        one_row(mixer_bias),
        one_row(norm_two_gain),
        one_row(norm_two_shift),
    )
    normed_two, first_sum, near_up, near_down = together(
        normed_two, first_sum, near_up, near_down
    )
    normed_two_other = lax.ppermute(normed_two, "c", swap)
    far_down = lax.ppermute(after(down_weight, far_up), ("c", "t"), to_far)
    normed_two_both = (normed_two, normed_two_other)

    grad_both = (output_grad, grad_other)
    pieces = (near_two, near_x, near_y, near_up, near_down, depth_near_one)
    near_outs = hidden_block(place, pieces, normed_two_both, grad_both, False)
    near_outs, far_down = together(near_outs, far_down)
    *grads_near, bias_near, out_near, out_send, back_near, back_send = near_outs
    stage_near = first_exchange(*grads_near)
    back_near_received = lax.ppermute(back_send, "c", swap)
    out_near_received = lax.ppermute(out_send, "c", swap)
    shards = (up_weight, down_weight, tail_one, far_up, far_down, far_mixer)
    far_outs = hidden_block(place, shards, normed_two_both, grad_both, True)
    far_outs, stage_near, back_near_received, out_near_received = together(
        far_outs, stage_near, back_near_received, out_near_received
    )
    grads_far, bias_far, out_far, out_send, back_far_mine, back_send = far_outs

    got_far = lax.ppermute(grads_far, ("c", "t"), home_far)
    back_received = lax.ppermute(back_send, "c", swap)
    (stage_near,) = sums(place, (first_sums_kernel, stage_near))
    back_received = after(back_received, *stage_near)
    stage_near = second_exchange(*stage_near)
    grad_first_low, sums_two = norm_two_back(
        (back_near, back_near_received, back_far_mine, back_received),
        first_sum,
        one_row(norm_two_gain),
        output_grad,
    )
    first_other = lax.ppermute(grad_first_low, "c", swap)
    out_received = lax.ppermute(after(out_send, first_other), "c", swap)

    normed_both = (normed_one, normed_other)
    first_both = (grad_first_low, first_other)
    *grads_one_near, bias_one_near, back_near, back_send = attention_back(
        place, 1, None, near_one, normed_both, first_both, saved, soft
    )
    grads_one_near, back_near, back_send, stage_near, got_far, out_received = together(
        grads_one_near, back_near, back_send, stage_near, got_far, out_received
    )
    one_near = direct(*grads_one_near)
    (plane_near,), (send_far,) = sums(
        place, (plane_sums_kernel, stage_near), (pair_send_kernel, (grads_far, got_far))
    )
    depth_near = lax.ppermute(plane_near, ("c", "t"), home_near)
    received_far = lax.ppermute(send_far, "c", swap)
    back_near_send = after(back_send, received_far)
    grad_low_late = after(grad_first_low, plane_near)
    *grads_one_far, bias_one_far, back_far_mine, back_send = attention_back(
        place, 0, own_one, far_one, normed_both, (grad_low_late, first_other), saved, soft
    )
    grads_one_far, back_far_mine, back_send, one_near, received_far, depth_near = together(
        grads_one_far, back_far_mine, back_send, one_near, received_far, depth_near
    )
    back_near_received = lax.ppermute(back_near_send, "c", swap)

    one_far = direct(*grads_one_far)
    back_received = lax.ppermute(back_send, "c", swap)
    (one_near,), sums_far, (keep_two, send_two) = sums(
        place,
        (total_kernel, one_near),
        (pair_sums_kernel, (grads_far, got_far, received_far)),
        (half_split_kernel, (depth_near,)),
    )
    one_depth_near = lax.ppermute(one_near, ("c", "t"), home_near)
    received_two = lax.ppermute(send_two, "c", swap)
    grad_tokens, vectors = norm_one_back(
        groups,
        place,
        (back_near, back_near_received, back_far_mine, back_received),
        tokens,
        one_row(norm_one_gain),
        grad_first_low,
        sums_two,
        bias_near,
        bias_far,
        bias_one_near,
        bias_one_far,
    )
    vectors_core = lax.ppermute(vectors, "c", swap)
    vectors_core, one_far, received_two = together(vectors_core, one_far, received_two)
    (one_far,), (vectors,) = sums(
        place, (total_kernel, one_far), (total_kernel, (vectors, vectors_core))
    )
    one_depth_far = lax.ppermute(one_far, ("c", "t"), home_far)
    sums_far = direct(*sums_far)
    result = (
        first_sum
        + (out_near.astype(F32) + out_near_received.astype(F32))
        + (out_far.astype(F32) + out_received.astype(F32))
        + down_bias
    ).astype(BF16)
    one_depth_far, one_depth_near, result = together(one_depth_far, one_depth_near, result)
    ((keep_one, send_one),) = sums(
        place, (depth_sums_kernel, (one_far, one_depth_far, one_depth_near))
    )
    received_one = lax.ppermute(send_one, "c", swap)
    vectors_plane = spread(vectors)
    received_one, vectors_plane, sums_far = together(received_one, vectors_plane, sums_far)
    (parts,), (vectors,) = sums(
        place,
        (last_sums_kernel, (keep_one, received_one, *sums_far, keep_two, received_two)),
        (total_kernel, vectors_plane),
    )
    mine = spread(over_outer(parts))
    turns = [
        lax.ppermute(vectors, "t", [(z, (z + k) % groups) for z in range(groups)])
        for k in range(1, groups)
    ]
    vectors = sum(turns, vectors)
    if outer > 1:
        vectors = lax.psum(vectors, "o")
    grad_up_bias = lax.dynamic_slice_in_dim(vectors, 6 + t, 1)[0]
    grad_input_bias = lax.dynamic_slice_in_dim(vectors, 6 + groups + t, 1).reshape(-1, cols)[:2]
    rows_out = [vectors[index] for index in range(6)]
    mine, rows_out, grad_up_bias, grad_input_bias = together(
        mine, rows_out, grad_up_bias, grad_input_bias
    )
    other = tuple(lax.ppermute(part, "c", swap) for part in mine)
    half_done = finish(place, mine, 0, None)
    other, half_done = together(other, half_done)
    grad_input, grad_mixer, grad_up, grad_down = finish(place, other, 1, half_done)
    grad_input = grad_input.reshape(3, cols, width).transpose(2, 0, 1)
    return (
        result,
        grad_tokens,
        rows_out[0],
        rows_out[1],
        grad_input,
        grad_input_bias,
        grad_mixer,
        rows_out[4],
        rows_out[2],
        rows_out[3],
        grad_up,
        grad_up_bias,
        grad_down,
        rows_out[5],
    )


def solution(mesh):
    dp, groups = mesh.shape["dp"], mesh.shape["tensor"]
    outer = dp // 8
    split = jax.sharding.Mesh(
        mesh.devices.reshape(outer, 2, 2, 2, groups), ("o", "a", "b", "c", "t")
    )
    dp_axes = ("o", "a", "b", "c")
    all_axes = dp_axes + ("t",)
    in_specs = (
        P(all_axes, None),
        P(dp_axes),
        P(),
        P(),
        P(None, None, "t"),
        P(None, "t"),
        P("t", None),
        P(),
        P(),
        P(),
        P(None, "t"),
        P("t"),
        P("t", None),
        P(),
        P(all_axes, None),
    )
    out_specs = (
        P(all_axes, None),
        P(all_axes, None),
        P(),
        P(),
        P(None, None, "t"),
        P(None, "t"),
        P("t", None),
        P(),
        P(),
        P(),
        P(None, "t"),
        P("t"),
        P("t", None),
        P(),
    )
    return jax.shard_map(
        functools.partial(local, groups=groups, outer=outer),
        mesh=split,
        in_specs=in_specs,
        out_specs=out_specs,
        check_vma=False,
    )
```

profile of v0, /device:TPU:0, one launch (start us, length us, event | category | flops | bytes accessed | tf_op | source)
XLA Modules:
  0.0 250.1 jit_solution(4202849220765050084)
XLA Ops:
  0.8 1.2 copy-done.1
  4.0 2.2 shard_map.254.normed.counts.rest_4_
  6.8 1.6 shard_map.255
  8.4 2.7 %collective-permute-start = (bf16[208,768]{1,0:T(8,128)(2,1)S(1)}, bf16[208,768]{1,0:T(8,128)(2,1)S(1)}, u32[]{:S(2)}, u32[]{:S(2)}) collective-permute-start(bf16[208,768]{1,0:T(8,128)(2,1)S(1)} %get-tuple-element.195), channel_id=1, source_target_pairs={{0,1},{1,2},{2,3},{3,0},{4,6},{5,7},{6,4},{7,5},{8,9},{9,10},{10,1... | collective-permute-start | bytes 958472 | tf_op jit(solution)/shard_map/ppermute | solution.py:1041
  11.0 1.6 shard_map.256
  12.7 8.7 %collective-permute-done.near0.rest_5_.rest_0_ = bf16[208,768]{1,0:T(8,128)(2,1)S(1)} collective-permute-done((bf16[208,768]{1,0:T(8,128)(2,1)S(1)}, bf16[208,768]{1,0:T(8,128)(2,1)S(1)}, u32[]{:S(2)}, u32[]{:S(2)}) %collective-permute-start) | collective-permute-done | bytes 319520 | tf_op jit(solution)/shard_map/ppermute | solution.py:1041
  23.0 1.6 collective-permute-start.2
  24.5 1.5 collective-permute-start.3
  26.5 3.5 %collective-permute-done.2.near1.rest_1_ = bf16[208,768]{1,0:T(8,128)(2,1)S(1)} collective-permute-done((bf16[208,768]{1,0:T(8,128)(2,1)S(1)}, bf16[208,768]{1,0:T(8,128)(2,1)S(1)}, u32[]{:S(2)}, u32[]{:S(2)}) %collective-permute-start.2) | collective-permute-done | bytes 319520 | tf_op jit(solution)/shard_map/ppermute | solution.py:1000
  30.0 5.2 %collective-permute-done.3.near2.rest_2_ = bf16[208,768]{1,0:T(8,128)(2,1)S(1)} collective-permute-done((bf16[208,768]{1,0:T(8,128)(2,1)S(1)}, bf16[208,768]{1,0:T(8,128)(2,1)S(1)}, u32[]{:S(2)}, u32[]{:S(2)}) %collective-permute-start.3) | collective-permute-done | bytes 319520 | tf_op jit(solution)/shard_map/ppermute | solution.py:1001
  35.3 2.2 collective-permute-start.7
  37.4 10.2 %shard_map.257 = (bf16[8,1280,192]{2,1,0:T(8,128)(2,1)}, bf16[1280,768]{1,0:T(8,128)(2,1)}, bf16[640,768]{1,0:T(8,128)(2,1)S(1)}) custom-call(s32[3]{0:T(128)S(1)} %pad_add_fusion.place, bf16[576,768]{1,0:T(8,128)(2,1)S(1)} %bitcast.11, bf16[208,768]{1,0:T(8,128)(2,1)S(1)} %get-tuple-element.200.tail.rest_2_.rest_1_, ...), custom_call_target="tpu_custom_call" | custom-call | flops 1765949440 | bytes 9915200 | tf_op jit(solution)/shard_map/pallas_call | solution.py:492
  47.6 2.2 collective-permute-done.7.rest_0_
  50.7 18.0 %collective-permute-start.12 = (bf16[640,768]{1,0:T(8,128)(2,1)S(1)}, bf16[640,768]{1,0:T(8,128)(2,1)S(1)}, u32[]{:S(2)}, u32[]{:S(2)}) collective-permute-start(bf16[640,768]{1,0:T(8,128)(2,1)S(1)} %copy-done.17), channel_id=1, source_target_pairs={{0,4},{4,0},{1,5},{5,1},{2,6},{6,2},{3,7},{7,3},{8,12},{12,8},{9,1... | collective-permute-start | bytes 2949128 | tf_op jit(solution)/shard_map/ppermute | solution.py:1054
  69.6 2.2 collective-permute-start.9
  71.7 10.2 %shard_map.258 = (bf16[8,1280,192]{2,1,0:T(8,128)(2,1)}, bf16[1280,768]{1,0:T(8,128)(2,1)}, f32[640,768]{1,0:T(8,128)S(1)}) custom-call(s32[3]{0:T(128)S(1)} %pad_add_fusion.place, bf16[576,768]{1,0:T(8,128)(2,1)S(1)} %bitcast.12, bf16[208,768]{1,0:T(8,128)(2,1)S(1)} %get-tuple-element.200.tail.rest_2_.rest_1_, ...), custom_call_target="tpu_custom_call", output_to_operand_aliasing={{0}: (11, {}), {1}: (12, {})} | custom-call | flops 1765949440 | bytes 9915200 | tf_op jit(solution)/shard_map/pallas_call | solution.py:492
  81.9 2.5 %collective-permute-done.10.rest_2_ = bf16[384,768]{1,0:T(8,128)(2,1)S(1)} collective-permute-done((bf16[384,768]{1,0:T(8,128)(2,1)S(1)}, bf16[384,768]{1,0:T(8,128)(2,1)S(1)}, u32[]{:S(2)}, u32[]{:S(2)}) %collective-permute-start.10) | collective-permute-done | bytes 589856 | tf_op jit(solution)/shard_map/ppermute | solution.py:1057
  84.4 1.0 collective-permute-done.9.rest_1_
  85.4 1.8 collective-permute-start.13
  87.9 3.8 %shard_map.259 = (f32[640,768]{1,0:T(8,128)}, bf16[640,768]{1,0:T(8,128)(2,1)S(1)}) custom-call(bf16[640,768]{1,0:T(8,128)(2,1)} %tokens.5, f32[640,768]{1,0:T(8,128)S(1)} %get-tuple-element.215.mine, bf16[640,768]{1,0:T(8,128)(2,1)S(1)} %collective-permute-done.8.received, f32[1,768]{1,0:T(1,128)S(1)} %reshape.55.bias, f32[1,768]{1,0:T(1,128)S(1)} %reshape.56.gain, ...), custom_call_target="tpu_custom_call" | custom-call | flops 5898240 | bytes 6881280 | tf_op jit(solution)/shard_map/pallas_call | solution.py:133
  91.7 2.4 collective-permute-done.13.rest_3_
  94.1 1.2 collective-permute-done.14.rest_4_
  95.3 0.9 collective-permute-start.16
  96.2 1.6 collective-permute-done.15.rest_7_
  97.9 0.9 copy-done.27
  98.8 15.1 %shard_map.260 = (bf16[2,2,96,768]{3,2,1,0:T(8,128)(2,1)}, bf16[2,2,96,768]{3,2,1,0:T(8,128)(2,1)}, bf16[2,2,96,768]{3,2,1,0:T(8,128)(2,1)}, bf16[2,2,96,768]{3,...) custom-call(s32[3]{0:T(128)S(1)} %pad_add_fusion.place, ...), custom_call_target="tpu_custom_call" | custom-call | flops 9059696640 | bytes 19796480 | tf_op jit(solution)/shard_map/pallas_call | solution.py:765
  115.2 1.2 collective-permute-start.18
  116.4 15.1 %shard_map.261 = (bf16[2,4,2,96,768]{4,3,2,1,0:T(8,128)(2,1)}, f32[8,768]{1,0:T(8,128)S(1)}, bf16[640,768]{1,0:T(8,128)(2,1)}, bf16[640,768]{1,0:T(8,128)(2,1)},...) custom-call(s32[3]{0:T(128)S(1)} %pad_add_fusion.place, bf16[768,768]{1,0:T(8,128)(2,1)S(1)} %copy-done.4, ...), custom_call_target="tpu_custom_call" | custom-call | flops 9059696640 | bytes 19796480 | tf_op jit(solution)/shard_map/pallas_call | solution.py:765
  131.7 0.9 collective-permute-start.25
  133.4 1.0 collective-permute-done.21.part3
  134.4 4.2 %shard_map.263 = (bf16[640,768]{1,0:T(8,128)(2,1)S(1)}, f32[8,768]{1,0:T(8,128)S(1)}) custom-call(bf16[640,768]{1,0:T(8,128)(2,1)S(1)} %copy-done.6, bf16[640,768]{1,0:T(8,128)(2,1)S(1)} %collective-permute-done.19.part1, bf16[640,768]{1,0:T(8,128)(2,1)S(1)} %copy-done.7, bf16[640,768]{1,0:T(8,128)(2,1)S(1)} %collective-permute-done.21.part3, ...), custom_call_target="tpu_custom_call" | custom-call | flops 12288000 | bytes 8847360 | tf_op jit(solution)/shard_map/pallas_call | solution.py:174
  138.6 0.9 collective-permute-start.22
  139.5 2.2 collective-permute-done.22.rest_7_
  142.1 1.6 collective-permute-start.23
  143.6 1.4 collective-permute-start.24
  145.0 12.4 %shard_map.264 = (bf16[2,1,96,768]{3,2,1,0:T(8,128)(2,1)S(1)}, bf16[2,1,96,768]{3,2,1,0:T(8,128)(2,1)S(1)}, bf16[2,1,96,768]{3,2,1,0:T(8,128)(2,1)S(1)}, bf16[2,...) custom-call(s32[3]{0:T(128)S(1)} %pad_add_fusion.place, ...), custom_call_target="tpu_custom_call" | custom-call | flops 3215155200 | bytes 13830400 | tf_op jit(solution)/shard_map/pallas_call | solution.py:623
  158.3 6.3 %collective-permute-start.27 = (bf16[4,2,96,768]{3,2,1,0:T(8,128)(2,1)S(1)}, bf16[4,2,96,768]{3,2,1,0:T(8,128)(2,1)S(1)}, u32[]{:S(2)}, u32[]{:S(2)}) collective-permute-start(bf16[4,2,96,768]{3,2,1,0:T(8,128)(2,1)S(1)} %get-tuple-element.278), channel_id=1, source_target_pairs={{0,4},{4,0},{1,5},{5,1},{2,6},{6,2},{3,7},{7,3},{8,12},{12,8},{9,1... | collective-permute-start | bytes 3538952 | tf_op jit(solution)/shard_map/ppermute | solution.py:1125
  164.6 1.7 collective-permute-start.29
  166.9 1.2 collective-permute-start.31
  168.1 12.2 %shard_map.266 = (bf16[2,1,96,768]{3,2,1,0:T(8,128)(2,1)S(1)}, bf16[2,1,96,768]{3,2,1,0:T(8,128)(2,1)S(1)}, bf16[2,1,96,768]{3,2,1,0:T(8,128)(2,1)S(1)}, bf16[2,...) custom-call(s32[3]{0:T(128)S(1)} %pad_add_fusion.place, ...), custom_call_target="tpu_custom_call" | custom-call | flops 3215155200 | bytes 13830400 | tf_op jit(solution)/shard_map/pallas_call | solution.py:623
  180.3 1.4 collective-permute-done.30.refs_2_
  181.7 3.4 %collective-permute-start.33 = (bf16[640,768]{1,0:T(8,128)(2,1)S(1)}, bf16[640,768]{1,0:T(8,128)(2,1)S(1)}, u32[]{:S(2)}, u32[]{:S(2)}) collective-permute-start(bf16[640,768]{1,0:T(8,128)(2,1)S(1)} %get-tuple-element.293), channel_id=1, source_target_pairs={{0,4},{4,0},{1,5},{5,1},{2,6},{6,2},{3,7},{7,3},{8,12},{12,8},{9,1... | collective-permute-start | bytes 2949128 | tf_op jit(solution)/shard_map/ppermute | solution.py:1137
  185.3 1.1 shard_map.268
  186.9 1.6 collective-permute-start.35
  188.4 1.4 collective-permute-start.36
  190.4 5.0 %shard_map.267 = (f32[640,768]{1,0:T(8,128)}, f32[16,768]{1,0:T(8,128)S(1)}) custom-call(s32[3]{0:T(128)S(1)} %pad_add_fusion.place, bf16[640,768]{1,0:T(8,128)(2,1)S(1)} %get-tuple-element.272.part0, bf16[640,768]{1,0:T(8,128)(2,1)S(1)} %collective-permute-done.28.part1, bf16[640,768]{1,0:T(8,128)(2,1)S(1)} %get-tuple-element.292.part2, ...), custom_call_target="tpu_custom_call" | custom-call | flops 12288000 | bytes 7864320 | tf_op jit(solution)/shard_map/pallas_call | solution.py:233
  195.5 2.0 collective-permute-start.40
  197.5 1.7 collective-permute-start.45
  199.2 4.2 %collective-permute-done.36.refs_2_ = bf16[2,1,96,768]{3,2,1,0:T(8,128)(2,1)S(1)} collective-permute-done((bf16[2,1,96,768]{3,2,1,0:T(8,128)(2,1)S(1)}, bf16[2,1,96,768]{3,2,1,0:T(8,128)(2,1)S(1)}, u32[]{:S(2)}, u32[]{:S(2)}) %collective-permute-start.36) | collective-permute-done | bytes 294944 | tf_op jit(solution)/shard_map/ppermute | solution.py:1023
  203.4 2.5 collective-permute-start.46
  207.4 1.7 add_convert_fusion
  209.7 4.6 %collective-permute-start.41 = (bf16[1,96,768]{2,1,0:T(8,128)(2,1)S(1)}, bf16[1,96,768]{2,1,0:T(8,128)(2,1)S(1)}, u32[]{:S(2)}, u32[]{:S(2)}) collective-permute-start(bf16[1,96,768]{2,1,0:T(8,128)(2,1)S(1)} %get-tuple-element.327), channel_id=1, source_target_pairs={{0,4},{4,0},{1,5},{5,1},{2,6},{6,2},{3,7},{7,3},{8,12},{12,8},{9,1... | collective-permute-start | bytes 442376 | tf_op jit(solution)/shard_map/ppermute | solution.py:1176
  214.8 1.6 collective-permute-start.43
  218.9 3.0 %collective-permute-done.44.refs_11_ = f32[16,768]{1,0:T(8,128)S(1)} collective-permute-done((f32[16,768]{1,0:T(8,128)S(1)}, f32[16,768]{1,0:T(8,128)S(1)}, u32[]{:S(2)}, u32[]{:S(2)}) %collective-permute-start.44) | collective-permute-done | bytes 49184 | tf_op jit(solution)/shard_map/ppermute | solution.py:1002
  222.8 1.7 collective-permute-start.51
  224.8 1.5 collective-permute-start.49
  226.2 1.7 collective-permute-start.50
  228.0 2.0 collective-permute-start.52
  230.4 2.6 %collective-permute-done.52 = f32[16,768]{1,0:T(8,128)S(1)} collective-permute-done((f32[16,768]{1,0:T(8,128)S(1)}, f32[16,768]{1,0:T(8,128)S(1)}, u32[]{:S(2)}, u32[]{:S(2)}) %collective-permute-start.52) | collective-permute-done | bytes 49184 | tf_op jit(solution)/shard_map/ppermute | solution.py:1186
  233.0 1.0 collective-permute-done.53
  235.4 2.2 collective-permute-done.48.refs_1_
  238.1 5.5 %collective-permute-done.50.refs_3_ = bf16[3,96,768]{2,1,0:T(8,128)(2,1)S(1)} collective-permute-done((bf16[3,96,768]{2,1,0:T(8,128)(2,1)S(1)}, bf16[3,96,768]{2,1,0:T(8,128)(2,1)S(1)}, u32[]{:S(2)}, u32[]{:S(2)}) %collective-permute-start.50) | collective-permute-done | bytes 442400 | tf_op jit(solution)/shard_map/ppermute | solution.py:1002
  244.7 2.5 shard_map.272
  247.4 2.5 shard_map.273
  (141 shorter events, 21.7 us)
Async XLA Ops:
  6.2 15.2 %collective-permute-start.1 = (bf16[656,768]{1,0:T(8,128)(2,1)S(1)}, bf16[656,768]{1,0:T(8,128)(2,1)S(1)}, u32[]{:S(2)}, u32[]{:S(2)}) collective-permute-start(bf16[656,768]{1,0:T(8,128)(2,1)S(1)} %shard_map.254.normed.counts.rest_4_), channel_id=1, source_target_pairs={{0,4},{4,0},{1,5},{5,1},{2,6},{6,2},{3,7},{7,3},{8,12},{12,8},{9,1... | collective-permute-start | bytes 3022856 | tf_op jit(solution)/shard_map/ppermute | solution.py:1042
  8.4 13.0 %collective-permute-start = (bf16[208,768]{1,0:T(8,128)(2,1)S(1)}, bf16[208,768]{1,0:T(8,128)(2,1)S(1)}, u32[]{:S(2)}, u32[]{:S(2)}) collective-permute-start(bf16[208,768]{1,0:T(8,128)(2,1)S(1)} %get-tuple-element.195), channel_id=1, source_target_pairs={{0,1},{1,2},{2,3},{3,0},{4,6},{5,7},{6,4},{7,5},{8,9},{9,10},{10,1... | collective-permute-start | bytes 958472 | tf_op jit(solution)/shard_map/ppermute | solution.py:1041
  21.4 16.0 %collective-permute-start.5 = (bf16[576,768]{1,0:T(8,128)(2,1)S(1)}, bf16[576,768]{1,0:T(8,128)(2,1)S(1)}, u32[]{:S(2)}, u32[]{:S(2)}) collective-permute-start(bf16[576,768]{1,0:T(8,128)(2,1)S(1)} %bitcast.10), channel_id=1, source_target_pairs={{4,7},{5,4},{6,5},{7,6},{12,15},{13,12},{14,13},{15,14},{20,23},{2... | collective-permute-start | bytes 2654216 | tf_op jit(solution)/shard_map/ppermute | solution.py:1046
  22.1 27.7 %copy-start.4 = (bf16[768,768]{1,0:T(8,128)(2,1)S(1)}, bf16[768,768]{1,0:T(8,128)(2,1)}, u32[]{:S(2)}) copy-start(bf16[768,768]{1,0:T(8,128)(2,1)} %rest_0_.1) | copy-start | bytes 3538948
  22.1 28.6 %copy-start.17 = (bf16[640,768]{1,0:T(8,128)(2,1)S(1)}, bf16[640,768]{1,0:T(8,128)(2,1)}, u32[]{:S(2)}) copy-start(bf16[640,768]{1,0:T(8,128)(2,1)} %output_grad.1) | copy-start | bytes 2949124
  22.1 4.4 %collective-permute-start.6 = (bf16[208,768]{1,0:T(8,128)(2,1)S(1)}, bf16[208,768]{1,0:T(8,128)(2,1)S(1)}, u32[]{:S(2)}, u32[]{:S(2)}) collective-permute-start(bf16[208,768]{1,0:T(8,128)(2,1)S(1)} %get-tuple-element.200.tail.rest_2_.rest_1_), channel_id=1, source_target_pairs={{4,7},{5,4},{6,5},{7,6},{12,15},{13,12},{14,13},{15,14},{20,23},{2... | collective-permute-start | bytes 958472 | tf_op jit(solution)/shard_map/ppermute | solution.py:1047
  23.0 7.1 %collective-permute-start.2 = (bf16[208,768]{1,0:T(8,128)(2,1)S(1)}, bf16[208,768]{1,0:T(8,128)(2,1)S(1)}, u32[]{:S(2)}, u32[]{:S(2)}) collective-permute-start(bf16[208,768]{1,0:T(8,128)(2,1)S(1)} %collective-permute-done.near0.rest_5_.rest_0_), channel_id=1, source_target_pairs={{0,8},{8,0},{1,9},{9,1},{2,10},{10,2},{3,11},{11,3},{4,12},{12,4},... | collective-permute-start | bytes 958472 | tf_op jit(solution)/shard_map/ppermute | solution.py:1000
  24.5 10.7 %collective-permute-start.3 = (bf16[208,768]{1,0:T(8,128)(2,1)S(1)}, bf16[208,768]{1,0:T(8,128)(2,1)S(1)}, u32[]{:S(2)}, u32[]{:S(2)}) collective-permute-start(bf16[208,768]{1,0:T(8,128)(2,1)S(1)} %collective-permute-done.near0.rest_5_.rest_0_), channel_id=1, source_target_pairs={{0,16},{16,0},{1,17},{17,1},{2,18},{18,2},{3,19},{19,3},{4,20},{20... | collective-permute-start | bytes 958472 | tf_op jit(solution)/shard_map/ppermute | solution.py:1001
  26.0 9.2 %collective-permute-start.4 = (bf16[208,768]{1,0:T(8,128)(2,1)S(1)}, bf16[208,768]{1,0:T(8,128)(2,1)S(1)}, u32[]{:S(2)}, u32[]{:S(2)}) collective-permute-start(bf16[208,768]{1,0:T(8,128)(2,1)S(1)} %collective-permute-done.near0.rest_5_.rest_0_), channel_id=1, source_target_pairs={{0,24},{8,16},{16,8},{24,0},{1,25},{9,17},{17,9},{25,1},{2,26},{10... | collective-permute-start | bytes 958472 | tf_op jit(solution)/shard_map/ppermute | solution.py:1002
  35.3 14.6 %collective-permute-start.7 = (bf16[384,768]{1,0:T(8,128)(2,1)S(1)}, bf16[384,768]{1,0:T(8,128)(2,1)S(1)}, u32[]{:S(2)}, u32[]{:S(2)}) collective-permute-start(bf16[384,768]{1,0:T(8,128)(2,1)S(1)} %shard_map.256), channel_id=1, source_target_pairs={{0,1},{1,2},{2,3},{3,0},{4,6},{5,7},{6,4},{7,5},{8,9},{9,10},{10,1... | collective-permute-start | bytes 1769480 | tf_op jit(solution)/shard_map/ppermute | solution.py:1048
  49.8 38.0 %copy-start.21 = (f32[768]{0:T(1024)S(1)}, f32[768]{0:T(1024)}, u32[]{:S(2)}) copy-start(f32[768]{0:T(1024)} %param.23) | copy-start | bytes 9220
  49.8 38.0 %copy-start.22 = (f32[768]{0:T(1024)S(1)}, f32[768]{0:T(1024)}, u32[]{:S(2)}) copy-start(f32[768]{0:T(1024)} %param.22) | copy-start | bytes 9220
  49.8 38.1 %copy-start.23 = (f32[768]{0:T(1024)S(1)}, f32[768]{0:T(1024)}, u32[]{:S(2)}) copy-start(f32[768]{0:T(1024)} %param.24) | copy-start | bytes 9220
  49.8 35.6 %collective-permute-start.11 = (bf16[768,768]{1,0:T(8,128)(2,1)S(1)}, bf16[768,768]{1,0:T(8,128)(2,1)S(1)}, u32[]{:S(2)}, u32[]{:S(2)}) collective-permute-start(bf16[768,768]{1,0:T(8,128)(2,1)S(1)} %copy-done.4), channel_id=1, source_target_pairs={{4,7},{5,4},{6,5},{7,6},{12,15},{13,12},{14,13},{15,14},{20,23},{2... | collective-permute-start | bytes 3538952 | tf_op jit(solution)/shard_map/ppermute | solution.py:1058
  50.7 34.7 %collective-permute-start.12 = (bf16[640,768]{1,0:T(8,128)(2,1)S(1)}, bf16[640,768]{1,0:T(8,128)(2,1)S(1)}, u32[]{:S(2)}, u32[]{:S(2)}) collective-permute-start(bf16[640,768]{1,0:T(8,128)(2,1)S(1)} %copy-done.17), channel_id=1, source_target_pairs={{0,4},{4,0},{1,5},{5,1},{2,6},{6,2},{3,7},{7,3},{8,12},{12,8},{9,1... | collective-permute-start | bytes 2949128 | tf_op jit(solution)/shard_map/ppermute | solution.py:1054
  68.7 16.7 %collective-permute-start.8 = (bf16[640,768]{1,0:T(8,128)(2,1)S(1)}, bf16[640,768]{1,0:T(8,128)(2,1)S(1)}, u32[]{:S(2)}, u32[]{:S(2)}) collective-permute-start(bf16[640,768]{1,0:T(8,128)(2,1)S(1)} %get-tuple-element.210), channel_id=1, source_target_pairs={{0,4},{4,0},{1,5},{5,1},{2,6},{6,2},{3,7},{7,3},{8,12},{12,8},{9,1... | collective-permute-start | bytes 2949128 | tf_op jit(solution)/shard_map/ppermute | solution.py:1055
  68.8 15.7 %collective-permute-start.10 = (bf16[384,768]{1,0:T(8,128)(2,1)S(1)}, bf16[384,768]{1,0:T(8,128)(2,1)S(1)}, u32[]{:S(2)}, u32[]{:S(2)}) collective-permute-start(bf16[384,768]{1,0:T(8,128)(2,1)S(1)} %collective-permute-done.7.rest_0_), channel_id=1, source_target_pairs={{0,16},{16,0},{1,17},{17,1},{2,18},{18,2},{3,19},{19,3},{4,20},{20... | collective-permute-start | bytes 1769480 | tf_op jit(solution)/shard_map/ppermute | solution.py:1057
  69.6 15.8 %collective-permute-start.9 = (bf16[384,768]{1,0:T(8,128)(2,1)S(1)}, bf16[384,768]{1,0:T(8,128)(2,1)S(1)}, u32[]{:S(2)}, u32[]{:S(2)}) collective-permute-start(bf16[384,768]{1,0:T(8,128)(2,1)S(1)} %collective-permute-done.7.rest_0_), channel_id=1, source_target_pairs={{0,8},{8,0},{1,9},{9,1},{2,10},{10,2},{3,11},{11,3},{4,12},{12,4},... | collective-permute-start | bytes 1769480 | tf_op jit(solution)/shard_map/ppermute | solution.py:1056
  85.4 8.6 %collective-permute-start.13 = (bf16[192,768]{1,0:T(8,128)(2,1)S(1)}, bf16[192,768]{1,0:T(8,128)(2,1)S(1)}, u32[]{:S(2)}, u32[]{:S(2)}) collective-permute-start(bf16[192,768]{1,0:T(8,128)(2,1)S(1)} %slice.30), channel_id=1, source_target_pairs={{0,8},{8,0},{1,9},{9,1},{2,10},{10,2},{3,11},{11,3},{4,12},{12,4},... | collective-permute-start | bytes 884744 | tf_op jit(solution)/shard_map/ppermute | solution.py:1066
  87.3 8.0 %collective-permute-start.14 = (bf16[192,768]{1,0:T(8,128)(2,1)S(1)}, bf16[192,768]{1,0:T(8,128)(2,1)S(1)}, u32[]{:S(2)}, u32[]{:S(2)}) collective-permute-start(bf16[192,768]{1,0:T(8,128)(2,1)S(1)} %slice.31), channel_id=1, source_target_pairs={{0,16},{16,0},{1,17},{17,1},{2,18},{18,2},{3,19},{19,3},{4,20},{20... | collective-permute-start | bytes 884744 | tf_op jit(solution)/shard_map/ppermute | solution.py:1067
  95.3 2.6 %collective-permute-start.15 = (bf16[640,768]{1,0:T(8,128)(2,1)S(1)}, bf16[640,768]{1,0:T(8,128)(2,1)S(1)}, u32[]{:S(2)}, u32[]{:S(2)}) collective-permute-start(bf16[640,768]{1,0:T(8,128)(2,1)S(1)} %get-tuple-element.221.rest_6_), channel_id=1, source_target_pairs={{0,4},{4,0},{1,5},{5,1},{2,6},{6,2},{3,7},{7,3},{8,12},{12,8},{9,1... | collective-permute-start | bytes 2949128 | tf_op jit(solution)/shard_map/ppermute | solution.py:1079
  95.3 18.6 %collective-permute-start.16 = (bf16[768,768]{1,0:T(8,128)(2,1)S(1)}, bf16[768,768]{1,0:T(8,128)(2,1)S(1)}, u32[]{:S(2)}, u32[]{:S(2)}) collective-permute-start(bf16[768,768]{1,0:T(8,128)(2,1)S(1)} %copy-done.5), channel_id=1, source_target_pairs={{4,7},{5,4},{6,5},{7,6},{12,15},{13,12},{14,13},{15,14},{20,23},{2... | collective-permute-start | bytes 3538952 | tf_op jit(solution)/shard_map/ppermute | solution.py:1080
  114.0 17.6 %collective-permute-start.19 = (bf16[640,768]{1,0:T(8,128)(2,1)}, bf16[640,768]{1,0:T(8,128)(2,1)S(1)}, u32[]{:S(2)}, u32[]{:S(2)}) collective-permute-start(bf16[640,768]{1,0:T(8,128)(2,1)} %get-tuple-element.246), channel_id=1, source_target_pairs={{0,4},{4,0},{1,5},{5,1},{2,6},{6,2},{3,7},{7,3},{8,12},{12,8},{9,1... | collective-permute-start | bytes 2949128 | tf_op jit(solution)/shard_map/ppermute | solution.py:1089
  114.5 17.0 %collective-permute-start.20 = (bf16[640,768]{1,0:T(8,128)(2,1)}, bf16[640,768]{1,0:T(8,128)(2,1)S(1)}, u32[]{:S(2)}, u32[]{:S(2)}) collective-permute-start(bf16[640,768]{1,0:T(8,128)(2,1)} %get-tuple-element.247), channel_id=1, source_target_pairs={{0,4},{4,0},{1,5},{5,1},{2,6},{6,2},{3,7},{7,3},{8,12},{12,8},{9,1... | collective-permute-start | bytes 2949128 | tf_op jit(solution)/shard_map/ppermute | solution.py:1090
  114.6 16.9 %collective-permute-start.17 = (bf16[2,2,96,768]{3,2,1,0:T(8,128)(2,1)}, bf16[2,2,96,768]{3,2,1,0:T(8,128)(2,1)S(1)}, u32[]{:S(2)}, u32[]{:S(2)}) collective-permute-start(bf16[2,2,96,768]{3,2,1,0:T(8,128)(2,1)} %get-tuple-element.244), channel_id=1, source_target_pairs={{0,8},{8,0},{1,9},{9,1},{2,10},{10,2},{3,11},{11,3},{4,12},{12,4},... | collective-permute-start | bytes 1769480 | tf_op jit(solution)/shard_map/ppermute | solution.py:1012
  115.2 16.4 %collective-permute-start.18 = (bf16[2,2,96,768]{3,2,1,0:T(8,128)(2,1)}, bf16[2,2,96,768]{3,2,1,0:T(8,128)(2,1)S(1)}, u32[]{:S(2)}, u32[]{:S(2)}) collective-permute-start(bf16[2,2,96,768]{3,2,1,0:T(8,128)(2,1)} %get-tuple-element.245), channel_id=1, source_target_pairs={{0,16},{16,0},{1,17},{17,1},{2,18},{18,2},{3,19},{19,3},{4,20},{20... | collective-permute-start | bytes 1769480 | tf_op jit(solution)/shard_map/ppermute | solution.py:1013
  131.6 2.8 %collective-permute-start.21 = (bf16[640,768]{1,0:T(8,128)(2,1)}, bf16[640,768]{1,0:T(8,128)(2,1)S(1)}, u32[]{:S(2)}, u32[]{:S(2)}) collective-permute-start(bf16[640,768]{1,0:T(8,128)(2,1)} %get-tuple-element.250), channel_id=1, source_target_pairs={{0,4},{4,0},{1,5},{5,1},{2,6},{6,2},{3,7},{7,3},{8,12},{12,8},{9,1... | collective-permute-start | bytes 2949128 | tf_op jit(solution)/shard_map/ppermute | solution.py:1099
  131.7 25.8 %collective-permute-start.25 = (bf16[2,4,2,96,768]{4,3,2,1,0:T(8,128)(2,1)}, bf16[2,4,2,96,768]{4,3,2,1,0:T(8,128)(2,1)S(1)}, u32[]{:S(2)}, u32[]{:S(2)}) collective-permute-start(bf16[2,4,2,96,768]{4,3,2,1,0:T(8,128)(2,1)} %get-tuple-element.269.refs_3_.refs_4_), channel_id=1, source_target_pairs={{7,4},{4,5},{5,6},{6,7},{15,12},{12,13},{13,14},{14,15},{23,20},{2... | collective-permute-start | bytes 7077896 | tf_op jit(solution)/shard_map/ppermute | solution.py:1098
  138.6 29.5 %copy-start.2 = (bf16[640,768]{1,0:T(8,128)(2,1)}, bf16[640,768]{1,0:T(8,128)(2,1)S(1)}, u32[]{:S(2)}) copy-start(bf16[640,768]{1,0:T(8,128)(2,1)S(1)} %get-tuple-element.281.rest_6_.grad_first) | copy-start | bytes 2949124
  138.6 3.1 %collective-permute-start.22 = (bf16[640,768]{1,0:T(8,128)(2,1)S(1)}, bf16[640,768]{1,0:T(8,128)(2,1)S(1)}, u32[]{:S(2)}, u32[]{:S(2)}) collective-permute-start(bf16[640,768]{1,0:T(8,128)(2,1)S(1)} %get-tuple-element.281.rest_6_.grad_first), channel_id=1, source_target_pairs={{0,4},{4,0},{1,5},{5,1},{2,6},{6,2},{3,7},{7,3},{8,12},{12,8},{9,1... | collective-permute-start | bytes 2949128 | tf_op jit(solution)/shard_map/ppermute | solution.py:1109
  141.7 15.8 %collective-permute-start.26 = (bf16[640,768]{1,0:T(8,128)(2,1)S(1)}, bf16[640,768]{1,0:T(8,128)(2,1)S(1)}, u32[]{:S(2)}, u32[]{:S(2)}) collective-permute-start(bf16[640,768]{1,0:T(8,128)(2,1)S(1)} %copy-done.26), channel_id=1, source_target_pairs={{0,4},{4,0},{1,5},{5,1},{2,6},{6,2},{3,7},{7,3},{8,12},{12,8},{9,1... | collective-permute-start | bytes 2949128 | tf_op jit(solution)/shard_map/ppermute | solution.py:1110
  142.1 15.4 %collective-permute-start.23 = (bf16[2,96,768]{2,1,0:T(8,128)(2,1)S(1)}, bf16[2,96,768]{2,1,0:T(8,128)(2,1)S(1)}, u32[]{:S(2)}, u32[]{:S(2)}) collective-permute-start(bf16[2,96,768]{2,1,0:T(8,128)(2,1)S(1)} %get-tuple-element.255), channel_id=1, source_target_pairs={{0,16},{16,0},{1,17},{17,1},{2,18},{18,2},{3,19},{19,3},{4,20},{20... | collective-permute-start | bytes 884744 | tf_op jit(solution)/shard_map/ppermute | solution.py:1017
  143.6 13.8 %collective-permute-start.24 = (bf16[2,96,768]{2,1,0:T(8,128)(2,1)S(1)}, bf16[2,96,768]{2,1,0:T(8,128)(2,1)S(1)}, u32[]{:S(2)}, u32[]{:S(2)}) collective-permute-start(bf16[2,96,768]{2,1,0:T(8,128)(2,1)S(1)} %get-tuple-element.256), channel_id=1, source_target_pairs={{0,8},{8,0},{1,9},{9,1},{2,10},{10,2},{3,11},{11,3},{4,12},{12,4},... | collective-permute-start | bytes 884744 | tf_op jit(solution)/shard_map/ppermute | solution.py:1017
  158.3 23.5 %collective-permute-start.27 = (bf16[4,2,96,768]{3,2,1,0:T(8,128)(2,1)S(1)}, bf16[4,2,96,768]{3,2,1,0:T(8,128)(2,1)S(1)}, u32[]{:S(2)}, u32[]{:S(2)}) collective-permute-start(bf16[4,2,96,768]{3,2,1,0:T(8,128)(2,1)S(1)} %get-tuple-element.278), channel_id=1, source_target_pairs={{0,4},{4,0},{1,5},{5,1},{2,6},{6,2},{3,7},{7,3},{8,12},{12,8},{9,1... | collective-permute-start | bytes 3538952 | tf_op jit(solution)/shard_map/ppermute | solution.py:1125
  164.6 17.1 %collective-permute-start.32 = (bf16[2,2,96,768]{3,2,1,0:T(8,128)(2,1)S(1)}, bf16[2,2,96,768]{3,2,1,0:T(8,128)(2,1)S(1)}, u32[]{:S(2)}, u32[]{:S(2)}) collective-permute-start(bf16[2,2,96,768]{3,2,1,0:T(8,128)(2,1)S(1)} %get-tuple-element.280), channel_id=1, source_target_pairs={{1,0},{2,1},{3,2},{0,3},{6,4},{7,5},{4,6},{5,7},{9,8},{10,9},{11,1... | collective-permute-start | bytes 1769480 | tf_op jit(solution)/shard_map/ppermute | solution.py:1124
  164.6 15.7 %collective-permute-start.29 = (bf16[2,1,96,768]{3,2,1,0:T(8,128)(2,1)S(1)}, bf16[2,1,96,768]{3,2,1,0:T(8,128)(2,1)S(1)}, u32[]{:S(2)}, u32[]{:S(2)}) collective-permute-start(bf16[2,1,96,768]{3,2,1,0:T(8,128)(2,1)S(1)} %get-tuple-element.289), channel_id=1, source_target_pairs={{0,8},{8,0},{1,9},{9,1},{2,10},{10,2},{3,11},{11,3},{4,12},{12,4},... | collective-permute-start | bytes 884744 | tf_op jit(solution)/shard_map/ppermute | solution.py:1022
  166.3 15.4 %collective-permute-start.30 = (bf16[2,1,96,768]{3,2,1,0:T(8,128)(2,1)S(1)}, bf16[2,1,96,768]{3,2,1,0:T(8,128)(2,1)S(1)}, u32[]{:S(2)}, u32[]{:S(2)}) collective-permute-start(bf16[2,1,96,768]{3,2,1,0:T(8,128)(2,1)S(1)} %get-tuple-element.290), channel_id=1, source_target_pairs={{0,16},{16,0},{1,17},{17,1},{2,18},{18,2},{3,19},{19,3},{4,20},{20... | collective-permute-start | bytes 884744 | tf_op jit(solution)/shard_map/ppermute | solution.py:1023
  166.9 14.9 %collective-permute-start.31 = (bf16[2,1,96,768]{3,2,1,0:T(8,128)(2,1)S(1)}, bf16[2,1,96,768]{3,2,1,0:T(8,128)(2,1)S(1)}, u32[]{:S(2)}, u32[]{:S(2)}) collective-permute-start(bf16[2,1,96,768]{3,2,1,0:T(8,128)(2,1)S(1)} %get-tuple-element.291), channel_id=1, source_target_pairs={{0,24},{8,16},{16,8},{24,0},{1,25},{9,17},{17,9},{25,1},{2,26},{10... | collective-permute-start | bytes 884744 | tf_op jit(solution)/shard_map/ppermute | solution.py:1024
  181.7 8.1 %collective-permute-start.33 = (bf16[640,768]{1,0:T(8,128)(2,1)S(1)}, bf16[640,768]{1,0:T(8,128)(2,1)S(1)}, u32[]{:S(2)}, u32[]{:S(2)}) collective-permute-start(bf16[640,768]{1,0:T(8,128)(2,1)S(1)} %get-tuple-element.293), channel_id=1, source_target_pairs={{0,4},{4,0},{1,5},{5,1},{2,6},{6,2},{3,7},{7,3},{8,12},{12,8},{9,1... | collective-permute-start | bytes 2949128 | tf_op jit(solution)/shard_map/ppermute | solution.py:1137
  185.2 5.2 %collective-permute-start.28 = (bf16[640,768]{1,0:T(8,128)(2,1)S(1)}, bf16[640,768]{1,0:T(8,128)(2,1)S(1)}, u32[]{:S(2)}, u32[]{:S(2)}) collective-permute-start(bf16[640,768]{1,0:T(8,128)(2,1)S(1)} %get-tuple-element.279), channel_id=1, source_target_pairs={{0,4},{4,0},{1,5},{5,1},{2,6},{6,2},{3,7},{7,3},{8,12},{12,8},{9,1... | collective-permute-start | bytes 2949128 | tf_op jit(solution)/shard_map/ppermute | solution.py:1134
  186.3 9.1 %collective-permute-start.38 = (bf16[2,96,768]{2,1,0:T(8,128)(2,1)S(1)}, bf16[2,96,768]{2,1,0:T(8,128)(2,1)S(1)}, u32[]{:S(2)}, u32[]{:S(2)}) collective-permute-start(bf16[2,96,768]{2,1,0:T(8,128)(2,1)S(1)} %get-tuple-element.310), channel_id=1, source_target_pairs={{0,4},{4,0},{1,5},{5,1},{2,6},{6,2},{3,7},{7,3},{8,12},{12,8},{9,1... | collective-permute-start | bytes 884744 | tf_op jit(solution)/shard_map/ppermute | solution.py:1145
  186.9 10.6 %collective-permute-start.35 = (bf16[2,1,96,768]{3,2,1,0:T(8,128)(2,1)S(1)}, bf16[2,1,96,768]{3,2,1,0:T(8,128)(2,1)S(1)}, u32[]{:S(2)}, u32[]{:S(2)}) collective-permute-start(bf16[2,1,96,768]{3,2,1,0:T(8,128)(2,1)S(1)} %get-tuple-element.301), channel_id=1, source_target_pairs={{0,8},{8,0},{1,9},{9,1},{2,10},{10,2},{3,11},{11,3},{4,12},{12,4},... | collective-permute-start | bytes 884744 | tf_op jit(solution)/shard_map/ppermute | solution.py:1022
  188.4 15.0 %collective-permute-start.36 = (bf16[2,1,96,768]{3,2,1,0:T(8,128)(2,1)S(1)}, bf16[2,1,96,768]{3,2,1,0:T(8,128)(2,1)S(1)}, u32[]{:S(2)}, u32[]{:S(2)}) collective-permute-start(bf16[2,1,96,768]{3,2,1,0:T(8,128)(2,1)S(1)} %get-tuple-element.302), channel_id=1, source_target_pairs={{0,16},{16,0},{1,17},{17,1},{2,18},{18,2},{3,19},{19,3},{4,20},{20... | collective-permute-start | bytes 884744 | tf_op jit(solution)/shard_map/ppermute | solution.py:1023
  189.8 16.1 %collective-permute-start.37 = (bf16[2,1,96,768]{3,2,1,0:T(8,128)(2,1)S(1)}, bf16[2,1,96,768]{3,2,1,0:T(8,128)(2,1)S(1)}, u32[]{:S(2)}, u32[]{:S(2)}) collective-permute-start(bf16[2,1,96,768]{3,2,1,0:T(8,128)(2,1)S(1)} %get-tuple-element.303), channel_id=1, source_target_pairs={{0,24},{8,16},{16,8},{24,0},{1,25},{9,17},{17,9},{25,1},{2,26},{10... | collective-permute-start | bytes 884744 | tf_op jit(solution)/shard_map/ppermute | solution.py:1024
  195.4 10.5 %collective-permute-start.34 = (f32[16,768]{1,0:T(8,128)S(1)}, f32[16,768]{1,0:T(8,128)S(1)}, u32[]{:S(2)}, u32[]{:S(2)}) collective-permute-start(f32[16,768]{1,0:T(8,128)S(1)} %get-tuple-element.299.refs_4_), channel_id=1, source_target_pairs={{0,4},{4,0},{1,5},{5,1},{2,6},{6,2},{3,7},{7,3},{8,12},{12,8},{9,1... | collective-permute-start | bytes 147464 | tf_op jit(solution)/shard_map/ppermute | solution.py:1159
  195.5 13.6 %collective-permute-start.40 = (bf16[2,1,96,768]{3,2,1,0:T(8,128)(2,1)S(1)}, bf16[2,1,96,768]{3,2,1,0:T(8,128)(2,1)S(1)}, u32[]{:S(2)}, u32[]{:S(2)}) collective-permute-start(bf16[2,1,96,768]{3,2,1,0:T(8,128)(2,1)S(1)} %get-tuple-element.317), channel_id=1, source_target_pairs={{1,0},{2,1},{3,2},{0,3},{6,4},{7,5},{4,6},{5,7},{9,8},{10,9},{11,1... | collective-permute-start | bytes 884744 | tf_op jit(solution)/shard_map/ppermute | solution.py:1144
  197.5 17.3 %collective-permute-start.45 = (bf16[2,96,768]{2,1,0:T(8,128)(2,1)S(1)}, bf16[2,96,768]{2,1,0:T(8,128)(2,1)S(1)}, u32[]{:S(2)}, u32[]{:S(2)}) collective-permute-start(bf16[2,96,768]{2,1,0:T(8,128)(2,1)S(1)} %get-tuple-element.330), channel_id=1, source_target_pairs={{0,8},{8,0},{1,9},{9,1},{2,10},{10,2},{3,11},{11,3},{4,12},{12,4},... | collective-permute-start | bytes 884744 | tf_op jit(solution)/shard_map/ppermute | solution.py:1022
  203.4 13.5 %collective-permute-start.46 = (bf16[2,96,768]{2,1,0:T(8,128)(2,1)S(1)}, bf16[2,96,768]{2,1,0:T(8,128)(2,1)S(1)}, u32[]{:S(2)}, u32[]{:S(2)}) collective-permute-start(bf16[2,96,768]{2,1,0:T(8,128)(2,1)S(1)} %get-tuple-element.331), channel_id=1, source_target_pairs={{0,16},{16,0},{1,17},{17,1},{2,18},{18,2},{3,19},{19,3},{4,20},{20... | collective-permute-start | bytes 884744 | tf_op jit(solution)/shard_map/ppermute | solution.py:1023
  205.9 11.9 %collective-permute-start.47 = (bf16[2,96,768]{2,1,0:T(8,128)(2,1)S(1)}, bf16[2,96,768]{2,1,0:T(8,128)(2,1)S(1)}, u32[]{:S(2)}, u32[]{:S(2)}) collective-permute-start(bf16[2,96,768]{2,1,0:T(8,128)(2,1)S(1)} %get-tuple-element.332), channel_id=1, source_target_pairs={{0,24},{8,16},{16,8},{24,0},{1,25},{9,17},{17,9},{25,1},{2,26},{10... | collective-permute-start | bytes 884744 | tf_op jit(solution)/shard_map/ppermute | solution.py:1024
  206.7 2.4 collective-permute-start.39
  209.7 12.2 %collective-permute-start.41 = (bf16[1,96,768]{2,1,0:T(8,128)(2,1)S(1)}, bf16[1,96,768]{2,1,0:T(8,128)(2,1)S(1)}, u32[]{:S(2)}, u32[]{:S(2)}) collective-permute-start(bf16[1,96,768]{2,1,0:T(8,128)(2,1)S(1)} %get-tuple-element.327), channel_id=1, source_target_pairs={{0,4},{4,0},{1,5},{5,1},{2,6},{6,2},{3,7},{7,3},{8,12},{12,8},{9,1... | collective-permute-start | bytes 442376 | tf_op jit(solution)/shard_map/ppermute | solution.py:1176
  214.3 4.2 %collective-permute-start.42 = (f32[16,768]{1,0:T(8,128)S(1)}, f32[16,768]{1,0:T(8,128)S(1)}, u32[]{:S(2)}, u32[]{:S(2)}) collective-permute-start(f32[16,768]{1,0:T(8,128)S(1)} %get-tuple-element.340.refs_8_), channel_id=1, source_target_pairs={{0,8},{8,0},{1,9},{9,1},{2,10},{10,2},{3,11},{11,3},{4,12},{12,4},... | collective-permute-start | bytes 147464 | tf_op jit(solution)/shard_map/ppermute | solution.py:1000
  214.8 4.1 %collective-permute-start.43 = (f32[16,768]{1,0:T(8,128)S(1)}, f32[16,768]{1,0:T(8,128)S(1)}, u32[]{:S(2)}, u32[]{:S(2)}) collective-permute-start(f32[16,768]{1,0:T(8,128)S(1)} %get-tuple-element.340.refs_8_), channel_id=1, source_target_pairs={{0,16},{16,0},{1,17},{17,1},{2,18},{18,2},{3,19},{19,3},{4,20},{20... | collective-permute-start | bytes 147464 | tf_op jit(solution)/shard_map/ppermute | solution.py:1001
  216.9 5.0 %collective-permute-start.44 = (f32[16,768]{1,0:T(8,128)S(1)}, f32[16,768]{1,0:T(8,128)S(1)}, u32[]{:S(2)}, u32[]{:S(2)}) collective-permute-start(f32[16,768]{1,0:T(8,128)S(1)} %get-tuple-element.340.refs_8_), channel_id=1, source_target_pairs={{0,24},{8,16},{16,8},{24,0},{1,25},{9,17},{17,9},{25,1},{2,26},{10... | collective-permute-start | bytes 147464 | tf_op jit(solution)/shard_map/ppermute | solution.py:1002
  222.8 7.2 %collective-permute-start.51 = (f32[16,768]{1,0:T(8,128)S(1)}, f32[16,768]{1,0:T(8,128)S(1)}, u32[]{:S(2)}, u32[]{:S(2)}) collective-permute-start(f32[16,768]{1,0:T(8,128)S(1)} %get-tuple-element.345), channel_id=1, source_target_pairs={{0,1},{1,2},{2,3},{3,0},{4,5},{5,6},{6,7},{7,4},{8,9},{9,10},{10,1... | collective-permute-start | bytes 147464 | tf_op jit(solution)/shard_map/ppermute | solution.py:1186
  224.5 13.1 %collective-permute-start.48 = (bf16[3,96,768]{2,1,0:T(8,128)(2,1)S(1)}, bf16[3,96,768]{2,1,0:T(8,128)(2,1)S(1)}, u32[]{:S(2)}, u32[]{:S(2)}) collective-permute-start(bf16[3,96,768]{2,1,0:T(8,128)(2,1)S(1)} %get-tuple-element.348.refs_0_), channel_id=1, source_target_pairs={{0,8},{8,0},{1,9},{9,1},{2,10},{10,2},{3,11},{11,3},{4,12},{12,4},... | collective-permute-start | bytes 1327112 | tf_op jit(solution)/shard_map/ppermute | solution.py:1000
  224.8 13.4 %collective-permute-start.49 = (bf16[3,96,768]{2,1,0:T(8,128)(2,1)S(1)}, bf16[3,96,768]{2,1,0:T(8,128)(2,1)S(1)}, u32[]{:S(2)}, u32[]{:S(2)}) collective-permute-start(bf16[3,96,768]{2,1,0:T(8,128)(2,1)S(1)} %get-tuple-element.348.refs_0_), channel_id=1, source_target_pairs={{0,16},{16,0},{1,17},{17,1},{2,18},{18,2},{3,19},{19,3},{4,20},{20... | collective-permute-start | bytes 1327112 | tf_op jit(solution)/shard_map/ppermute | solution.py:1001
  226.2 17.4 %collective-permute-start.50 = (bf16[3,96,768]{2,1,0:T(8,128)(2,1)S(1)}, bf16[3,96,768]{2,1,0:T(8,128)(2,1)S(1)}, u32[]{:S(2)}, u32[]{:S(2)}) collective-permute-start(bf16[3,96,768]{2,1,0:T(8,128)(2,1)S(1)} %get-tuple-element.348.refs_0_), channel_id=1, source_target_pairs={{0,24},{8,16},{16,8},{24,0},{1,25},{9,17},{17,9},{25,1},{2,26},{10... | collective-permute-start | bytes 1327112 | tf_op jit(solution)/shard_map/ppermute | solution.py:1002
  228.0 5.0 %collective-permute-start.52 = (f32[16,768]{1,0:T(8,128)S(1)}, f32[16,768]{1,0:T(8,128)S(1)}, u32[]{:S(2)}, u32[]{:S(2)}) collective-permute-start(f32[16,768]{1,0:T(8,128)S(1)} %get-tuple-element.345), channel_id=1, source_target_pairs={{0,2},{1,3},{2,0},{3,1},{4,6},{5,7},{6,4},{7,5},{8,10},{9,11},{10,... | collective-permute-start | bytes 147464 | tf_op jit(solution)/shard_map/ppermute | solution.py:1186
  230.0 4.1 %collective-permute-start.53 = (f32[16,768]{1,0:T(8,128)S(1)}, f32[16,768]{1,0:T(8,128)S(1)}, u32[]{:S(2)}, u32[]{:S(2)}) collective-permute-start(f32[16,768]{1,0:T(8,128)S(1)} %get-tuple-element.345), channel_id=1, source_target_pairs={{0,3},{1,0},{2,1},{3,2},{4,7},{5,4},{6,5},{7,6},{8,11},{9,8},{10,9... | collective-permute-start | bytes 147464 | tf_op jit(solution)/shard_map/ppermute | solution.py:1186
  243.7 3.5 %collective-permute-start.54 = (bf16[3,96,768]{2,1,0:T(8,128)(2,1)S(1)}, bf16[3,96,768]{2,1,0:T(8,128)(2,1)S(1)}, u32[]{:S(2)}, u32[]{:S(2)}) collective-permute-start(bf16[3,96,768]{2,1,0:T(8,128)(2,1)S(1)} %get-tuple-element.348.refs_0_), channel_id=1, source_target_pairs={{0,4},{4,0},{1,5},{5,1},{2,6},{6,2},{3,7},{7,3},{8,12},{12,8},{9,1... | collective-permute-start | bytes 1327112 | tf_op jit(solution)/shard_map/ppermute | solution.py:1198
  243.7 3.5 %collective-permute-start.55 = (bf16[3,96,768]{2,1,0:T(8,128)(2,1)S(1)}, bf16[3,96,768]{2,1,0:T(8,128)(2,1)S(1)}, u32[]{:S(2)}, u32[]{:S(2)}) collective-permute-start(bf16[3,96,768]{2,1,0:T(8,128)(2,1)S(1)} %collective-permute-done.48.refs_1_), channel_id=1, source_target_pairs={{0,4},{4,0},{1,5},{5,1},{2,6},{6,2},{3,7},{7,3},{8,12},{12,8},{9,1... | collective-permute-start | bytes 1327112 | tf_op jit(solution)/shard_map/ppermute | solution.py:1198
  244.2 3.0 %collective-permute-start.56 = (bf16[3,96,768]{2,1,0:T(8,128)(2,1)S(1)}, bf16[3,96,768]{2,1,0:T(8,128)(2,1)S(1)}, u32[]{:S(2)}, u32[]{:S(2)}) collective-permute-start(bf16[3,96,768]{2,1,0:T(8,128)(2,1)S(1)} %collective-permute-done.49.refs_2_), channel_id=1, source_target_pairs={{0,4},{4,0},{1,5},{5,1},{2,6},{6,2},{3,7},{7,3},{8,12},{12,8},{9,1... | collective-permute-start | bytes 1327112 | tf_op jit(solution)/shard_map/ppermute | solution.py:1198
  244.2 3.2 %collective-permute-start.57 = (bf16[3,96,768]{2,1,0:T(8,128)(2,1)S(1)}, bf16[3,96,768]{2,1,0:T(8,128)(2,1)S(1)}, u32[]{:S(2)}, u32[]{:S(2)}) collective-permute-start(bf16[3,96,768]{2,1,0:T(8,128)(2,1)S(1)} %collective-permute-done.50.refs_3_), channel_id=1, source_target_pairs={{0,4},{4,0},{1,5},{5,1},{2,6},{6,2},{3,7},{7,3},{8,12},{12,8},{9,1... | collective-permute-start | bytes 1327112 | tf_op jit(solution)/shard_map/ppermute | solution.py:1198
  (22 other events, 190.2 us)
where the time goes:
time: 251 us; the launch traced here: 250 us
  Pallas kernels  103 us (41%)
  starting transfers between devices  83.7 us (33%)
  waiting for transfers between devices  54 us (22%)
  local copies, waits for them, and re-layouts  5.69 us (2%)
    pallas_call x2, Pallas kernels, hidden_block(): pl.pallas_call(functools.partial(hidden_kernel, last), out_shape=(*grad_s...  30.2 us
    pallas_call x2, Pallas kernels, attention_back(): pl.pallas_call(functools.partial(attention_back_kernel, heads, far), grid...  24.6 us
    pallas_call x2, Pallas kernels, attention(): pl.pallas_call(functools.partial(attention_kernel, heads), grid=(tiles,),...  20.4 us
    ppermute x1, starting transfers between devices, local(): grad_other = lax.ppermute(after(output_grad, part), 'c', swap)  18 us
    ppermute x1, waiting for transfers between devices, local(): depth_near_one = lax.ppermute(piece_one, ('c', 't'), to_near)  8.73 us
    ppermute x3, waiting for transfers between devices, spread(): lax.ppermute(piece, ('a', 'b'), cross)  8.58 us
    ppermute x3, waiting for transfers between devices, spread(): lax.ppermute(piece, 'b', swap)  6.4 us
    ppermute x1, starting transfers between devices, local(): received_far = lax.ppermute(send_far, 'c', swap)  6.33 us
  transfers between devices with their start and end apart: 58, of which 23 were waited for; matrix products, arithmetic and copies ran while one was open for 1% of the time, Pallas kernels for 39%

commit v1 on v0

--- a/solution.py
+++ b/solution.py
@@ -399,12 +399,8 @@
 def start_matrices(place, own, far, target, sems):
     def cut(parts):
         size = parts[0].shape[0]
-        bias = parts[2].at[pl.ds(parts[2].shape[0] - 16, 16)]
-        return [
-            (parts[0], target.at[pl.ds(0, size)]),
-            (parts[1], target.at[pl.ds(size, size)]),
-            (bias, target.at[pl.ds(2 * size, 16)]),
-        ]
+        bias = parts[1].at[pl.ds(parts[1].shape[0] - 16, 16)]
+        return [(parts[0], target.at[pl.ds(0, size)]), (bias, target.at[pl.ds(size, 16)])]
 
     return start_on_core(place, own, far, cut, sems)
 
@@ -652,7 +648,8 @@
 
 
 def hidden_kernel(last, place, *rest):
-    pieces, rest = rest[:6], rest[6:]
+    count = 4 if last else 6
+    pieces, rest = rest[:count], rest[count:]
     normed_parts, grad_parts, rest = rest[:2], rest[2:4], rest[4:]
     if last:
         whole_grads, rest = rest[0], rest[1:]
@@ -675,8 +672,8 @@
     for copy in normed_copies:
         copy.start()
     if last:
-        starts = start_matrices(place, pieces[:3], pieces[3:], weights, piece_sems)
-        first_needed, then_needed = [starts[0], starts[2]], [starts[1]]
+        first_needed = start_matrices(place, pieces[:2], pieces[2:], weights, piece_sems)
+        then_needed = []
     else:
         starts = hidden_copies(place, pieces[:5], pieces[5], weights, piece_sems)
         first_needed, then_needed = starts[0:8:2] + [starts[8]], starts[1:8:2]
@@ -772,7 +769,7 @@
             kept((rows, width), BF16),
             kept((rows, width), BF16),
         ),
-        in_specs=[SMEM] + [ANY] * 10,
+        in_specs=[SMEM] + [ANY] * (len(pieces) + 4),
         out_specs=(ANY,) * len(grad_shapes) + (VMEM,) + (ANY,) * 4,
         scratch_shapes=[
             pltpu.VMEM((2 * width + 16, width), BF16),
@@ -1041,7 +1038,10 @@
     depth_near_one = lax.ppermute(piece_one, ("c", "t"), to_near)
     normed_other = lax.ppermute(normed_one, "c", swap)
     piece_two = pack_hidden(place, up_weight, down_weight)
-    depth_near_one, normed_other, piece_two = together(depth_near_one, normed_other, piece_two)
+    both_two = jnp.concatenate([up_weight, down_weight])
+    depth_near_one, normed_other, piece_two, both_two = together(
+        depth_near_one, normed_other, piece_two, both_two
+    )
     near_one = spread(depth_near_one)
     far_projection = lax.ppermute(after(projection, depth_near_one), ("c", "t"), to_far)
     far_mixer = lax.ppermute(after(tail_one, depth_near_one), ("c", "t"), to_far)
@@ -1055,12 +1055,12 @@
     part_received = lax.ppermute(part, "c", swap)
     near_x = lax.ppermute(near_two, "b", swap)
     near_y = lax.ppermute(near_two, "a", swap)
-    far_up = lax.ppermute(after(up_weight, near_two), ("c", "t"), to_far)
+    far_two = lax.ppermute(after(both_two, near_two), ("c", "t"), to_far)
     saved, soft, part = attention(
         place, own_one, near_one, far_one, normed_one, (saved, soft), F32
     )
-    part, part_received, near_x, near_y, far_up, grad_other = together(
-        part, part_received, near_x, near_y, far_up, grad_other
+    part, part_received, near_x, near_y, grad_other = together(
+        part, part_received, near_x, near_y, grad_other
     )
     quarter = near_two.shape[0] // 2
     near_up = lax.ppermute(near_y[:quarter], "b", swap)
@@ -1077,18 +1077,17 @@
         normed_two, first_sum, near_up, near_down
     )
     normed_two_other = lax.ppermute(normed_two, "c", swap)
-    far_down = lax.ppermute(after(down_weight, far_up), ("c", "t"), to_far)
     normed_two_both = (normed_two, normed_two_other)
 
     grad_both = (output_grad, grad_other)
     pieces = (near_two, near_x, near_y, near_up, near_down, depth_near_one)
     near_outs = hidden_block(place, pieces, normed_two_both, grad_both, False)
-    near_outs, far_down = together(near_outs, far_down)
+    near_outs, far_two = together(near_outs, far_two)
     *grads_near, bias_near, out_near, out_send, back_near, back_send = near_outs
     stage_near = first_exchange(*grads_near)
     back_near_received = lax.ppermute(back_send, "c", swap)
     out_near_received = lax.ppermute(out_send, "c", swap)
-    shards = (up_weight, down_weight, tail_one, far_up, far_down, far_mixer)
+    shards = (both_two, tail_one, far_two, far_mixer)
     far_outs = hidden_block(place, shards, normed_two_both, grad_both, True)
     far_outs, stage_near, back_near_received, out_near_received = together(
         far_outs, stage_near, back_near_received, out_near_received

time: 251 us -> 245 us (0.976)
  starting transfers between devices: 83.7 us -> 79.2 us
    ppermute x1, starting transfers between devices: 18 us -> 11.3 us  [local(): grad_other = lax.ppermute(after(output_grad, part), 'c', swap)]
    ppermute x3, waiting for transfers between devices: 6.13 us -> 12.7 us  [spread(): lax.ppermute(piece, 'a', swap)]
    ppermute x3, waiting for transfers between devices: 8.58 us -> 3.05 us  [spread(): lax.ppermute(piece, ('a', 'b'), cross)]
  transfers between devices with their start and end apart: 58 -> 57, of which waited for: 23 -> 22; matrix products, arithmetic and copies ran while one was open for 1% -> 1% of each run, Pallas kernels for 39% -> 40%
where the time goes in v1:
time: 245 us; the launch traced here: 244 us
  Pallas kernels  104 us (42%)
  starting transfers between devices  79.2 us (32%)
  waiting for transfers between devices  52.5 us (21%)
  local copies, waits for them, and re-layouts  5.69 us (2%)
    pallas_call x2, Pallas kernels, hidden_block(): pl.pallas_call(functools.partial(hidden_kernel, last), out_shape=(*grad_s...  30.3 us
    pallas_call x2, Pallas kernels, attention_back(): pl.pallas_call(functools.partial(attention_back_kernel, heads, far), grid...  24.6 us
    pallas_call x2, Pallas kernels, attention(): pl.pallas_call(functools.partial(attention_kernel, heads), grid=(tiles,),...  20.4 us
    ppermute x3, waiting for transfers between devices, spread(): lax.ppermute(piece, 'a', swap)  12.7 us
    ppermute x1, starting transfers between devices, local(): grad_other = lax.ppermute(after(output_grad, part), 'c', swap)  11.3 us
    ppermute x1, waiting for transfers between devices, local(): depth_near_one = lax.ppermute(piece_one, ('c', 't'), to_near)  8.54 us
    ppermute x1, starting transfers between devices, local(): received_far = lax.ppermute(send_far, 'c', swap)  5.92 us
    ppermute x3, starting transfers between devices, direct(): lax.ppermute(send_y, 'a', swap)  5.32 us
  transfers between devices with their start and end apart: 57, of which 22 were waited for; matrix products, arithmetic and copies ran while one was open for 1% of the time, Pallas kernels for 40%

profile of v1, /device:TPU:0, one launch (start us, length us, event | category | flops | bytes accessed | tf_op | source)
XLA Modules:
  0.0 244.3 jit_solution(16737825937794422581)
XLA Ops:
  0.8 1.2 copy-done.1
  4.0 2.2 shard_map.254.normed.counts.rest_4_
  6.8 1.8 shard_map.255
  8.5 2.7 %collective-permute-start = (bf16[208,768]{1,0:T(8,128)(2,1)S(1)}, bf16[208,768]{1,0:T(8,128)(2,1)S(1)}, u32[]{:S(2)}, u32[]{:S(2)}) collective-permute-start(bf16[208,768]{1,0:T(8,128)(2,1)S(1)} %get-tuple-element.194), channel_id=1, source_target_pairs={{0,1},{1,2},{2,3},{3,0},{4,6},{5,7},{6,4},{7,5},{8,9},{9,10},{10,1... | collective-permute-start | bytes 958472 | tf_op jit(solution)/shard_map/ppermute | solution.py:1038
  11.2 1.6 shard_map.256
  13.0 8.5 %collective-permute-done.near0.rest_5_.rest_0_ = bf16[208,768]{1,0:T(8,128)(2,1)S(1)} collective-permute-done((bf16[208,768]{1,0:T(8,128)(2,1)S(1)}, bf16[208,768]{1,0:T(8,128)(2,1)S(1)}, u32[]{:S(2)}, u32[]{:S(2)}) %collective-permute-start) | collective-permute-done | bytes 319520 | tf_op jit(solution)/shard_map/ppermute | solution.py:1038
  23.1 1.6 collective-permute-start.2
  24.7 1.5 collective-permute-start.3
  26.7 3.5 %collective-permute-done.2.near1.rest_1_ = bf16[208,768]{1,0:T(8,128)(2,1)S(1)} collective-permute-done((bf16[208,768]{1,0:T(8,128)(2,1)S(1)}, bf16[208,768]{1,0:T(8,128)(2,1)S(1)}, u32[]{:S(2)}, u32[]{:S(2)}) %collective-permute-start.2) | collective-permute-done | bytes 319520 | tf_op jit(solution)/shard_map/ppermute | solution.py:997
  30.2 5.2 %collective-permute-done.3.near2.rest_2_ = bf16[208,768]{1,0:T(8,128)(2,1)S(1)} collective-permute-done((bf16[208,768]{1,0:T(8,128)(2,1)S(1)}, bf16[208,768]{1,0:T(8,128)(2,1)S(1)}, u32[]{:S(2)}, u32[]{:S(2)}) %collective-permute-start.3) | collective-permute-done | bytes 319520 | tf_op jit(solution)/shard_map/ppermute | solution.py:998
  35.4 2.2 collective-permute-start.7
  37.6 10.2 %shard_map.257 = (bf16[8,1280,192]{2,1,0:T(8,128)(2,1)}, bf16[1280,768]{1,0:T(8,128)(2,1)}, bf16[640,768]{1,0:T(8,128)(2,1)S(1)}) custom-call(s32[3]{0:T(128)S(1)} %pad_add_fusion.place, bf16[576,768]{1,0:T(8,128)(2,1)S(1)} %bitcast.11, bf16[208,768]{1,0:T(8,128)(2,1)S(1)} %get-tuple-element.199.tail.rest_1_, ...), custom_call_target="tpu_custom_call" | custom-call | flops 1765949440 | bytes 9915200 | tf_op jit(solution)/shard_map/pallas_call | solution.py:488
  47.8 2.3 collective-permute-done.7.rest_0_
  50.0 11.3 %collective-permute-start.11 = (bf16[640,768]{1,0:T(8,128)(2,1)S(1)}, bf16[640,768]{1,0:T(8,128)(2,1)S(1)}, u32[]{:S(2)}, u32[]{:S(2)}) collective-permute-start(bf16[640,768]{1,0:T(8,128)(2,1)S(1)} %copy-done.17), channel_id=1, source_target_pairs={{0,4},{4,0},{1,5},{5,1},{2,6},{6,2},{3,7},{7,3},{8,12},{12,8},{9,1... | collective-permute-start | bytes 2949128 | tf_op jit(solution)/shard_map/ppermute | solution.py:1054
  61.4 1.5 collective-permute-start.10
  62.9 2.0 collective-permute-start.9
  64.9 1.0 collective-permute-start.15
  65.9 10.2 %shard_map.258 = (bf16[8,1280,192]{2,1,0:T(8,128)(2,1)}, bf16[1280,768]{1,0:T(8,128)(2,1)}, f32[640,768]{1,0:T(8,128)S(1)}) custom-call(s32[3]{0:T(128)S(1)} %pad_add_fusion.place, bf16[576,768]{1,0:T(8,128)(2,1)S(1)} %bitcast.12, bf16[208,768]{1,0:T(8,128)(2,1)S(1)} %get-tuple-element.199.tail.rest_1_, ...), custom_call_target="tpu_custom_call", output_to_operand_aliasing={{0}: (11, {}), {1}: (12, {})} | custom-call | flops 1765949440 | bytes 9915200 | tf_op jit(solution)/shard_map/pallas_call | solution.py:488
  76.1 0.9 collective-permute-done.10.rest_2_
  77.0 1.5 collective-permute-done.9.rest_1_
  78.6 1.8 collective-permute-start.12
  80.8 3.7 %shard_map.259 = (f32[640,768]{1,0:T(8,128)}, bf16[640,768]{1,0:T(8,128)(2,1)S(1)}) custom-call(bf16[640,768]{1,0:T(8,128)(2,1)} %tokens.5, f32[640,768]{1,0:T(8,128)S(1)} %get-tuple-element.213.mine, bf16[640,768]{1,0:T(8,128)(2,1)S(1)} %collective-permute-done.8.received, f32[1,768]{1,0:T(1,128)S(1)} %reshape.55.bias, f32[1,768]{1,0:T(1,128)S(1)} %reshape.56.gain, ...), custom_call_target="tpu_custom_call" | custom-call | flops 5898240 | bytes 6881280 | tf_op jit(solution)/shard_map/pallas_call | solution.py:133
  84.5 2.2 collective-permute-done.12.rest_3_
  86.7 2.9 %collective-permute-done.13.rest_4_ = bf16[192,768]{1,0:T(8,128)(2,1)S(1)} collective-permute-done((bf16[192,768]{1,0:T(8,128)(2,1)S(1)}, bf16[192,768]{1,0:T(8,128)(2,1)S(1)}, u32[]{:S(2)}, u32[]{:S(2)}) %collective-permute-start.13) | collective-permute-done | bytes 294944 | tf_op jit(solution)/shard_map/ppermute | solution.py:1067
  90.2 2.2 collective-permute-done.14.rest_7_.rest_5_
  92.4 0.9 copy-done.27
  93.3 15.2 %shard_map.260 = (bf16[2,2,96,768]{3,2,1,0:T(8,128)(2,1)}, bf16[2,2,96,768]{3,2,1,0:T(8,128)(2,1)}, bf16[2,2,96,768]{3,2,1,0:T(8,128)(2,1)}, bf16[2,2,96,768]{3,...) custom-call(s32[3]{0:T(128)S(1)} %pad_add_fusion.place, ...), custom_call_target="tpu_custom_call" | custom-call | flops 9059696640 | bytes 19796480 | tf_op jit(solution)/shard_map/pallas_call | solution.py:762
  109.7 15.1 %shard_map.261 = (bf16[2,4,2,96,768]{4,3,2,1,0:T(8,128)(2,1)}, f32[8,768]{1,0:T(8,128)S(1)}, bf16[640,768]{1,0:T(8,128)(2,1)}, bf16[640,768]{1,0:T(8,128)(2,1)},...) custom-call(s32[3]{0:T(128)S(1)} %pad_add_fusion.place, bf16[1536,768]{1,0:T(8,128)(2,1)S(1)} %pad_maximum_fusion.rest_0_, ...), custom_call_target="tpu_custom_call" | custom-call | flops 9059696640 | bytes 19796480 | tf_op jit(solution)/shard_map/pallas_call | solution.py:762
  125.0 0.9 collective-permute-start.24
  126.8 1.0 collective-permute-done.20.part3
  127.8 4.2 %shard_map.263 = (bf16[640,768]{1,0:T(8,128)(2,1)S(1)}, f32[8,768]{1,0:T(8,128)S(1)}) custom-call(bf16[640,768]{1,0:T(8,128)(2,1)S(1)} %copy-done.4, bf16[640,768]{1,0:T(8,128)(2,1)S(1)} %collective-permute-done.18.part1, bf16[640,768]{1,0:T(8,128)(2,1)S(1)} %copy-done.5, bf16[640,768]{1,0:T(8,128)(2,1)S(1)} %collective-permute-done.20.part3, ...), custom_call_target="tpu_custom_call" | custom-call | flops 12288000 | bytes 8847360 | tf_op jit(solution)/shard_map/pallas_call | solution.py:174
  132.0 2.1 collective-permute-start.21
  134.1 2.2 collective-permute-done.21.rest_7_
  136.6 1.6 collective-permute-start.22
  138.2 1.4 collective-permute-start.23
  139.6 12.4 %shard_map.264 = (bf16[2,1,96,768]{3,2,1,0:T(8,128)(2,1)S(1)}, bf16[2,1,96,768]{3,2,1,0:T(8,128)(2,1)S(1)}, bf16[2,1,96,768]{3,2,1,0:T(8,128)(2,1)S(1)}, bf16[2,...) custom-call(s32[3]{0:T(128)S(1)} %pad_add_fusion.place, ...), custom_call_target="tpu_custom_call" | custom-call | flops 3215155200 | bytes 13830400 | tf_op jit(solution)/shard_map/pallas_call | solution.py:619
  152.8 5.9 %collective-permute-start.26 = (bf16[4,2,96,768]{3,2,1,0:T(8,128)(2,1)S(1)}, bf16[4,2,96,768]{3,2,1,0:T(8,128)(2,1)S(1)}, u32[]{:S(2)}, u32[]{:S(2)}) collective-permute-start(bf16[4,2,96,768]{3,2,1,0:T(8,128)(2,1)S(1)} %get-tuple-element.276), channel_id=1, source_target_pairs={{0,4},{4,0},{1,5},{5,1},{2,6},{6,2},{3,7},{7,3},{8,12},{12,8},{9,1... | collective-permute-start | bytes 3538952 | tf_op jit(solution)/shard_map/ppermute | solution.py:1124
  158.7 1.7 collective-permute-start.31
  160.5 1.6 collective-permute-start.28
  162.0 1.4 collective-permute-start.29
  164.0 12.2 %shard_map.266 = (bf16[2,1,96,768]{3,2,1,0:T(8,128)(2,1)S(1)}, bf16[2,1,96,768]{3,2,1,0:T(8,128)(2,1)S(1)}, bf16[2,1,96,768]{3,2,1,0:T(8,128)(2,1)S(1)}, bf16[2,...) custom-call(s32[3]{0:T(128)S(1)} %pad_add_fusion.place, ...), custom_call_target="tpu_custom_call" | custom-call | flops 3215155200 | bytes 13830400 | tf_op jit(solution)/shard_map/pallas_call | solution.py:619
  176.3 3.5 %collective-permute-start.32 = (bf16[640,768]{1,0:T(8,128)(2,1)S(1)}, bf16[640,768]{1,0:T(8,128)(2,1)S(1)}, u32[]{:S(2)}, u32[]{:S(2)}) collective-permute-start(bf16[640,768]{1,0:T(8,128)(2,1)S(1)} %get-tuple-element.291), channel_id=1, source_target_pairs={{0,4},{4,0},{1,5},{5,1},{2,6},{6,2},{3,7},{7,3},{8,12},{12,8},{9,1... | collective-permute-start | bytes 2949128 | tf_op jit(solution)/shard_map/ppermute | solution.py:1136
  179.8 1.1 shard_map.268
  181.4 1.6 collective-permute-start.34
  183.0 1.4 collective-permute-start.35
  185.0 5.0 %shard_map.267 = (f32[640,768]{1,0:T(8,128)}, f32[16,768]{1,0:T(8,128)S(1)}) custom-call(s32[3]{0:T(128)S(1)} %pad_add_fusion.place, bf16[640,768]{1,0:T(8,128)(2,1)S(1)} %get-tuple-element.270.part0, bf16[640,768]{1,0:T(8,128)(2,1)S(1)} %collective-permute-done.27.part1, bf16[640,768]{1,0:T(8,128)(2,1)S(1)} %get-tuple-element.290.part2, ...), custom_call_target="tpu_custom_call" | custom-call | flops 12288000 | bytes 7864320 | tf_op jit(solution)/shard_map/pallas_call | solution.py:233
  190.0 2.8 %collective-permute-start.39 = (bf16[2,1,96,768]{3,2,1,0:T(8,128)(2,1)S(1)}, bf16[2,1,96,768]{3,2,1,0:T(8,128)(2,1)S(1)}, u32[]{:S(2)}, u32[]{:S(2)}) collective-permute-start(bf16[2,1,96,768]{3,2,1,0:T(8,128)(2,1)S(1)} %get-tuple-element.315), channel_id=1, source_target_pairs={{1,0},{2,1},{3,2},{0,3},{6,4},{7,5},{4,6},{5,7},{9,8},{10,9},{11,1... | collective-permute-start | bytes 884744 | tf_op jit(solution)/shard_map/ppermute | solution.py:1143
  192.9 1.6 collective-permute-start.44
  194.4 3.6 %collective-permute-done.35.refs_2_ = bf16[2,1,96,768]{3,2,1,0:T(8,128)(2,1)S(1)} collective-permute-done((bf16[2,1,96,768]{3,2,1,0:T(8,128)(2,1)S(1)}, bf16[2,1,96,768]{3,2,1,0:T(8,128)(2,1)S(1)}, u32[]{:S(2)}, u32[]{:S(2)}) %collective-permute-start.35) | collective-permute-done | bytes 294944 | tf_op jit(solution)/shard_map/ppermute | solution.py:1020
  198.0 2.5 %collective-permute-start.45 = (bf16[2,96,768]{2,1,0:T(8,128)(2,1)S(1)}, bf16[2,96,768]{2,1,0:T(8,128)(2,1)S(1)}, u32[]{:S(2)}, u32[]{:S(2)}) collective-permute-start(bf16[2,96,768]{2,1,0:T(8,128)(2,1)S(1)} %get-tuple-element.329), channel_id=1, source_target_pairs={{0,16},{16,0},{1,17},{17,1},{2,18},{18,2},{3,19},{19,3},{4,20},{20... | collective-permute-start | bytes 884744 | tf_op jit(solution)/shard_map/ppermute | solution.py:1020
  201.9 1.6 add_convert_fusion
  204.2 4.7 %collective-permute-start.40 = (bf16[1,96,768]{2,1,0:T(8,128)(2,1)S(1)}, bf16[1,96,768]{2,1,0:T(8,128)(2,1)S(1)}, u32[]{:S(2)}, u32[]{:S(2)}) collective-permute-start(bf16[1,96,768]{2,1,0:T(8,128)(2,1)S(1)} %get-tuple-element.325), channel_id=1, source_target_pairs={{0,4},{4,0},{1,5},{5,1},{2,6},{6,2},{3,7},{7,3},{8,12},{12,8},{9,1... | collective-permute-start | bytes 442376 | tf_op jit(solution)/shard_map/ppermute | solution.py:1175
  209.4 1.6 collective-permute-start.42
  211.5 0.9 collective-permute-start.43
  213.5 3.0 %collective-permute-done.43.refs_11_ = f32[16,768]{1,0:T(8,128)S(1)} collective-permute-done((f32[16,768]{1,0:T(8,128)S(1)}, f32[16,768]{1,0:T(8,128)S(1)}, u32[]{:S(2)}, u32[]{:S(2)}) %collective-permute-start.43) | collective-permute-done | bytes 49184 | tf_op jit(solution)/shard_map/ppermute | solution.py:999
  217.7 1.0 collective-permute-start.47
  218.7 1.5 collective-permute-start.48
  220.2 1.5 collective-permute-start.49
  221.7 3.4 %collective-permute-start.51 = (f32[16,768]{1,0:T(8,128)S(1)}, f32[16,768]{1,0:T(8,128)S(1)}, u32[]{:S(2)}, u32[]{:S(2)}) collective-permute-start(f32[16,768]{1,0:T(8,128)S(1)} %get-tuple-element.343), channel_id=1, source_target_pairs={{0,2},{1,3},{2,0},{3,1},{4,6},{5,7},{6,4},{7,5},{8,10},{9,11},{10,... | collective-permute-start | bytes 147464 | tf_op jit(solution)/shard_map/ppermute | solution.py:1185
  225.1 2.2 collective-permute-done.51
  227.3 1.9 collective-permute-done.52
  230.8 7.1 %collective-permute-done.48.refs_2_ = bf16[3,96,768]{2,1,0:T(8,128)(2,1)S(1)} collective-permute-done((bf16[3,96,768]{2,1,0:T(8,128)(2,1)S(1)}, bf16[3,96,768]{2,1,0:T(8,128)(2,1)S(1)}, u32[]{:S(2)}, u32[]{:S(2)}) %collective-permute-start.48) | collective-permute-done | bytes 442400 | tf_op jit(solution)/shard_map/ppermute | solution.py:998
  238.9 2.5 %shard_map.272 = (f32[576,768]{1,0:T(8,128)}, f32[192,768]{1,0:T(8,128)}, f32[768,768]{1,0:T(8,128)}, f32[768,768]{1,0:T(8,128)}) custom-call(s32[3]{0:T(128)S(1)} %pad_add_fusion.place, bf16[3,96,768]{2,1,0:T(8,128)(2,1)S(1)} %get-tuple-element.346.refs_0_, bf16[3,96,768]{2,1,0:T(8,128)(2,1)S(1)} %collective-permute-done.47.refs_1_, ...), custom_call_target="tpu_custom_call" | custom-call | bytes 5308416 | tf_op jit(solution)/shard_map/pallas_call | solution.py:943
  241.6 2.5 %shard_map.273 = (f32[576,768]{1,0:T(8,128)}, f32[192,768]{1,0:T(8,128)}, f32[768,768]{1,0:T(8,128)}, f32[768,768]{1,0:T(8,128)}) custom-call(s32[3]{0:T(128)S(1)} %pad_add_fusion.place, bf16[3,96,768]{2,1,0:T(8,128)(2,1)S(1)} %collective-permute-done.53.refs_0_, ...), custom_call_target="tpu_custom_call", output_to_operand_aliasing={{0}: (5, {}), {1}: (6, {}), {2}: (7, {}), {3}: (8, {})} | custom-call | bytes 5308416 | tf_op jit(solution)/shard_map/pallas_call | solution.py:943
  (140 shorter events, 19.3 us)
Async XLA Ops:
  6.2 15.4 %collective-permute-start.1 = (bf16[656,768]{1,0:T(8,128)(2,1)S(1)}, bf16[656,768]{1,0:T(8,128)(2,1)S(1)}, u32[]{:S(2)}, u32[]{:S(2)}) collective-permute-start(bf16[656,768]{1,0:T(8,128)(2,1)S(1)} %shard_map.254.normed.counts.rest_4_), channel_id=1, source_target_pairs={{0,4},{4,0},{1,5},{5,1},{2,6},{6,2},{3,7},{7,3},{8,12},{12,8},{9,1... | collective-permute-start | bytes 3022856 | tf_op jit(solution)/shard_map/ppermute | solution.py:1039
  8.5 13.0 %collective-permute-start = (bf16[208,768]{1,0:T(8,128)(2,1)S(1)}, bf16[208,768]{1,0:T(8,128)(2,1)S(1)}, u32[]{:S(2)}, u32[]{:S(2)}) collective-permute-start(bf16[208,768]{1,0:T(8,128)(2,1)S(1)} %get-tuple-element.194), channel_id=1, source_target_pairs={{0,1},{1,2},{2,3},{3,0},{4,6},{5,7},{6,4},{7,5},{8,9},{9,10},{10,1... | collective-permute-start | bytes 958472 | tf_op jit(solution)/shard_map/ppermute | solution.py:1038
  21.6 16.0 %collective-permute-start.5 = (bf16[576,768]{1,0:T(8,128)(2,1)S(1)}, bf16[576,768]{1,0:T(8,128)(2,1)S(1)}, u32[]{:S(2)}, u32[]{:S(2)}) collective-permute-start(bf16[576,768]{1,0:T(8,128)(2,1)S(1)} %bitcast.10), channel_id=1, source_target_pairs={{4,7},{5,4},{6,5},{7,6},{12,15},{13,12},{14,13},{15,14},{20,23},{2... | collective-permute-start | bytes 2654216 | tf_op jit(solution)/shard_map/ppermute | solution.py:1046
  22.3 27.7 %copy-start.17 = (bf16[640,768]{1,0:T(8,128)(2,1)S(1)}, bf16[640,768]{1,0:T(8,128)(2,1)}, u32[]{:S(2)}) copy-start(bf16[640,768]{1,0:T(8,128)(2,1)} %output_grad.1) | copy-start | bytes 2949124
  22.3 4.4 %collective-permute-start.6 = (bf16[208,768]{1,0:T(8,128)(2,1)S(1)}, bf16[208,768]{1,0:T(8,128)(2,1)S(1)}, u32[]{:S(2)}, u32[]{:S(2)}) collective-permute-start(bf16[208,768]{1,0:T(8,128)(2,1)S(1)} %get-tuple-element.199.tail.rest_1_), channel_id=1, source_target_pairs={{4,7},{5,4},{6,5},{7,6},{12,15},{13,12},{14,13},{15,14},{20,23},{2... | collective-permute-start | bytes 958472 | tf_op jit(solution)/shard_map/ppermute | solution.py:1047
  23.1 7.1 %collective-permute-start.2 = (bf16[208,768]{1,0:T(8,128)(2,1)S(1)}, bf16[208,768]{1,0:T(8,128)(2,1)S(1)}, u32[]{:S(2)}, u32[]{:S(2)}) collective-permute-start(bf16[208,768]{1,0:T(8,128)(2,1)S(1)} %collective-permute-done.near0.rest_5_.rest_0_), channel_id=1, source_target_pairs={{0,8},{8,0},{1,9},{9,1},{2,10},{10,2},{3,11},{11,3},{4,12},{12,4},... | collective-permute-start | bytes 958472 | tf_op jit(solution)/shard_map/ppermute | solution.py:997
  24.7 10.7 %collective-permute-start.3 = (bf16[208,768]{1,0:T(8,128)(2,1)S(1)}, bf16[208,768]{1,0:T(8,128)(2,1)S(1)}, u32[]{:S(2)}, u32[]{:S(2)}) collective-permute-start(bf16[208,768]{1,0:T(8,128)(2,1)S(1)} %collective-permute-done.near0.rest_5_.rest_0_), channel_id=1, source_target_pairs={{0,16},{16,0},{1,17},{17,1},{2,18},{18,2},{3,19},{19,3},{4,20},{20... | collective-permute-start | bytes 958472 | tf_op jit(solution)/shard_map/ppermute | solution.py:998
  26.2 9.2 %collective-permute-start.4 = (bf16[208,768]{1,0:T(8,128)(2,1)S(1)}, bf16[208,768]{1,0:T(8,128)(2,1)S(1)}, u32[]{:S(2)}, u32[]{:S(2)}) collective-permute-start(bf16[208,768]{1,0:T(8,128)(2,1)S(1)} %collective-permute-done.near0.rest_5_.rest_0_), channel_id=1, source_target_pairs={{0,24},{8,16},{16,8},{24,0},{1,25},{9,17},{17,9},{25,1},{2,26},{10... | collective-permute-start | bytes 958472 | tf_op jit(solution)/shard_map/ppermute | solution.py:999
  35.4 14.6 %collective-permute-start.7 = (bf16[384,768]{1,0:T(8,128)(2,1)S(1)}, bf16[384,768]{1,0:T(8,128)(2,1)S(1)}, u32[]{:S(2)}, u32[]{:S(2)}) collective-permute-start(bf16[384,768]{1,0:T(8,128)(2,1)S(1)} %shard_map.256), channel_id=1, source_target_pairs={{0,1},{1,2},{2,3},{3,0},{4,6},{5,7},{6,4},{7,5},{8,9},{9,10},{10,1... | collective-permute-start | bytes 1769480 | tf_op jit(solution)/shard_map/ppermute | solution.py:1048
  50.0 30.8 %copy-start.21 = (f32[768]{0:T(1024)S(1)}, f32[768]{0:T(1024)}, u32[]{:S(2)}) copy-start(f32[768]{0:T(1024)} %param.23) | copy-start | bytes 9220
  50.0 30.8 %copy-start.22 = (f32[768]{0:T(1024)S(1)}, f32[768]{0:T(1024)}, u32[]{:S(2)}) copy-start(f32[768]{0:T(1024)} %param.22) | copy-start | bytes 9220
  50.0 30.8 %copy-start.23 = (f32[768]{0:T(1024)S(1)}, f32[768]{0:T(1024)}, u32[]{:S(2)}) copy-start(f32[768]{0:T(1024)} %param.24) | copy-start | bytes 9220
  50.0 28.5 %collective-permute-start.11 = (bf16[640,768]{1,0:T(8,128)(2,1)S(1)}, bf16[640,768]{1,0:T(8,128)(2,1)S(1)}, u32[]{:S(2)}, u32[]{:S(2)}) collective-permute-start(bf16[640,768]{1,0:T(8,128)(2,1)S(1)} %copy-done.17), channel_id=1, source_target_pairs={{0,4},{4,0},{1,5},{5,1},{2,6},{6,2},{3,7},{7,3},{8,12},{12,8},{9,1... | collective-permute-start | bytes 2949128 | tf_op jit(solution)/shard_map/ppermute | solution.py:1054
  61.3 17.3 %collective-permute-start.8 = (bf16[640,768]{1,0:T(8,128)(2,1)S(1)}, bf16[640,768]{1,0:T(8,128)(2,1)S(1)}, u32[]{:S(2)}, u32[]{:S(2)}) collective-permute-start(bf16[640,768]{1,0:T(8,128)(2,1)S(1)} %get-tuple-element.209), channel_id=1, source_target_pairs={{0,4},{4,0},{1,5},{5,1},{2,6},{6,2},{3,7},{7,3},{8,12},{12,8},{9,1... | collective-permute-start | bytes 2949128 | tf_op jit(solution)/shard_map/ppermute | solution.py:1055
  61.4 15.7 %collective-permute-start.10 = (bf16[384,768]{1,0:T(8,128)(2,1)S(1)}, bf16[384,768]{1,0:T(8,128)(2,1)S(1)}, u32[]{:S(2)}, u32[]{:S(2)}) collective-permute-start(bf16[384,768]{1,0:T(8,128)(2,1)S(1)} %collective-permute-done.7.rest_0_), channel_id=1, source_target_pairs={{0,16},{16,0},{1,17},{17,1},{2,18},{18,2},{3,19},{19,3},{4,20},{20... | collective-permute-start | bytes 1769480 | tf_op jit(solution)/shard_map/ppermute | solution.py:1057
  62.9 15.7 %collective-permute-start.9 = (bf16[384,768]{1,0:T(8,128)(2,1)S(1)}, bf16[384,768]{1,0:T(8,128)(2,1)S(1)}, u32[]{:S(2)}, u32[]{:S(2)}) collective-permute-start(bf16[384,768]{1,0:T(8,128)(2,1)S(1)} %collective-permute-done.7.rest_0_), channel_id=1, source_target_pairs={{0,8},{8,0},{1,9},{9,1},{2,10},{10,2},{3,11},{11,3},{4,12},{12,4},... | collective-permute-start | bytes 1769480 | tf_op jit(solution)/shard_map/ppermute | solution.py:1056
  64.9 43.6 %collective-permute-start.15 = (bf16[1536,768]{1,0:T(8,128)(2,1)S(1)}, bf16[1536,768]{1,0:T(8,128)(2,1)S(1)}, u32[]{:S(2)}, u32[]{:S(2)}) collective-permute-start(bf16[1536,768]{1,0:T(8,128)(2,1)S(1)} %pad_maximum_fusion.rest_0_), channel_id=1, source_target_pairs={{4,7},{5,4},{6,5},{7,6},{12,15},{13,12},{14,13},{15,14},{20,23},{2... | collective-permute-start | bytes 7077896 | tf_op jit(solution)/shard_map/ppermute | solution.py:1058
  78.6 8.1 %collective-permute-start.12 = (bf16[192,768]{1,0:T(8,128)(2,1)S(1)}, bf16[192,768]{1,0:T(8,128)(2,1)S(1)}, u32[]{:S(2)}, u32[]{:S(2)}) collective-permute-start(bf16[192,768]{1,0:T(8,128)(2,1)S(1)} %slice.30), channel_id=1, source_target_pairs={{0,8},{8,0},{1,9},{9,1},{2,10},{10,2},{3,11},{11,3},{4,12},{12,4},... | collective-permute-start | bytes 884744 | tf_op jit(solution)/shard_map/ppermute | solution.py:1066
  80.4 9.1 %collective-permute-start.13 = (bf16[192,768]{1,0:T(8,128)(2,1)S(1)}, bf16[192,768]{1,0:T(8,128)(2,1)S(1)}, u32[]{:S(2)}, u32[]{:S(2)}) collective-permute-start(bf16[192,768]{1,0:T(8,128)(2,1)S(1)} %slice.31), channel_id=1, source_target_pairs={{0,16},{16,0},{1,17},{17,1},{2,18},{18,2},{3,19},{19,3},{4,20},{20... | collective-permute-start | bytes 884744 | tf_op jit(solution)/shard_map/ppermute | solution.py:1067
  89.5 2.8 %collective-permute-start.14 = (bf16[640,768]{1,0:T(8,128)(2,1)S(1)}, bf16[640,768]{1,0:T(8,128)(2,1)S(1)}, u32[]{:S(2)}, u32[]{:S(2)}) collective-permute-start(bf16[640,768]{1,0:T(8,128)(2,1)S(1)} %get-tuple-element.219.rest_6_.rest_4_), channel_id=1, source_target_pairs={{0,4},{4,0},{1,5},{5,1},{2,6},{6,2},{3,7},{7,3},{8,12},{12,8},{9,1... | collective-permute-start | bytes 2949128 | tf_op jit(solution)/shard_map/ppermute | solution.py:1079
  108.5 17.5 %copy-start.6 = (bf16[2,2,96,768]{3,2,1,0:T(8,128)(2,1)S(1)}, bf16[2,2,96,768]{3,2,1,0:T(8,128)(2,1)}, u32[]{:S(2)}) copy-start(bf16[2,2,96,768]{3,2,1,0:T(8,128)(2,1)} %get-tuple-element.249.refs_0_) | copy-start | bytes 1769476
  108.5 17.5 %copy-start.7 = (bf16[2,2,96,768]{3,2,1,0:T(8,128)(2,1)S(1)}, bf16[2,2,96,768]{3,2,1,0:T(8,128)(2,1)}, u32[]{:S(2)}) copy-start(bf16[2,2,96,768]{3,2,1,0:T(8,128)(2,1)} %get-tuple-element.250.refs_1_) | copy-start | bytes 1769476
  108.6 16.4 %collective-permute-start.18 = (bf16[640,768]{1,0:T(8,128)(2,1)}, bf16[640,768]{1,0:T(8,128)(2,1)S(1)}, u32[]{:S(2)}, u32[]{:S(2)}) collective-permute-start(bf16[640,768]{1,0:T(8,128)(2,1)} %get-tuple-element.244), channel_id=1, source_target_pairs={{0,4},{4,0},{1,5},{5,1},{2,6},{6,2},{3,7},{7,3},{8,12},{12,8},{9,1... | collective-permute-start | bytes 2949128 | tf_op jit(solution)/shard_map/ppermute | solution.py:1088
  109.0 16.0 %collective-permute-start.19 = (bf16[640,768]{1,0:T(8,128)(2,1)}, bf16[640,768]{1,0:T(8,128)(2,1)S(1)}, u32[]{:S(2)}, u32[]{:S(2)}) collective-permute-start(bf16[640,768]{1,0:T(8,128)(2,1)} %get-tuple-element.245), channel_id=1, source_target_pairs={{0,4},{4,0},{1,5},{5,1},{2,6},{6,2},{3,7},{7,3},{8,12},{12,8},{9,1... | collective-permute-start | bytes 2949128 | tf_op jit(solution)/shard_map/ppermute | solution.py:1089
  109.1 15.8 %collective-permute-start.16 = (bf16[2,2,96,768]{3,2,1,0:T(8,128)(2,1)}, bf16[2,2,96,768]{3,2,1,0:T(8,128)(2,1)S(1)}, u32[]{:S(2)}, u32[]{:S(2)}) collective-permute-start(bf16[2,2,96,768]{3,2,1,0:T(8,128)(2,1)} %get-tuple-element.242), channel_id=1, source_target_pairs={{0,8},{8,0},{1,9},{9,1},{2,10},{10,2},{3,11},{11,3},{4,12},{12,4},... | collective-permute-start | bytes 1769480 | tf_op jit(solution)/shard_map/ppermute | solution.py:1009
  109.4 15.5 %collective-permute-start.17 = (bf16[2,2,96,768]{3,2,1,0:T(8,128)(2,1)}, bf16[2,2,96,768]{3,2,1,0:T(8,128)(2,1)S(1)}, u32[]{:S(2)}, u32[]{:S(2)}) collective-permute-start(bf16[2,2,96,768]{3,2,1,0:T(8,128)(2,1)} %get-tuple-element.243), channel_id=1, source_target_pairs={{0,16},{16,0},{1,17},{17,1},{2,18},{18,2},{3,19},{19,3},{4,20},{20... | collective-permute-start | bytes 1769480 | tf_op jit(solution)/shard_map/ppermute | solution.py:1010
  125.0 2.8 %collective-permute-start.20 = (bf16[640,768]{1,0:T(8,128)(2,1)}, bf16[640,768]{1,0:T(8,128)(2,1)S(1)}, u32[]{:S(2)}, u32[]{:S(2)}) collective-permute-start(bf16[640,768]{1,0:T(8,128)(2,1)} %get-tuple-element.248), channel_id=1, source_target_pairs={{0,4},{4,0},{1,5},{5,1},{2,6},{6,2},{3,7},{7,3},{8,12},{12,8},{9,1... | collective-permute-start | bytes 2949128 | tf_op jit(solution)/shard_map/ppermute | solution.py:1098
  125.0 27.0 %collective-permute-start.24 = (bf16[2,4,2,96,768]{4,3,2,1,0:T(8,128)(2,1)}, bf16[2,4,2,96,768]{4,3,2,1,0:T(8,128)(2,1)S(1)}, u32[]{:S(2)}, u32[]{:S(2)}) collective-permute-start(bf16[2,4,2,96,768]{4,3,2,1,0:T(8,128)(2,1)} %get-tuple-element.267.refs_3_.refs_4_), channel_id=1, source_target_pairs={{7,4},{4,5},{5,6},{6,7},{15,12},{12,13},{13,14},{14,15},{23,20},{2... | collective-permute-start | bytes 7077896 | tf_op jit(solution)/shard_map/ppermute | solution.py:1097
  132.0 32.0 %copy-start.2 = (bf16[640,768]{1,0:T(8,128)(2,1)}, bf16[640,768]{1,0:T(8,128)(2,1)S(1)}, u32[]{:S(2)}) copy-start(bf16[640,768]{1,0:T(8,128)(2,1)S(1)} %get-tuple-element.279.rest_6_.grad_first) | copy-start | bytes 2949124
  132.0 4.3 %collective-permute-start.21 = (bf16[640,768]{1,0:T(8,128)(2,1)S(1)}, bf16[640,768]{1,0:T(8,128)(2,1)S(1)}, u32[]{:S(2)}, u32[]{:S(2)}) collective-permute-start(bf16[640,768]{1,0:T(8,128)(2,1)S(1)} %get-tuple-element.279.rest_6_.grad_first), channel_id=1, source_target_pairs={{0,4},{4,0},{1,5},{5,1},{2,6},{6,2},{3,7},{7,3},{8,12},{12,8},{9,1... | collective-permute-start | bytes 2949128 | tf_op jit(solution)/shard_map/ppermute | solution.py:1108
  136.3 15.8 %collective-permute-start.25 = (bf16[640,768]{1,0:T(8,128)(2,1)S(1)}, bf16[640,768]{1,0:T(8,128)(2,1)S(1)}, u32[]{:S(2)}, u32[]{:S(2)}) collective-permute-start(bf16[640,768]{1,0:T(8,128)(2,1)S(1)} %copy-done.26), channel_id=1, source_target_pairs={{0,4},{4,0},{1,5},{5,1},{2,6},{6,2},{3,7},{7,3},{8,12},{12,8},{9,1... | collective-permute-start | bytes 2949128 | tf_op jit(solution)/shard_map/ppermute | solution.py:1109
  136.6 15.4 %collective-permute-start.22 = (bf16[2,96,768]{2,1,0:T(8,128)(2,1)S(1)}, bf16[2,96,768]{2,1,0:T(8,128)(2,1)S(1)}, u32[]{:S(2)}, u32[]{:S(2)}) collective-permute-start(bf16[2,96,768]{2,1,0:T(8,128)(2,1)S(1)} %get-tuple-element.253), channel_id=1, source_target_pairs={{0,16},{16,0},{1,17},{17,1},{2,18},{18,2},{3,19},{19,3},{4,20},{20... | collective-permute-start | bytes 884744 | tf_op jit(solution)/shard_map/ppermute | solution.py:1014
  138.2 13.8 %collective-permute-start.23 = (bf16[2,96,768]{2,1,0:T(8,128)(2,1)S(1)}, bf16[2,96,768]{2,1,0:T(8,128)(2,1)S(1)}, u32[]{:S(2)}, u32[]{:S(2)}) collective-permute-start(bf16[2,96,768]{2,1,0:T(8,128)(2,1)S(1)} %get-tuple-element.254), channel_id=1, source_target_pairs={{0,8},{8,0},{1,9},{9,1},{2,10},{10,2},{3,11},{11,3},{4,12},{12,4},... | collective-permute-start | bytes 884744 | tf_op jit(solution)/shard_map/ppermute | solution.py:1014
  152.8 23.4 %collective-permute-start.26 = (bf16[4,2,96,768]{3,2,1,0:T(8,128)(2,1)S(1)}, bf16[4,2,96,768]{3,2,1,0:T(8,128)(2,1)S(1)}, u32[]{:S(2)}, u32[]{:S(2)}) collective-permute-start(bf16[4,2,96,768]{3,2,1,0:T(8,128)(2,1)S(1)} %get-tuple-element.276), channel_id=1, source_target_pairs={{0,4},{4,0},{1,5},{5,1},{2,6},{6,2},{3,7},{7,3},{8,12},{12,8},{9,1... | collective-permute-start | bytes 3538952 | tf_op jit(solution)/shard_map/ppermute | solution.py:1124
  158.7 17.5 %collective-permute-start.31 = (bf16[2,2,96,768]{3,2,1,0:T(8,128)(2,1)S(1)}, bf16[2,2,96,768]{3,2,1,0:T(8,128)(2,1)S(1)}, u32[]{:S(2)}, u32[]{:S(2)}) collective-permute-start(bf16[2,2,96,768]{3,2,1,0:T(8,128)(2,1)S(1)} %get-tuple-element.278), channel_id=1, source_target_pairs={{1,0},{2,1},{3,2},{0,3},{6,4},{7,5},{4,6},{5,7},{9,8},{10,9},{11,1... | collective-permute-start | bytes 1769480 | tf_op jit(solution)/shard_map/ppermute | solution.py:1123
  160.5 15.7 %collective-permute-start.28 = (bf16[2,1,96,768]{3,2,1,0:T(8,128)(2,1)S(1)}, bf16[2,1,96,768]{3,2,1,0:T(8,128)(2,1)S(1)}, u32[]{:S(2)}, u32[]{:S(2)}) collective-permute-start(bf16[2,1,96,768]{3,2,1,0:T(8,128)(2,1)S(1)} %get-tuple-element.287), channel_id=1, source_target_pairs={{0,8},{8,0},{1,9},{9,1},{2,10},{10,2},{3,11},{11,3},{4,12},{12,4},... | collective-permute-start | bytes 884744 | tf_op jit(solution)/shard_map/ppermute | solution.py:1019
  162.0 14.2 %collective-permute-start.29 = (bf16[2,1,96,768]{3,2,1,0:T(8,128)(2,1)S(1)}, bf16[2,1,96,768]{3,2,1,0:T(8,128)(2,1)S(1)}, u32[]{:S(2)}, u32[]{:S(2)}) collective-permute-start(bf16[2,1,96,768]{3,2,1,0:T(8,128)(2,1)S(1)} %get-tuple-element.288), channel_id=1, source_target_pairs={{0,16},{16,0},{1,17},{17,1},{2,18},{18,2},{3,19},{19,3},{4,20},{20... | collective-permute-start | bytes 884744 | tf_op jit(solution)/shard_map/ppermute | solution.py:1020
  163.5 12.7 %collective-permute-start.30 = (bf16[2,1,96,768]{3,2,1,0:T(8,128)(2,1)S(1)}, bf16[2,1,96,768]{3,2,1,0:T(8,128)(2,1)S(1)}, u32[]{:S(2)}, u32[]{:S(2)}) collective-permute-start(bf16[2,1,96,768]{3,2,1,0:T(8,128)(2,1)S(1)} %get-tuple-element.289), channel_id=1, source_target_pairs={{0,24},{8,16},{16,8},{24,0},{1,25},{9,17},{17,9},{25,1},{2,26},{10... | collective-permute-start | bytes 884744 | tf_op jit(solution)/shard_map/ppermute | solution.py:1021
  176.3 8.1 %collective-permute-start.32 = (bf16[640,768]{1,0:T(8,128)(2,1)S(1)}, bf16[640,768]{1,0:T(8,128)(2,1)S(1)}, u32[]{:S(2)}, u32[]{:S(2)}) collective-permute-start(bf16[640,768]{1,0:T(8,128)(2,1)S(1)} %get-tuple-element.291), channel_id=1, source_target_pairs={{0,4},{4,0},{1,5},{5,1},{2,6},{6,2},{3,7},{7,3},{8,12},{12,8},{9,1... | collective-permute-start | bytes 2949128 | tf_op jit(solution)/shard_map/ppermute | solution.py:1136
  179.8 5.2 %collective-permute-start.27 = (bf16[640,768]{1,0:T(8,128)(2,1)S(1)}, bf16[640,768]{1,0:T(8,128)(2,1)S(1)}, u32[]{:S(2)}, u32[]{:S(2)}) collective-permute-start(bf16[640,768]{1,0:T(8,128)(2,1)S(1)} %get-tuple-element.277), channel_id=1, source_target_pairs={{0,4},{4,0},{1,5},{5,1},{2,6},{6,2},{3,7},{7,3},{8,12},{12,8},{9,1... | collective-permute-start | bytes 2949128 | tf_op jit(solution)/shard_map/ppermute | solution.py:1133
  180.9 9.1 %collective-permute-start.37 = (bf16[2,96,768]{2,1,0:T(8,128)(2,1)S(1)}, bf16[2,96,768]{2,1,0:T(8,128)(2,1)S(1)}, u32[]{:S(2)}, u32[]{:S(2)}) collective-permute-start(bf16[2,96,768]{2,1,0:T(8,128)(2,1)S(1)} %get-tuple-element.308), channel_id=1, source_target_pairs={{0,4},{4,0},{1,5},{5,1},{2,6},{6,2},{3,7},{7,3},{8,12},{12,8},{9,1... | collective-permute-start | bytes 884744 | tf_op jit(solution)/shard_map/ppermute | solution.py:1144
  181.4 11.4 %collective-permute-start.34 = (bf16[2,1,96,768]{3,2,1,0:T(8,128)(2,1)S(1)}, bf16[2,1,96,768]{3,2,1,0:T(8,128)(2,1)S(1)}, u32[]{:S(2)}, u32[]{:S(2)}) collective-permute-start(bf16[2,1,96,768]{3,2,1,0:T(8,128)(2,1)S(1)} %get-tuple-element.299), channel_id=1, source_target_pairs={{0,8},{8,0},{1,9},{9,1},{2,10},{10,2},{3,11},{11,3},{4,12},{12,4},... | collective-permute-start | bytes 884744 | tf_op jit(solution)/shard_map/ppermute | solution.py:1019
  183.0 15.0 %collective-permute-start.35 = (bf16[2,1,96,768]{3,2,1,0:T(8,128)(2,1)S(1)}, bf16[2,1,96,768]{3,2,1,0:T(8,128)(2,1)S(1)}, u32[]{:S(2)}, u32[]{:S(2)}) collective-permute-start(bf16[2,1,96,768]{3,2,1,0:T(8,128)(2,1)S(1)} %get-tuple-element.300), channel_id=1, source_target_pairs={{0,16},{16,0},{1,17},{17,1},{2,18},{18,2},{3,19},{19,3},{4,20},{20... | collective-permute-start | bytes 884744 | tf_op jit(solution)/shard_map/ppermute | solution.py:1020
  184.4 16.1 %collective-permute-start.36 = (bf16[2,1,96,768]{3,2,1,0:T(8,128)(2,1)S(1)}, bf16[2,1,96,768]{3,2,1,0:T(8,128)(2,1)S(1)}, u32[]{:S(2)}, u32[]{:S(2)}) collective-permute-start(bf16[2,1,96,768]{3,2,1,0:T(8,128)(2,1)S(1)} %get-tuple-element.301), channel_id=1, source_target_pairs={{0,24},{8,16},{16,8},{24,0},{1,25},{9,17},{17,9},{25,1},{2,26},{10... | collective-permute-start | bytes 884744 | tf_op jit(solution)/shard_map/ppermute | solution.py:1021
  190.0 10.5 %collective-permute-start.33 = (f32[16,768]{1,0:T(8,128)S(1)}, f32[16,768]{1,0:T(8,128)S(1)}, u32[]{:S(2)}, u32[]{:S(2)}) collective-permute-start(f32[16,768]{1,0:T(8,128)S(1)} %get-tuple-element.297.refs_4_), channel_id=1, source_target_pairs={{0,4},{4,0},{1,5},{5,1},{2,6},{6,2},{3,7},{7,3},{8,12},{12,8},{9,1... | collective-permute-start | bytes 147464 | tf_op jit(solution)/shard_map/ppermute | solution.py:1158
  190.0 13.6 %collective-permute-start.39 = (bf16[2,1,96,768]{3,2,1,0:T(8,128)(2,1)S(1)}, bf16[2,1,96,768]{3,2,1,0:T(8,128)(2,1)S(1)}, u32[]{:S(2)}, u32[]{:S(2)}) collective-permute-start(bf16[2,1,96,768]{3,2,1,0:T(8,128)(2,1)S(1)} %get-tuple-element.315), channel_id=1, source_target_pairs={{1,0},{2,1},{3,2},{0,3},{6,4},{7,5},{4,6},{5,7},{9,8},{10,9},{11,1... | collective-permute-start | bytes 884744 | tf_op jit(solution)/shard_map/ppermute | solution.py:1143
  192.9 16.5 %collective-permute-start.44 = (bf16[2,96,768]{2,1,0:T(8,128)(2,1)S(1)}, bf16[2,96,768]{2,1,0:T(8,128)(2,1)S(1)}, u32[]{:S(2)}, u32[]{:S(2)}) collective-permute-start(bf16[2,96,768]{2,1,0:T(8,128)(2,1)S(1)} %get-tuple-element.328), channel_id=1, source_target_pairs={{0,8},{8,0},{1,9},{9,1},{2,10},{10,2},{3,11},{11,3},{4,12},{12,4},... | collective-permute-start | bytes 884744 | tf_op jit(solution)/shard_map/ppermute | solution.py:1019
  198.0 13.5 %collective-permute-start.45 = (bf16[2,96,768]{2,1,0:T(8,128)(2,1)S(1)}, bf16[2,96,768]{2,1,0:T(8,128)(2,1)S(1)}, u32[]{:S(2)}, u32[]{:S(2)}) collective-permute-start(bf16[2,96,768]{2,1,0:T(8,128)(2,1)S(1)} %get-tuple-element.329), channel_id=1, source_target_pairs={{0,16},{16,0},{1,17},{17,1},{2,18},{18,2},{3,19},{19,3},{4,20},{20... | collective-permute-start | bytes 884744 | tf_op jit(solution)/shard_map/ppermute | solution.py:1020
  200.5 11.9 %collective-permute-start.46 = (bf16[2,96,768]{2,1,0:T(8,128)(2,1)S(1)}, bf16[2,96,768]{2,1,0:T(8,128)(2,1)S(1)}, u32[]{:S(2)}, u32[]{:S(2)}) collective-permute-start(bf16[2,96,768]{2,1,0:T(8,128)(2,1)S(1)} %get-tuple-element.330), channel_id=1, source_target_pairs={{0,24},{8,16},{16,8},{24,0},{1,25},{9,17},{17,9},{25,1},{2,26},{10... | collective-permute-start | bytes 884744 | tf_op jit(solution)/shard_map/ppermute | solution.py:1021
  201.2 2.4 collective-permute-start.38
  204.2 12.3 %collective-permute-start.40 = (bf16[1,96,768]{2,1,0:T(8,128)(2,1)S(1)}, bf16[1,96,768]{2,1,0:T(8,128)(2,1)S(1)}, u32[]{:S(2)}, u32[]{:S(2)}) collective-permute-start(bf16[1,96,768]{2,1,0:T(8,128)(2,1)S(1)} %get-tuple-element.325), channel_id=1, source_target_pairs={{0,4},{4,0},{1,5},{5,1},{2,6},{6,2},{3,7},{7,3},{8,12},{12,8},{9,1... | collective-permute-start | bytes 442376 | tf_op jit(solution)/shard_map/ppermute | solution.py:1175
  208.9 4.2 %collective-permute-start.41 = (f32[16,768]{1,0:T(8,128)S(1)}, f32[16,768]{1,0:T(8,128)S(1)}, u32[]{:S(2)}, u32[]{:S(2)}) collective-permute-start(f32[16,768]{1,0:T(8,128)S(1)} %get-tuple-element.338.refs_8_), channel_id=1, source_target_pairs={{0,8},{8,0},{1,9},{9,1},{2,10},{10,2},{3,11},{11,3},{4,12},{12,4},... | collective-permute-start | bytes 147464 | tf_op jit(solution)/shard_map/ppermute | solution.py:997
  209.4 4.1 %collective-permute-start.42 = (f32[16,768]{1,0:T(8,128)S(1)}, f32[16,768]{1,0:T(8,128)S(1)}, u32[]{:S(2)}, u32[]{:S(2)}) collective-permute-start(f32[16,768]{1,0:T(8,128)S(1)} %get-tuple-element.338.refs_8_), channel_id=1, source_target_pairs={{0,16},{16,0},{1,17},{17,1},{2,18},{18,2},{3,19},{19,3},{4,20},{20... | collective-permute-start | bytes 147464 | tf_op jit(solution)/shard_map/ppermute | solution.py:998
  211.5 5.0 %collective-permute-start.43 = (f32[16,768]{1,0:T(8,128)S(1)}, f32[16,768]{1,0:T(8,128)S(1)}, u32[]{:S(2)}, u32[]{:S(2)}) collective-permute-start(f32[16,768]{1,0:T(8,128)S(1)} %get-tuple-element.338.refs_8_), channel_id=1, source_target_pairs={{0,24},{8,16},{16,8},{24,0},{1,25},{9,17},{17,9},{25,1},{2,26},{10... | collective-permute-start | bytes 147464 | tf_op jit(solution)/shard_map/ppermute | solution.py:999
  217.3 7.8 %collective-permute-start.50 = (f32[16,768]{1,0:T(8,128)S(1)}, f32[16,768]{1,0:T(8,128)S(1)}, u32[]{:S(2)}, u32[]{:S(2)}) collective-permute-start(f32[16,768]{1,0:T(8,128)S(1)} %get-tuple-element.343), channel_id=1, source_target_pairs={{0,1},{1,2},{2,3},{3,0},{4,5},{5,6},{6,7},{7,4},{8,9},{9,10},{10,1... | collective-permute-start | bytes 147464 | tf_op jit(solution)/shard_map/ppermute | solution.py:1185
  217.7 13.1 %collective-permute-start.47 = (bf16[3,96,768]{2,1,0:T(8,128)(2,1)S(1)}, bf16[3,96,768]{2,1,0:T(8,128)(2,1)S(1)}, u32[]{:S(2)}, u32[]{:S(2)}) collective-permute-start(bf16[3,96,768]{2,1,0:T(8,128)(2,1)S(1)} %get-tuple-element.346.refs_0_), channel_id=1, source_target_pairs={{0,8},{8,0},{1,9},{9,1},{2,10},{10,2},{3,11},{11,3},{4,12},{12,4},... | collective-permute-start | bytes 1327112 | tf_op jit(solution)/shard_map/ppermute | solution.py:997
  218.7 19.2 %collective-permute-start.48 = (bf16[3,96,768]{2,1,0:T(8,128)(2,1)S(1)}, bf16[3,96,768]{2,1,0:T(8,128)(2,1)S(1)}, u32[]{:S(2)}, u32[]{:S(2)}) collective-permute-start(bf16[3,96,768]{2,1,0:T(8,128)(2,1)S(1)} %get-tuple-element.346.refs_0_), channel_id=1, source_target_pairs={{0,16},{16,0},{1,17},{17,1},{2,18},{18,2},{3,19},{19,3},{4,20},{20... | collective-permute-start | bytes 1327112 | tf_op jit(solution)/shard_map/ppermute | solution.py:998
  220.2 17.7 %collective-permute-start.49 = (bf16[3,96,768]{2,1,0:T(8,128)(2,1)S(1)}, bf16[3,96,768]{2,1,0:T(8,128)(2,1)S(1)}, u32[]{:S(2)}, u32[]{:S(2)}) collective-permute-start(bf16[3,96,768]{2,1,0:T(8,128)(2,1)S(1)} %get-tuple-element.346.refs_0_), channel_id=1, source_target_pairs={{0,24},{8,16},{16,8},{24,0},{1,25},{9,17},{17,9},{25,1},{2,26},{10... | collective-permute-start | bytes 1327112 | tf_op jit(solution)/shard_map/ppermute | solution.py:999
  221.7 5.6 %collective-permute-start.51 = (f32[16,768]{1,0:T(8,128)S(1)}, f32[16,768]{1,0:T(8,128)S(1)}, u32[]{:S(2)}, u32[]{:S(2)}) collective-permute-start(f32[16,768]{1,0:T(8,128)S(1)} %get-tuple-element.343), channel_id=1, source_target_pairs={{0,2},{1,3},{2,0},{3,1},{4,6},{5,7},{6,4},{7,5},{8,10},{9,11},{10,... | collective-permute-start | bytes 147464 | tf_op jit(solution)/shard_map/ppermute | solution.py:1185
  225.1 4.1 %collective-permute-start.52 = (f32[16,768]{1,0:T(8,128)S(1)}, f32[16,768]{1,0:T(8,128)S(1)}, u32[]{:S(2)}, u32[]{:S(2)}) collective-permute-start(f32[16,768]{1,0:T(8,128)S(1)} %get-tuple-element.343), channel_id=1, source_target_pairs={{0,3},{1,0},{2,1},{3,2},{4,7},{5,4},{6,5},{7,6},{8,11},{9,8},{10,9... | collective-permute-start | bytes 147464 | tf_op jit(solution)/shard_map/ppermute | solution.py:1185
  237.9 3.5 %collective-permute-start.53 = (bf16[3,96,768]{2,1,0:T(8,128)(2,1)S(1)}, bf16[3,96,768]{2,1,0:T(8,128)(2,1)S(1)}, u32[]{:S(2)}, u32[]{:S(2)}) collective-permute-start(bf16[3,96,768]{2,1,0:T(8,128)(2,1)S(1)} %get-tuple-element.346.refs_0_), channel_id=1, source_target_pairs={{0,4},{4,0},{1,5},{5,1},{2,6},{6,2},{3,7},{7,3},{8,12},{12,8},{9,1... | collective-permute-start | bytes 1327112 | tf_op jit(solution)/shard_map/ppermute | solution.py:1197
  237.9 3.5 %collective-permute-start.54 = (bf16[3,96,768]{2,1,0:T(8,128)(2,1)S(1)}, bf16[3,96,768]{2,1,0:T(8,128)(2,1)S(1)}, u32[]{:S(2)}, u32[]{:S(2)}) collective-permute-start(bf16[3,96,768]{2,1,0:T(8,128)(2,1)S(1)} %collective-permute-done.47.refs_1_), channel_id=1, source_target_pairs={{0,4},{4,0},{1,5},{5,1},{2,6},{6,2},{3,7},{7,3},{8,12},{12,8},{9,1... | collective-permute-start | bytes 1327112 | tf_op jit(solution)/shard_map/ppermute | solution.py:1197
  238.4 3.0 %collective-permute-start.55 = (bf16[3,96,768]{2,1,0:T(8,128)(2,1)S(1)}, bf16[3,96,768]{2,1,0:T(8,128)(2,1)S(1)}, u32[]{:S(2)}, u32[]{:S(2)}) collective-permute-start(bf16[3,96,768]{2,1,0:T(8,128)(2,1)S(1)} %collective-permute-done.48.refs_2_), channel_id=1, source_target_pairs={{0,4},{4,0},{1,5},{5,1},{2,6},{6,2},{3,7},{7,3},{8,12},{12,8},{9,1... | collective-permute-start | bytes 1327112 | tf_op jit(solution)/shard_map/ppermute | solution.py:1197
  238.4 3.2 %collective-permute-start.56 = (bf16[3,96,768]{2,1,0:T(8,128)(2,1)S(1)}, bf16[3,96,768]{2,1,0:T(8,128)(2,1)S(1)}, u32[]{:S(2)}, u32[]{:S(2)}) collective-permute-start(bf16[3,96,768]{2,1,0:T(8,128)(2,1)S(1)} %collective-permute-done.49.refs_3_), channel_id=1, source_target_pairs={{0,4},{4,0},{1,5},{5,1},{2,6},{6,2},{3,7},{7,3},{8,12},{12,8},{9,1... | collective-permute-start | bytes 1327112 | tf_op jit(solution)/shard_map/ppermute | solution.py:1197
  (21 other events, 154.5 us)

commit v2 on v1

--- a/solution.py
+++ b/solution.py
@@ -107,7 +107,7 @@
         out_specs=VMEM,
         compiler_params=params(16),
         cost_estimate=cost(rows * width * 10, rows * width * 4),
-    )(place, counts, tokens, gain, shift)
+    )(place, counts, *from_hbm(tokens, gain, shift))
 
 
 def norm_two_kernel(tokens, mine, received, bias, gain, shift, first_sum, normed):
@@ -287,7 +287,7 @@
         scratch_shapes=[pltpu.SemaphoreType.DMA(()), pltpu.SemaphoreType.DMA(())],
         compiler_params=params(16),
         cost_estimate=cost(0, 2 * size * width),
-    )(place, *from_hbm(projection, mixer), bias, up_bias)
+    )(place, *from_hbm(projection, mixer, bias, up_bias))
 
 
 def pack_hidden_kernel(place, up, down, out, sems):

time: 245 us -> 244 us (level)
    unnamed x56 -> x48, local copies, waits for them, and re-layouts: 4.28 us -> 1.7 us
  transfers between devices with their start and end apart: 57 -> 57, of which waited for: 22 -> 21; matrix products, arithmetic and copies ran while one was open for 1% -> 2% of each run, Pallas kernels for 40% -> 40%
where the time goes in v2:
time: 244 us; the launch traced here: 243 us
  Pallas kernels  104 us (43%)
  starting transfers between devices  79.2 us (32%)
  waiting for transfers between devices  52.4 us (21%)
  local copies, waits for them, and re-layouts  3.68 us (2%)
    pallas_call x2, Pallas kernels, hidden_block(): pl.pallas_call(functools.partial(hidden_kernel, last), out_shape=(*grad_s...  30.3 us
    pallas_call x2, Pallas kernels, attention_back(): pl.pallas_call(functools.partial(attention_back_kernel, heads, far), grid...  24.6 us
    pallas_call x2, Pallas kernels, attention(): pl.pallas_call(functools.partial(attention_kernel, heads), grid=(tiles,),...  20.4 us
    ppermute x3, waiting for transfers between devices, spread(): lax.ppermute(piece, 'a', swap)  12.7 us
    ppermute x1, starting transfers between devices, local(): grad_other = lax.ppermute(after(output_grad, part), 'c', swap)  11.3 us
    ppermute x1, waiting for transfers between devices, local(): depth_near_one = lax.ppermute(piece_one, ('c', 't'), to_near)  8.55 us
    ppermute x1, starting transfers between devices, local(): received_far = lax.ppermute(send_far, 'c', swap)  5.93 us
    ppermute x3, starting transfers between devices, direct(): lax.ppermute(send_y, 'a', swap)  5.29 us
  transfers between devices with their start and end apart: 57, of which 21 were waited for; matrix products, arithmetic and copies ran while one was open for 2% of the time, Pallas kernels for 40%

profile of v2, /device:TPU:0, one launch (start us, length us, event | category | flops | bytes accessed | tf_op | source)
XLA Modules:
  0.0 243.1 jit_solution(7719020920689977360)
XLA Ops:
  1.4 2.9 %shard_map.254.normed.counts.rest_4_ = bf16[656,768]{1,0:T(8,128)(2,1)S(1)} custom-call(s32[3]{0:T(128)S(1)} %pad_add_fusion.place, s32[32]{0:T(128)S(1)} %copy-done.7, bf16[640,768]{1,0:T(8,128)(2,1)} %tokens.5, f32[768]{0:T(1024)} %gain.1, f32[768]{0:T(1024)} %shift.1), custom_call_target="tpu_custom_call" | custom-call | flops 4915200 | bytes 1966080 | tf_op jit(solution)/shard_map/pallas_call | solution.py:103
  5.4 1.9 shard_map.255
  7.4 2.6 %collective-permute-start = (bf16[208,768]{1,0:T(8,128)(2,1)S(1)}, bf16[208,768]{1,0:T(8,128)(2,1)S(1)}, u32[]{:S(2)}, u32[]{:S(2)}) collective-permute-start(bf16[208,768]{1,0:T(8,128)(2,1)S(1)} %get-tuple-element.194), channel_id=1, source_target_pairs={{0,1},{1,2},{2,3},{3,0},{4,6},{5,7},{6,4},{7,5},{8,9},{9,10},{10,1... | collective-permute-start | bytes 958472 | tf_op jit(solution)/shard_map/ppermute | solution.py:1038
  10.0 1.6 shard_map.256
  11.8 8.6 %collective-permute-done.near0.rest_5_.rest_0_ = bf16[208,768]{1,0:T(8,128)(2,1)S(1)} collective-permute-done((bf16[208,768]{1,0:T(8,128)(2,1)S(1)}, bf16[208,768]{1,0:T(8,128)(2,1)S(1)}, u32[]{:S(2)}, u32[]{:S(2)}) %collective-permute-start) | collective-permute-done | bytes 319520 | tf_op jit(solution)/shard_map/ppermute | solution.py:1038
  21.1 0.8 collective-permute-start.6
  21.9 1.6 collective-permute-start.2
  23.5 1.5 collective-permute-start.3
  25.5 3.5 %collective-permute-done.2.near1.rest_1_ = bf16[208,768]{1,0:T(8,128)(2,1)S(1)} collective-permute-done((bf16[208,768]{1,0:T(8,128)(2,1)S(1)}, bf16[208,768]{1,0:T(8,128)(2,1)S(1)}, u32[]{:S(2)}, u32[]{:S(2)}) %collective-permute-start.2) | collective-permute-done | bytes 319520 | tf_op jit(solution)/shard_map/ppermute | solution.py:997
  29.0 5.2 %collective-permute-done.3.near2.rest_2_ = bf16[208,768]{1,0:T(8,128)(2,1)S(1)} collective-permute-done((bf16[208,768]{1,0:T(8,128)(2,1)S(1)}, bf16[208,768]{1,0:T(8,128)(2,1)S(1)}, u32[]{:S(2)}, u32[]{:S(2)}) %collective-permute-start.3) | collective-permute-done | bytes 319520 | tf_op jit(solution)/shard_map/ppermute | solution.py:998
  34.2 2.1 collective-permute-start.7
  36.3 10.2 %shard_map.257 = (bf16[8,1280,192]{2,1,0:T(8,128)(2,1)}, bf16[1280,768]{1,0:T(8,128)(2,1)}, bf16[640,768]{1,0:T(8,128)(2,1)S(1)}) custom-call(s32[3]{0:T(128)S(1)} %pad_add_fusion.place, bf16[576,768]{1,0:T(8,128)(2,1)S(1)} %bitcast.11, bf16[208,768]{1,0:T(8,128)(2,1)S(1)} %get-tuple-element.199.tail.rest_1_, ...), custom_call_target="tpu_custom_call" | custom-call | flops 1765949440 | bytes 9915200 | tf_op jit(solution)/shard_map/pallas_call | solution.py:488
  46.5 2.3 collective-permute-done.7.rest_0_
  48.8 11.3 %collective-permute-start.11 = (bf16[640,768]{1,0:T(8,128)(2,1)S(1)}, bf16[640,768]{1,0:T(8,128)(2,1)S(1)}, u32[]{:S(2)}, u32[]{:S(2)}) collective-permute-start(bf16[640,768]{1,0:T(8,128)(2,1)S(1)} %copy-done.12), channel_id=1, source_target_pairs={{0,4},{4,0},{1,5},{5,1},{2,6},{6,2},{3,7},{7,3},{8,12},{12,8},{9,1... | collective-permute-start | bytes 2949128 | tf_op jit(solution)/shard_map/ppermute | solution.py:1054
  60.2 1.5 collective-permute-start.10
  61.7 2.0 collective-permute-start.9
  63.7 1.0 collective-permute-start.15
  64.7 10.2 %shard_map.258 = (bf16[8,1280,192]{2,1,0:T(8,128)(2,1)}, bf16[1280,768]{1,0:T(8,128)(2,1)}, f32[640,768]{1,0:T(8,128)S(1)}) custom-call(s32[3]{0:T(128)S(1)} %pad_add_fusion.place, bf16[576,768]{1,0:T(8,128)(2,1)S(1)} %bitcast.12, bf16[208,768]{1,0:T(8,128)(2,1)S(1)} %get-tuple-element.199.tail.rest_1_, ...), custom_call_target="tpu_custom_call", output_to_operand_aliasing={{0}: (11, {}), {1}: (12, {})} | custom-call | flops 1765949440 | bytes 9915200 | tf_op jit(solution)/shard_map/pallas_call | solution.py:488
  74.9 0.9 collective-permute-done.10.rest_2_
  75.9 1.5 collective-permute-done.9.rest_1_
  77.4 1.8 collective-permute-start.12
  79.6 3.7 %shard_map.259 = (f32[640,768]{1,0:T(8,128)}, bf16[640,768]{1,0:T(8,128)(2,1)S(1)}) custom-call(bf16[640,768]{1,0:T(8,128)(2,1)} %tokens.5, f32[640,768]{1,0:T(8,128)S(1)} %get-tuple-element.213.mine, bf16[640,768]{1,0:T(8,128)(2,1)S(1)} %collective-permute-done.8.received, f32[1,768]{1,0:T(1,128)S(1)} %reshape.55.bias, f32[1,768]{1,0:T(1,128)S(1)} %reshape.56.gain, ...), custom_call_target="tpu_custom_call" | custom-call | flops 5898240 | bytes 6881280 | tf_op jit(solution)/shard_map/pallas_call | solution.py:133
  83.3 2.2 collective-permute-done.12.rest_3_
  85.5 2.9 %collective-permute-done.13.rest_4_ = bf16[192,768]{1,0:T(8,128)(2,1)S(1)} collective-permute-done((bf16[192,768]{1,0:T(8,128)(2,1)S(1)}, bf16[192,768]{1,0:T(8,128)(2,1)S(1)}, u32[]{:S(2)}, u32[]{:S(2)}) %collective-permute-start.13) | collective-permute-done | bytes 294944 | tf_op jit(solution)/shard_map/ppermute | solution.py:1067
  89.0 2.2 collective-permute-done.14.rest_7_.rest_5_
  91.2 0.9 copy-done.23
  92.2 15.1 %shard_map.260 = (bf16[2,2,96,768]{3,2,1,0:T(8,128)(2,1)}, bf16[2,2,96,768]{3,2,1,0:T(8,128)(2,1)}, bf16[2,2,96,768]{3,2,1,0:T(8,128)(2,1)}, bf16[2,2,96,768]{3,...) custom-call(s32[3]{0:T(128)S(1)} %pad_add_fusion.place, ...), custom_call_target="tpu_custom_call" | custom-call | flops 9059696640 | bytes 19796480 | tf_op jit(solution)/shard_map/pallas_call | solution.py:762
  108.4 15.2 %shard_map.261 = (bf16[2,4,2,96,768]{4,3,2,1,0:T(8,128)(2,1)}, f32[8,768]{1,0:T(8,128)S(1)}, bf16[640,768]{1,0:T(8,128)(2,1)}, bf16[640,768]{1,0:T(8,128)(2,1)},...) custom-call(s32[3]{0:T(128)S(1)} %pad_add_fusion.place, bf16[1536,768]{1,0:T(8,128)(2,1)S(1)} %pad_maximum_fusion.rest_0_, ...), custom_call_target="tpu_custom_call" | custom-call | flops 9059696640 | bytes 19796480 | tf_op jit(solution)/shard_map/pallas_call | solution.py:762
  123.8 0.9 collective-permute-start.24
  125.6 1.0 collective-permute-done.20.part3
  126.5 4.2 %shard_map.263 = (bf16[640,768]{1,0:T(8,128)(2,1)S(1)}, f32[8,768]{1,0:T(8,128)S(1)}) custom-call(bf16[640,768]{1,0:T(8,128)(2,1)S(1)} %copy-done.3, bf16[640,768]{1,0:T(8,128)(2,1)S(1)} %collective-permute-done.18.part1, bf16[640,768]{1,0:T(8,128)(2,1)S(1)} %copy-done.4, bf16[640,768]{1,0:T(8,128)(2,1)S(1)} %collective-permute-done.20.part3, ...), custom_call_target="tpu_custom_call" | custom-call | flops 12288000 | bytes 8847360 | tf_op jit(solution)/shard_map/pallas_call | solution.py:174
  130.7 2.1 collective-permute-start.21
  132.9 2.2 collective-permute-done.21.rest_7_
  135.4 1.5 collective-permute-start.22
  137.0 1.4 collective-permute-start.23
  138.4 12.4 %shard_map.264 = (bf16[2,1,96,768]{3,2,1,0:T(8,128)(2,1)S(1)}, bf16[2,1,96,768]{3,2,1,0:T(8,128)(2,1)S(1)}, bf16[2,1,96,768]{3,2,1,0:T(8,128)(2,1)S(1)}, bf16[2,...) custom-call(s32[3]{0:T(128)S(1)} %pad_add_fusion.place, ...), custom_call_target="tpu_custom_call" | custom-call | flops 3215155200 | bytes 13830400 | tf_op jit(solution)/shard_map/pallas_call | solution.py:619
  151.6 5.9 %collective-permute-start.26 = (bf16[4,2,96,768]{3,2,1,0:T(8,128)(2,1)S(1)}, bf16[4,2,96,768]{3,2,1,0:T(8,128)(2,1)S(1)}, u32[]{:S(2)}, u32[]{:S(2)}) collective-permute-start(bf16[4,2,96,768]{3,2,1,0:T(8,128)(2,1)S(1)} %get-tuple-element.276), channel_id=1, source_target_pairs={{0,4},{4,0},{1,5},{5,1},{2,6},{6,2},{3,7},{7,3},{8,12},{12,8},{9,1... | collective-permute-start | bytes 3538952 | tf_op jit(solution)/shard_map/ppermute | solution.py:1124
  157.6 1.7 collective-permute-start.31
  159.3 1.6 collective-permute-start.28
  160.9 1.4 collective-permute-start.29
  162.8 12.2 %shard_map.266 = (bf16[2,1,96,768]{3,2,1,0:T(8,128)(2,1)S(1)}, bf16[2,1,96,768]{3,2,1,0:T(8,128)(2,1)S(1)}, bf16[2,1,96,768]{3,2,1,0:T(8,128)(2,1)S(1)}, bf16[2,...) custom-call(s32[3]{0:T(128)S(1)} %pad_add_fusion.place, ...), custom_call_target="tpu_custom_call" | custom-call | flops 3215155200 | bytes 13830400 | tf_op jit(solution)/shard_map/pallas_call | solution.py:619
  175.1 3.5 %collective-permute-start.32 = (bf16[640,768]{1,0:T(8,128)(2,1)S(1)}, bf16[640,768]{1,0:T(8,128)(2,1)S(1)}, u32[]{:S(2)}, u32[]{:S(2)}) collective-permute-start(bf16[640,768]{1,0:T(8,128)(2,1)S(1)} %get-tuple-element.291), channel_id=1, source_target_pairs={{0,4},{4,0},{1,5},{5,1},{2,6},{6,2},{3,7},{7,3},{8,12},{12,8},{9,1... | collective-permute-start | bytes 2949128 | tf_op jit(solution)/shard_map/ppermute | solution.py:1136
  178.6 1.1 shard_map.268
  180.2 1.6 collective-permute-start.34
  181.8 1.4 collective-permute-start.35
  183.8 5.0 %shard_map.267 = (f32[640,768]{1,0:T(8,128)}, f32[16,768]{1,0:T(8,128)S(1)}) custom-call(s32[3]{0:T(128)S(1)} %pad_add_fusion.place, bf16[640,768]{1,0:T(8,128)(2,1)S(1)} %get-tuple-element.270.part0, bf16[640,768]{1,0:T(8,128)(2,1)S(1)} %collective-permute-done.27.part1, bf16[640,768]{1,0:T(8,128)(2,1)S(1)} %get-tuple-element.290.part2, ...), custom_call_target="tpu_custom_call" | custom-call | flops 12288000 | bytes 7864320 | tf_op jit(solution)/shard_map/pallas_call | solution.py:233
  188.8 2.8 %collective-permute-start.39 = (bf16[2,1,96,768]{3,2,1,0:T(8,128)(2,1)S(1)}, bf16[2,1,96,768]{3,2,1,0:T(8,128)(2,1)S(1)}, u32[]{:S(2)}, u32[]{:S(2)}) collective-permute-start(bf16[2,1,96,768]{3,2,1,0:T(8,128)(2,1)S(1)} %get-tuple-element.315), channel_id=1, source_target_pairs={{1,0},{2,1},{3,2},{0,3},{6,4},{7,5},{4,6},{5,7},{9,8},{10,9},{11,1... | collective-permute-start | bytes 884744 | tf_op jit(solution)/shard_map/ppermute | solution.py:1143
  191.7 1.6 collective-permute-start.44
  193.2 3.6 %collective-permute-done.35.refs_2_ = bf16[2,1,96,768]{3,2,1,0:T(8,128)(2,1)S(1)} collective-permute-done((bf16[2,1,96,768]{3,2,1,0:T(8,128)(2,1)S(1)}, bf16[2,1,96,768]{3,2,1,0:T(8,128)(2,1)S(1)}, u32[]{:S(2)}, u32[]{:S(2)}) %collective-permute-start.35) | collective-permute-done | bytes 294944 | tf_op jit(solution)/shard_map/ppermute | solution.py:1020
  196.8 2.5 %collective-permute-start.45 = (bf16[2,96,768]{2,1,0:T(8,128)(2,1)S(1)}, bf16[2,96,768]{2,1,0:T(8,128)(2,1)S(1)}, u32[]{:S(2)}, u32[]{:S(2)}) collective-permute-start(bf16[2,96,768]{2,1,0:T(8,128)(2,1)S(1)} %get-tuple-element.329), channel_id=1, source_target_pairs={{0,16},{16,0},{1,17},{17,1},{2,18},{18,2},{3,19},{19,3},{4,20},{20... | collective-permute-start | bytes 884744 | tf_op jit(solution)/shard_map/ppermute | solution.py:1020
  200.7 1.6 add_convert_fusion
  203.0 4.7 %collective-permute-start.40 = (bf16[1,96,768]{2,1,0:T(8,128)(2,1)S(1)}, bf16[1,96,768]{2,1,0:T(8,128)(2,1)S(1)}, u32[]{:S(2)}, u32[]{:S(2)}) collective-permute-start(bf16[1,96,768]{2,1,0:T(8,128)(2,1)S(1)} %get-tuple-element.325), channel_id=1, source_target_pairs={{0,4},{4,0},{1,5},{5,1},{2,6},{6,2},{3,7},{7,3},{8,12},{12,8},{9,1... | collective-permute-start | bytes 442376 | tf_op jit(solution)/shard_map/ppermute | solution.py:1175
  208.2 1.5 collective-permute-start.42
  210.3 0.9 collective-permute-start.43
  212.3 3.0 %collective-permute-done.43.refs_11_ = f32[16,768]{1,0:T(8,128)S(1)} collective-permute-done((f32[16,768]{1,0:T(8,128)S(1)}, f32[16,768]{1,0:T(8,128)S(1)}, u32[]{:S(2)}, u32[]{:S(2)}) %collective-permute-start.43) | collective-permute-done | bytes 49184 | tf_op jit(solution)/shard_map/ppermute | solution.py:999
  216.5 1.0 collective-permute-start.47
  217.5 1.5 collective-permute-start.48
  219.0 1.5 collective-permute-start.49
  220.4 3.4 %collective-permute-start.51 = (f32[16,768]{1,0:T(8,128)S(1)}, f32[16,768]{1,0:T(8,128)S(1)}, u32[]{:S(2)}, u32[]{:S(2)}) collective-permute-start(f32[16,768]{1,0:T(8,128)S(1)} %get-tuple-element.343), channel_id=1, source_target_pairs={{0,2},{1,3},{2,0},{3,1},{4,6},{5,7},{6,4},{7,5},{8,10},{9,11},{10,... | collective-permute-start | bytes 147464 | tf_op jit(solution)/shard_map/ppermute | solution.py:1185
  223.9 2.2 collective-permute-done.51
  226.1 1.9 collective-permute-done.52
  229.6 7.1 %collective-permute-done.48.refs_2_ = bf16[3,96,768]{2,1,0:T(8,128)(2,1)S(1)} collective-permute-done((bf16[3,96,768]{2,1,0:T(8,128)(2,1)S(1)}, bf16[3,96,768]{2,1,0:T(8,128)(2,1)S(1)}, u32[]{:S(2)}, u32[]{:S(2)}) %collective-permute-start.48) | collective-permute-done | bytes 442400 | tf_op jit(solution)/shard_map/ppermute | solution.py:998
  237.7 2.5 %shard_map.272 = (f32[576,768]{1,0:T(8,128)}, f32[192,768]{1,0:T(8,128)}, f32[768,768]{1,0:T(8,128)}, f32[768,768]{1,0:T(8,128)}) custom-call(s32[3]{0:T(128)S(1)} %pad_add_fusion.place, bf16[3,96,768]{2,1,0:T(8,128)(2,1)S(1)} %get-tuple-element.346.refs_0_, bf16[3,96,768]{2,1,0:T(8,128)(2,1)S(1)} %collective-permute-done.47.refs_1_, ...), custom_call_target="tpu_custom_call" | custom-call | bytes 5308416 | tf_op jit(solution)/shard_map/pallas_call | solution.py:943
  240.4 2.5 %shard_map.273 = (f32[576,768]{1,0:T(8,128)}, f32[192,768]{1,0:T(8,128)}, f32[768,768]{1,0:T(8,128)}, f32[768,768]{1,0:T(8,128)}) custom-call(s32[3]{0:T(128)S(1)} %pad_add_fusion.place, bf16[3,96,768]{2,1,0:T(8,128)(2,1)S(1)} %collective-permute-done.53.refs_0_, ...), custom_call_target="tpu_custom_call", output_to_operand_aliasing={{0}: (5, {}), {1}: (6, {}), {2}: (7, {}), {3}: (8, {})} | custom-call | bytes 5308416 | tf_op jit(solution)/shard_map/pallas_call | solution.py:943
  (132 shorter events, 17.5 us)
Async XLA Ops:
  4.3 16.1 %collective-permute-start.1 = (bf16[656,768]{1,0:T(8,128)(2,1)S(1)}, bf16[656,768]{1,0:T(8,128)(2,1)S(1)}, u32[]{:S(2)}, u32[]{:S(2)}) collective-permute-start(bf16[656,768]{1,0:T(8,128)(2,1)S(1)} %shard_map.254.normed.counts.rest_4_), channel_id=1, source_target_pairs={{0,4},{4,0},{1,5},{5,1},{2,6},{6,2},{3,7},{7,3},{8,12},{12,8},{9,1... | collective-permute-start | bytes 3022856 | tf_op jit(solution)/shard_map/ppermute | solution.py:1039
  7.4 13.0 %collective-permute-start = (bf16[208,768]{1,0:T(8,128)(2,1)S(1)}, bf16[208,768]{1,0:T(8,128)(2,1)S(1)}, u32[]{:S(2)}, u32[]{:S(2)}) collective-permute-start(bf16[208,768]{1,0:T(8,128)(2,1)S(1)} %get-tuple-element.194), channel_id=1, source_target_pairs={{0,1},{1,2},{2,3},{3,0},{4,6},{5,7},{6,4},{7,5},{8,9},{9,10},{10,1... | collective-permute-start | bytes 958472 | tf_op jit(solution)/shard_map/ppermute | solution.py:1038
  20.4 16.0 %collective-permute-start.5 = (bf16[576,768]{1,0:T(8,128)(2,1)S(1)}, bf16[576,768]{1,0:T(8,128)(2,1)S(1)}, u32[]{:S(2)}, u32[]{:S(2)}) collective-permute-start(bf16[576,768]{1,0:T(8,128)(2,1)S(1)} %bitcast.10), channel_id=1, source_target_pairs={{4,7},{5,4},{6,5},{7,6},{12,15},{13,12},{14,13},{15,14},{20,23},{2... | collective-permute-start | bytes 2654216 | tf_op jit(solution)/shard_map/ppermute | solution.py:1046
  21.1 27.7 %copy-start.12 = (bf16[640,768]{1,0:T(8,128)(2,1)S(1)}, bf16[640,768]{1,0:T(8,128)(2,1)}, u32[]{:S(2)}) copy-start(bf16[640,768]{1,0:T(8,128)(2,1)} %output_grad.1) | copy-start | bytes 2949124
  21.1 4.4 %collective-permute-start.6 = (bf16[208,768]{1,0:T(8,128)(2,1)S(1)}, bf16[208,768]{1,0:T(8,128)(2,1)S(1)}, u32[]{:S(2)}, u32[]{:S(2)}) collective-permute-start(bf16[208,768]{1,0:T(8,128)(2,1)S(1)} %get-tuple-element.199.tail.rest_1_), channel_id=1, source_target_pairs={{4,7},{5,4},{6,5},{7,6},{12,15},{13,12},{14,13},{15,14},{20,23},{2... | collective-permute-start | bytes 958472 | tf_op jit(solution)/shard_map/ppermute | solution.py:1047
  21.9 7.1 %collective-permute-start.2 = (bf16[208,768]{1,0:T(8,128)(2,1)S(1)}, bf16[208,768]{1,0:T(8,128)(2,1)S(1)}, u32[]{:S(2)}, u32[]{:S(2)}) collective-permute-start(bf16[208,768]{1,0:T(8,128)(2,1)S(1)} %collective-permute-done.near0.rest_5_.rest_0_), channel_id=1, source_target_pairs={{0,8},{8,0},{1,9},{9,1},{2,10},{10,2},{3,11},{11,3},{4,12},{12,4},... | collective-permute-start | bytes 958472 | tf_op jit(solution)/shard_map/ppermute | solution.py:997
  23.5 10.7 %collective-permute-start.3 = (bf16[208,768]{1,0:T(8,128)(2,1)S(1)}, bf16[208,768]{1,0:T(8,128)(2,1)S(1)}, u32[]{:S(2)}, u32[]{:S(2)}) collective-permute-start(bf16[208,768]{1,0:T(8,128)(2,1)S(1)} %collective-permute-done.near0.rest_5_.rest_0_), channel_id=1, source_target_pairs={{0,16},{16,0},{1,17},{17,1},{2,18},{18,2},{3,19},{19,3},{4,20},{20... | collective-permute-start | bytes 958472 | tf_op jit(solution)/shard_map/ppermute | solution.py:998
  25.0 9.2 %collective-permute-start.4 = (bf16[208,768]{1,0:T(8,128)(2,1)S(1)}, bf16[208,768]{1,0:T(8,128)(2,1)S(1)}, u32[]{:S(2)}, u32[]{:S(2)}) collective-permute-start(bf16[208,768]{1,0:T(8,128)(2,1)S(1)} %collective-permute-done.near0.rest_5_.rest_0_), channel_id=1, source_target_pairs={{0,24},{8,16},{16,8},{24,0},{1,25},{9,17},{17,9},{25,1},{2,26},{10... | collective-permute-start | bytes 958472 | tf_op jit(solution)/shard_map/ppermute | solution.py:999
  34.2 14.6 %collective-permute-start.7 = (bf16[384,768]{1,0:T(8,128)(2,1)S(1)}, bf16[384,768]{1,0:T(8,128)(2,1)S(1)}, u32[]{:S(2)}, u32[]{:S(2)}) collective-permute-start(bf16[384,768]{1,0:T(8,128)(2,1)S(1)} %shard_map.256), channel_id=1, source_target_pairs={{0,1},{1,2},{2,3},{3,0},{4,6},{5,7},{6,4},{7,5},{8,9},{9,10},{10,1... | collective-permute-start | bytes 1769480 | tf_op jit(solution)/shard_map/ppermute | solution.py:1048
  48.8 30.8 %copy-start.17 = (f32[768]{0:T(1024)S(1)}, f32[768]{0:T(1024)}, u32[]{:S(2)}) copy-start(f32[768]{0:T(1024)} %param.23) | copy-start | bytes 9220
  48.8 30.8 %copy-start.18 = (f32[768]{0:T(1024)S(1)}, f32[768]{0:T(1024)}, u32[]{:S(2)}) copy-start(f32[768]{0:T(1024)} %param.22) | copy-start | bytes 9220
  48.8 30.8 %copy-start.19 = (f32[768]{0:T(1024)S(1)}, f32[768]{0:T(1024)}, u32[]{:S(2)}) copy-start(f32[768]{0:T(1024)} %param.24) | copy-start | bytes 9220
  48.8 28.5 %collective-permute-start.11 = (bf16[640,768]{1,0:T(8,128)(2,1)S(1)}, bf16[640,768]{1,0:T(8,128)(2,1)S(1)}, u32[]{:S(2)}, u32[]{:S(2)}) collective-permute-start(bf16[640,768]{1,0:T(8,128)(2,1)S(1)} %copy-done.12), channel_id=1, source_target_pairs={{0,4},{4,0},{1,5},{5,1},{2,6},{6,2},{3,7},{7,3},{8,12},{12,8},{9,1... | collective-permute-start | bytes 2949128 | tf_op jit(solution)/shard_map/ppermute | solution.py:1054
  60.1 17.3 %collective-permute-start.8 = (bf16[640,768]{1,0:T(8,128)(2,1)S(1)}, bf16[640,768]{1,0:T(8,128)(2,1)S(1)}, u32[]{:S(2)}, u32[]{:S(2)}) collective-permute-start(bf16[640,768]{1,0:T(8,128)(2,1)S(1)} %get-tuple-element.209), channel_id=1, source_target_pairs={{0,4},{4,0},{1,5},{5,1},{2,6},{6,2},{3,7},{7,3},{8,12},{12,8},{9,1... | collective-permute-start | bytes 2949128 | tf_op jit(solution)/shard_map/ppermute | solution.py:1055
  60.2 15.7 %collective-permute-start.10 = (bf16[384,768]{1,0:T(8,128)(2,1)S(1)}, bf16[384,768]{1,0:T(8,128)(2,1)S(1)}, u32[]{:S(2)}, u32[]{:S(2)}) collective-permute-start(bf16[384,768]{1,0:T(8,128)(2,1)S(1)} %collective-permute-done.7.rest_0_), channel_id=1, source_target_pairs={{0,16},{16,0},{1,17},{17,1},{2,18},{18,2},{3,19},{19,3},{4,20},{20... | collective-permute-start | bytes 1769480 | tf_op jit(solution)/shard_map/ppermute | solution.py:1057
  61.7 15.7 %collective-permute-start.9 = (bf16[384,768]{1,0:T(8,128)(2,1)S(1)}, bf16[384,768]{1,0:T(8,128)(2,1)S(1)}, u32[]{:S(2)}, u32[]{:S(2)}) collective-permute-start(bf16[384,768]{1,0:T(8,128)(2,1)S(1)} %collective-permute-done.7.rest_0_), channel_id=1, source_target_pairs={{0,8},{8,0},{1,9},{9,1},{2,10},{10,2},{3,11},{11,3},{4,12},{12,4},... | collective-permute-start | bytes 1769480 | tf_op jit(solution)/shard_map/ppermute | solution.py:1056
  63.7 43.5 %collective-permute-start.15 = (bf16[1536,768]{1,0:T(8,128)(2,1)S(1)}, bf16[1536,768]{1,0:T(8,128)(2,1)S(1)}, u32[]{:S(2)}, u32[]{:S(2)}) collective-permute-start(bf16[1536,768]{1,0:T(8,128)(2,1)S(1)} %pad_maximum_fusion.rest_0_), channel_id=1, source_target_pairs={{4,7},{5,4},{6,5},{7,6},{12,15},{13,12},{14,13},{15,14},{20,23},{2... | collective-permute-start | bytes 7077896 | tf_op jit(solution)/shard_map/ppermute | solution.py:1058
  77.4 8.1 %collective-permute-start.12 = (bf16[192,768]{1,0:T(8,128)(2,1)S(1)}, bf16[192,768]{1,0:T(8,128)(2,1)S(1)}, u32[]{:S(2)}, u32[]{:S(2)}) collective-permute-start(bf16[192,768]{1,0:T(8,128)(2,1)S(1)} %slice.30), channel_id=1, source_target_pairs={{0,8},{8,0},{1,9},{9,1},{2,10},{10,2},{3,11},{11,3},{4,12},{12,4},... | collective-permute-start | bytes 884744 | tf_op jit(solution)/shard_map/ppermute | solution.py:1066
  79.2 9.2 %collective-permute-start.13 = (bf16[192,768]{1,0:T(8,128)(2,1)S(1)}, bf16[192,768]{1,0:T(8,128)(2,1)S(1)}, u32[]{:S(2)}, u32[]{:S(2)}) collective-permute-start(bf16[192,768]{1,0:T(8,128)(2,1)S(1)} %slice.31), channel_id=1, source_target_pairs={{0,16},{16,0},{1,17},{17,1},{2,18},{18,2},{3,19},{19,3},{4,20},{20... | collective-permute-start | bytes 884744 | tf_op jit(solution)/shard_map/ppermute | solution.py:1067
  88.4 2.8 %collective-permute-start.14 = (bf16[640,768]{1,0:T(8,128)(2,1)S(1)}, bf16[640,768]{1,0:T(8,128)(2,1)S(1)}, u32[]{:S(2)}, u32[]{:S(2)}) collective-permute-start(bf16[640,768]{1,0:T(8,128)(2,1)S(1)} %get-tuple-element.219.rest_6_.rest_4_), channel_id=1, source_target_pairs={{0,4},{4,0},{1,5},{5,1},{2,6},{6,2},{3,7},{7,3},{8,12},{12,8},{9,1... | collective-permute-start | bytes 2949128 | tf_op jit(solution)/shard_map/ppermute | solution.py:1079
  107.2 17.5 %copy-start.5 = (bf16[2,2,96,768]{3,2,1,0:T(8,128)(2,1)S(1)}, bf16[2,2,96,768]{3,2,1,0:T(8,128)(2,1)}, u32[]{:S(2)}) copy-start(bf16[2,2,96,768]{3,2,1,0:T(8,128)(2,1)} %get-tuple-element.249.refs_0_) | copy-start | bytes 1769476
  107.3 17.5 %copy-start.6 = (bf16[2,2,96,768]{3,2,1,0:T(8,128)(2,1)S(1)}, bf16[2,2,96,768]{3,2,1,0:T(8,128)(2,1)}, u32[]{:S(2)}) copy-start(bf16[2,2,96,768]{3,2,1,0:T(8,128)(2,1)} %get-tuple-element.250.refs_1_) | copy-start | bytes 1769476
  107.3 16.4 %collective-permute-start.18 = (bf16[640,768]{1,0:T(8,128)(2,1)}, bf16[640,768]{1,0:T(8,128)(2,1)S(1)}, u32[]{:S(2)}, u32[]{:S(2)}) collective-permute-start(bf16[640,768]{1,0:T(8,128)(2,1)} %get-tuple-element.244), channel_id=1, source_target_pairs={{0,4},{4,0},{1,5},{5,1},{2,6},{6,2},{3,7},{7,3},{8,12},{12,8},{9,1... | collective-permute-start | bytes 2949128 | tf_op jit(solution)/shard_map/ppermute | solution.py:1088
  107.7 16.0 %collective-permute-start.19 = (bf16[640,768]{1,0:T(8,128)(2,1)}, bf16[640,768]{1,0:T(8,128)(2,1)S(1)}, u32[]{:S(2)}, u32[]{:S(2)}) collective-permute-start(bf16[640,768]{1,0:T(8,128)(2,1)} %get-tuple-element.245), channel_id=1, source_target_pairs={{0,4},{4,0},{1,5},{5,1},{2,6},{6,2},{3,7},{7,3},{8,12},{12,8},{9,1... | collective-permute-start | bytes 2949128 | tf_op jit(solution)/shard_map/ppermute | solution.py:1089
  107.8 15.8 %collective-permute-start.16 = (bf16[2,2,96,768]{3,2,1,0:T(8,128)(2,1)}, bf16[2,2,96,768]{3,2,1,0:T(8,128)(2,1)S(1)}, u32[]{:S(2)}, u32[]{:S(2)}) collective-permute-start(bf16[2,2,96,768]{3,2,1,0:T(8,128)(2,1)} %get-tuple-element.242), channel_id=1, source_target_pairs={{0,8},{8,0},{1,9},{9,1},{2,10},{10,2},{3,11},{11,3},{4,12},{12,4},... | collective-permute-start | bytes 1769480 | tf_op jit(solution)/shard_map/ppermute | solution.py:1009
  108.1 15.5 %collective-permute-start.17 = (bf16[2,2,96,768]{3,2,1,0:T(8,128)(2,1)}, bf16[2,2,96,768]{3,2,1,0:T(8,128)(2,1)S(1)}, u32[]{:S(2)}, u32[]{:S(2)}) collective-permute-start(bf16[2,2,96,768]{3,2,1,0:T(8,128)(2,1)} %get-tuple-element.243), channel_id=1, source_target_pairs={{0,16},{16,0},{1,17},{17,1},{2,18},{18,2},{3,19},{19,3},{4,20},{20... | collective-permute-start | bytes 1769480 | tf_op jit(solution)/shard_map/ppermute | solution.py:1010
  123.7 2.8 %collective-permute-start.20 = (bf16[640,768]{1,0:T(8,128)(2,1)}, bf16[640,768]{1,0:T(8,128)(2,1)S(1)}, u32[]{:S(2)}, u32[]{:S(2)}) collective-permute-start(bf16[640,768]{1,0:T(8,128)(2,1)} %get-tuple-element.248), channel_id=1, source_target_pairs={{0,4},{4,0},{1,5},{5,1},{2,6},{6,2},{3,7},{7,3},{8,12},{12,8},{9,1... | collective-permute-start | bytes 2949128 | tf_op jit(solution)/shard_map/ppermute | solution.py:1098
  123.8 27.0 %collective-permute-start.24 = (bf16[2,4,2,96,768]{4,3,2,1,0:T(8,128)(2,1)}, bf16[2,4,2,96,768]{4,3,2,1,0:T(8,128)(2,1)S(1)}, u32[]{:S(2)}, u32[]{:S(2)}) collective-permute-start(bf16[2,4,2,96,768]{4,3,2,1,0:T(8,128)(2,1)} %get-tuple-element.267.refs_3_.refs_4_), channel_id=1, source_target_pairs={{7,4},{4,5},{5,6},{6,7},{15,12},{12,13},{13,14},{14,15},{23,20},{2... | collective-permute-start | bytes 7077896 | tf_op jit(solution)/shard_map/ppermute | solution.py:1097
  130.7 32.1 %copy-start.1 = (bf16[640,768]{1,0:T(8,128)(2,1)}, bf16[640,768]{1,0:T(8,128)(2,1)S(1)}, u32[]{:S(2)}) copy-start(bf16[640,768]{1,0:T(8,128)(2,1)S(1)} %get-tuple-element.279.rest_6_.grad_first) | copy-start | bytes 2949124
  130.7 4.3 %collective-permute-start.21 = (bf16[640,768]{1,0:T(8,128)(2,1)S(1)}, bf16[640,768]{1,0:T(8,128)(2,1)S(1)}, u32[]{:S(2)}, u32[]{:S(2)}) collective-permute-start(bf16[640,768]{1,0:T(8,128)(2,1)S(1)} %get-tuple-element.279.rest_6_.grad_first), channel_id=1, source_target_pairs={{0,4},{4,0},{1,5},{5,1},{2,6},{6,2},{3,7},{7,3},{8,12},{12,8},{9,1... | collective-permute-start | bytes 2949128 | tf_op jit(solution)/shard_map/ppermute | solution.py:1108
  135.1 15.8 %collective-permute-start.25 = (bf16[640,768]{1,0:T(8,128)(2,1)S(1)}, bf16[640,768]{1,0:T(8,128)(2,1)S(1)}, u32[]{:S(2)}, u32[]{:S(2)}) collective-permute-start(bf16[640,768]{1,0:T(8,128)(2,1)S(1)} %copy-done.22), channel_id=1, source_target_pairs={{0,4},{4,0},{1,5},{5,1},{2,6},{6,2},{3,7},{7,3},{8,12},{12,8},{9,1... | collective-permute-start | bytes 2949128 | tf_op jit(solution)/shard_map/ppermute | solution.py:1109
  135.4 15.3 %collective-permute-start.22 = (bf16[2,96,768]{2,1,0:T(8,128)(2,1)S(1)}, bf16[2,96,768]{2,1,0:T(8,128)(2,1)S(1)}, u32[]{:S(2)}, u32[]{:S(2)}) collective-permute-start(bf16[2,96,768]{2,1,0:T(8,128)(2,1)S(1)} %get-tuple-element.253), channel_id=1, source_target_pairs={{0,16},{16,0},{1,17},{17,1},{2,18},{18,2},{3,19},{19,3},{4,20},{20... | collective-permute-start | bytes 884744 | tf_op jit(solution)/shard_map/ppermute | solution.py:1014
  137.0 13.8 %collective-permute-start.23 = (bf16[2,96,768]{2,1,0:T(8,128)(2,1)S(1)}, bf16[2,96,768]{2,1,0:T(8,128)(2,1)S(1)}, u32[]{:S(2)}, u32[]{:S(2)}) collective-permute-start(bf16[2,96,768]{2,1,0:T(8,128)(2,1)S(1)} %get-tuple-element.254), channel_id=1, source_target_pairs={{0,8},{8,0},{1,9},{9,1},{2,10},{10,2},{3,11},{11,3},{4,12},{12,4},... | collective-permute-start | bytes 884744 | tf_op jit(solution)/shard_map/ppermute | solution.py:1014
  151.6 23.4 %collective-permute-start.26 = (bf16[4,2,96,768]{3,2,1,0:T(8,128)(2,1)S(1)}, bf16[4,2,96,768]{3,2,1,0:T(8,128)(2,1)S(1)}, u32[]{:S(2)}, u32[]{:S(2)}) collective-permute-start(bf16[4,2,96,768]{3,2,1,0:T(8,128)(2,1)S(1)} %get-tuple-element.276), channel_id=1, source_target_pairs={{0,4},{4,0},{1,5},{5,1},{2,6},{6,2},{3,7},{7,3},{8,12},{12,8},{9,1... | collective-permute-start | bytes 3538952 | tf_op jit(solution)/shard_map/ppermute | solution.py:1124
  157.6 17.5 %collective-permute-start.31 = (bf16[2,2,96,768]{3,2,1,0:T(8,128)(2,1)S(1)}, bf16[2,2,96,768]{3,2,1,0:T(8,128)(2,1)S(1)}, u32[]{:S(2)}, u32[]{:S(2)}) collective-permute-start(bf16[2,2,96,768]{3,2,1,0:T(8,128)(2,1)S(1)} %get-tuple-element.278), channel_id=1, source_target_pairs={{1,0},{2,1},{3,2},{0,3},{6,4},{7,5},{4,6},{5,7},{9,8},{10,9},{11,1... | collective-permute-start | bytes 1769480 | tf_op jit(solution)/shard_map/ppermute | solution.py:1123
  159.3 15.7 %collective-permute-start.28 = (bf16[2,1,96,768]{3,2,1,0:T(8,128)(2,1)S(1)}, bf16[2,1,96,768]{3,2,1,0:T(8,128)(2,1)S(1)}, u32[]{:S(2)}, u32[]{:S(2)}) collective-permute-start(bf16[2,1,96,768]{3,2,1,0:T(8,128)(2,1)S(1)} %get-tuple-element.287), channel_id=1, source_target_pairs={{0,8},{8,0},{1,9},{9,1},{2,10},{10,2},{3,11},{11,3},{4,12},{12,4},... | collective-permute-start | bytes 884744 | tf_op jit(solution)/shard_map/ppermute | solution.py:1019
  160.9 14.2 %collective-permute-start.29 = (bf16[2,1,96,768]{3,2,1,0:T(8,128)(2,1)S(1)}, bf16[2,1,96,768]{3,2,1,0:T(8,128)(2,1)S(1)}, u32[]{:S(2)}, u32[]{:S(2)}) collective-permute-start(bf16[2,1,96,768]{3,2,1,0:T(8,128)(2,1)S(1)} %get-tuple-element.288), channel_id=1, source_target_pairs={{0,16},{16,0},{1,17},{17,1},{2,18},{18,2},{3,19},{19,3},{4,20},{20... | collective-permute-start | bytes 884744 | tf_op jit(solution)/shard_map/ppermute | solution.py:1020
  162.3 12.8 %collective-permute-start.30 = (bf16[2,1,96,768]{3,2,1,0:T(8,128)(2,1)S(1)}, bf16[2,1,96,768]{3,2,1,0:T(8,128)(2,1)S(1)}, u32[]{:S(2)}, u32[]{:S(2)}) collective-permute-start(bf16[2,1,96,768]{3,2,1,0:T(8,128)(2,1)S(1)} %get-tuple-element.289), channel_id=1, source_target_pairs={{0,24},{8,16},{16,8},{24,0},{1,25},{9,17},{17,9},{25,1},{2,26},{10... | collective-permute-start | bytes 884744 | tf_op jit(solution)/shard_map/ppermute | solution.py:1021
  175.1 8.1 %collective-permute-start.32 = (bf16[640,768]{1,0:T(8,128)(2,1)S(1)}, bf16[640,768]{1,0:T(8,128)(2,1)S(1)}, u32[]{:S(2)}, u32[]{:S(2)}) collective-permute-start(bf16[640,768]{1,0:T(8,128)(2,1)S(1)} %get-tuple-element.291), channel_id=1, source_target_pairs={{0,4},{4,0},{1,5},{5,1},{2,6},{6,2},{3,7},{7,3},{8,12},{12,8},{9,1... | collective-permute-start | bytes 2949128 | tf_op jit(solution)/shard_map/ppermute | solution.py:1136
  178.6 5.2 %collective-permute-start.27 = (bf16[640,768]{1,0:T(8,128)(2,1)S(1)}, bf16[640,768]{1,0:T(8,128)(2,1)S(1)}, u32[]{:S(2)}, u32[]{:S(2)}) collective-permute-start(bf16[640,768]{1,0:T(8,128)(2,1)S(1)} %get-tuple-element.277), channel_id=1, source_target_pairs={{0,4},{4,0},{1,5},{5,1},{2,6},{6,2},{3,7},{7,3},{8,12},{12,8},{9,1... | collective-permute-start | bytes 2949128 | tf_op jit(solution)/shard_map/ppermute | solution.py:1133
  179.7 9.1 %collective-permute-start.37 = (bf16[2,96,768]{2,1,0:T(8,128)(2,1)S(1)}, bf16[2,96,768]{2,1,0:T(8,128)(2,1)S(1)}, u32[]{:S(2)}, u32[]{:S(2)}) collective-permute-start(bf16[2,96,768]{2,1,0:T(8,128)(2,1)S(1)} %get-tuple-element.308), channel_id=1, source_target_pairs={{0,4},{4,0},{1,5},{5,1},{2,6},{6,2},{3,7},{7,3},{8,12},{12,8},{9,1... | collective-permute-start | bytes 884744 | tf_op jit(solution)/shard_map/ppermute | solution.py:1144
  180.2 11.5 %collective-permute-start.34 = (bf16[2,1,96,768]{3,2,1,0:T(8,128)(2,1)S(1)}, bf16[2,1,96,768]{3,2,1,0:T(8,128)(2,1)S(1)}, u32[]{:S(2)}, u32[]{:S(2)}) collective-permute-start(bf16[2,1,96,768]{3,2,1,0:T(8,128)(2,1)S(1)} %get-tuple-element.299), channel_id=1, source_target_pairs={{0,8},{8,0},{1,9},{9,1},{2,10},{10,2},{3,11},{11,3},{4,12},{12,4},... | collective-permute-start | bytes 884744 | tf_op jit(solution)/shard_map/ppermute | solution.py:1019
  181.8 15.0 %collective-permute-start.35 = (bf16[2,1,96,768]{3,2,1,0:T(8,128)(2,1)S(1)}, bf16[2,1,96,768]{3,2,1,0:T(8,128)(2,1)S(1)}, u32[]{:S(2)}, u32[]{:S(2)}) collective-permute-start(bf16[2,1,96,768]{3,2,1,0:T(8,128)(2,1)S(1)} %get-tuple-element.300), channel_id=1, source_target_pairs={{0,16},{16,0},{1,17},{17,1},{2,18},{18,2},{3,19},{19,3},{4,20},{20... | collective-permute-start | bytes 884744 | tf_op jit(solution)/shard_map/ppermute | solution.py:1020
  183.2 16.1 %collective-permute-start.36 = (bf16[2,1,96,768]{3,2,1,0:T(8,128)(2,1)S(1)}, bf16[2,1,96,768]{3,2,1,0:T(8,128)(2,1)S(1)}, u32[]{:S(2)}, u32[]{:S(2)}) collective-permute-start(bf16[2,1,96,768]{3,2,1,0:T(8,128)(2,1)S(1)} %get-tuple-element.301), channel_id=1, source_target_pairs={{0,24},{8,16},{16,8},{24,0},{1,25},{9,17},{17,9},{25,1},{2,26},{10... | collective-permute-start | bytes 884744 | tf_op jit(solution)/shard_map/ppermute | solution.py:1021
  188.8 10.5 %collective-permute-start.33 = (f32[16,768]{1,0:T(8,128)S(1)}, f32[16,768]{1,0:T(8,128)S(1)}, u32[]{:S(2)}, u32[]{:S(2)}) collective-permute-start(f32[16,768]{1,0:T(8,128)S(1)} %get-tuple-element.297.refs_4_), channel_id=1, source_target_pairs={{0,4},{4,0},{1,5},{5,1},{2,6},{6,2},{3,7},{7,3},{8,12},{12,8},{9,1... | collective-permute-start | bytes 147464 | tf_op jit(solution)/shard_map/ppermute | solution.py:1158
  188.8 13.5 %collective-permute-start.39 = (bf16[2,1,96,768]{3,2,1,0:T(8,128)(2,1)S(1)}, bf16[2,1,96,768]{3,2,1,0:T(8,128)(2,1)S(1)}, u32[]{:S(2)}, u32[]{:S(2)}) collective-permute-start(bf16[2,1,96,768]{3,2,1,0:T(8,128)(2,1)S(1)} %get-tuple-element.315), channel_id=1, source_target_pairs={{1,0},{2,1},{3,2},{0,3},{6,4},{7,5},{4,6},{5,7},{9,8},{10,9},{11,1... | collective-permute-start | bytes 884744 | tf_op jit(solution)/shard_map/ppermute | solution.py:1143
  191.7 16.5 %collective-permute-start.44 = (bf16[2,96,768]{2,1,0:T(8,128)(2,1)S(1)}, bf16[2,96,768]{2,1,0:T(8,128)(2,1)S(1)}, u32[]{:S(2)}, u32[]{:S(2)}) collective-permute-start(bf16[2,96,768]{2,1,0:T(8,128)(2,1)S(1)} %get-tuple-element.328), channel_id=1, source_target_pairs={{0,8},{8,0},{1,9},{9,1},{2,10},{10,2},{3,11},{11,3},{4,12},{12,4},... | collective-permute-start | bytes 884744 | tf_op jit(solution)/shard_map/ppermute | solution.py:1019
  196.8 13.5 %collective-permute-start.45 = (bf16[2,96,768]{2,1,0:T(8,128)(2,1)S(1)}, bf16[2,96,768]{2,1,0:T(8,128)(2,1)S(1)}, u32[]{:S(2)}, u32[]{:S(2)}) collective-permute-start(bf16[2,96,768]{2,1,0:T(8,128)(2,1)S(1)} %get-tuple-element.329), channel_id=1, source_target_pairs={{0,16},{16,0},{1,17},{17,1},{2,18},{18,2},{3,19},{19,3},{4,20},{20... | collective-permute-start | bytes 884744 | tf_op jit(solution)/shard_map/ppermute | solution.py:1020
  199.3 11.9 %collective-permute-start.46 = (bf16[2,96,768]{2,1,0:T(8,128)(2,1)S(1)}, bf16[2,96,768]{2,1,0:T(8,128)(2,1)S(1)}, u32[]{:S(2)}, u32[]{:S(2)}) collective-permute-start(bf16[2,96,768]{2,1,0:T(8,128)(2,1)S(1)} %get-tuple-element.330), channel_id=1, source_target_pairs={{0,24},{8,16},{16,8},{24,0},{1,25},{9,17},{17,9},{25,1},{2,26},{10... | collective-permute-start | bytes 884744 | tf_op jit(solution)/shard_map/ppermute | solution.py:1021
  200.0 2.4 collective-permute-start.38
  203.0 12.3 %collective-permute-start.40 = (bf16[1,96,768]{2,1,0:T(8,128)(2,1)S(1)}, bf16[1,96,768]{2,1,0:T(8,128)(2,1)S(1)}, u32[]{:S(2)}, u32[]{:S(2)}) collective-permute-start(bf16[1,96,768]{2,1,0:T(8,128)(2,1)S(1)} %get-tuple-element.325), channel_id=1, source_target_pairs={{0,4},{4,0},{1,5},{5,1},{2,6},{6,2},{3,7},{7,3},{8,12},{12,8},{9,1... | collective-permute-start | bytes 442376 | tf_op jit(solution)/shard_map/ppermute | solution.py:1175
  207.7 4.2 %collective-permute-start.41 = (f32[16,768]{1,0:T(8,128)S(1)}, f32[16,768]{1,0:T(8,128)S(1)}, u32[]{:S(2)}, u32[]{:S(2)}) collective-permute-start(f32[16,768]{1,0:T(8,128)S(1)} %get-tuple-element.338.refs_8_), channel_id=1, source_target_pairs={{0,8},{8,0},{1,9},{9,1},{2,10},{10,2},{3,11},{11,3},{4,12},{12,4},... | collective-permute-start | bytes 147464 | tf_op jit(solution)/shard_map/ppermute | solution.py:997
  208.2 4.1 %collective-permute-start.42 = (f32[16,768]{1,0:T(8,128)S(1)}, f32[16,768]{1,0:T(8,128)S(1)}, u32[]{:S(2)}, u32[]{:S(2)}) collective-permute-start(f32[16,768]{1,0:T(8,128)S(1)} %get-tuple-element.338.refs_8_), channel_id=1, source_target_pairs={{0,16},{16,0},{1,17},{17,1},{2,18},{18,2},{3,19},{19,3},{4,20},{20... | collective-permute-start | bytes 147464 | tf_op jit(solution)/shard_map/ppermute | solution.py:998
  210.3 5.0 %collective-permute-start.43 = (f32[16,768]{1,0:T(8,128)S(1)}, f32[16,768]{1,0:T(8,128)S(1)}, u32[]{:S(2)}, u32[]{:S(2)}) collective-permute-start(f32[16,768]{1,0:T(8,128)S(1)} %get-tuple-element.338.refs_8_), channel_id=1, source_target_pairs={{0,24},{8,16},{16,8},{24,0},{1,25},{9,17},{17,9},{25,1},{2,26},{10... | collective-permute-start | bytes 147464 | tf_op jit(solution)/shard_map/ppermute | solution.py:999
  216.1 7.8 %collective-permute-start.50 = (f32[16,768]{1,0:T(8,128)S(1)}, f32[16,768]{1,0:T(8,128)S(1)}, u32[]{:S(2)}, u32[]{:S(2)}) collective-permute-start(f32[16,768]{1,0:T(8,128)S(1)} %get-tuple-element.343), channel_id=1, source_target_pairs={{0,1},{1,2},{2,3},{3,0},{4,5},{5,6},{6,7},{7,4},{8,9},{9,10},{10,1... | collective-permute-start | bytes 147464 | tf_op jit(solution)/shard_map/ppermute | solution.py:1185
  216.5 13.1 %collective-permute-start.47 = (bf16[3,96,768]{2,1,0:T(8,128)(2,1)S(1)}, bf16[3,96,768]{2,1,0:T(8,128)(2,1)S(1)}, u32[]{:S(2)}, u32[]{:S(2)}) collective-permute-start(bf16[3,96,768]{2,1,0:T(8,128)(2,1)S(1)} %get-tuple-element.346.refs_0_), channel_id=1, source_target_pairs={{0,8},{8,0},{1,9},{9,1},{2,10},{10,2},{3,11},{11,3},{4,12},{12,4},... | collective-permute-start | bytes 1327112 | tf_op jit(solution)/shard_map/ppermute | solution.py:997
  217.5 19.2 %collective-permute-start.48 = (bf16[3,96,768]{2,1,0:T(8,128)(2,1)S(1)}, bf16[3,96,768]{2,1,0:T(8,128)(2,1)S(1)}, u32[]{:S(2)}, u32[]{:S(2)}) collective-permute-start(bf16[3,96,768]{2,1,0:T(8,128)(2,1)S(1)} %get-tuple-element.346.refs_0_), channel_id=1, source_target_pairs={{0,16},{16,0},{1,17},{17,1},{2,18},{18,2},{3,19},{19,3},{4,20},{20... | collective-permute-start | bytes 1327112 | tf_op jit(solution)/shard_map/ppermute | solution.py:998
  219.0 17.8 %collective-permute-start.49 = (bf16[3,96,768]{2,1,0:T(8,128)(2,1)S(1)}, bf16[3,96,768]{2,1,0:T(8,128)(2,1)S(1)}, u32[]{:S(2)}, u32[]{:S(2)}) collective-permute-start(bf16[3,96,768]{2,1,0:T(8,128)(2,1)S(1)} %get-tuple-element.346.refs_0_), channel_id=1, source_target_pairs={{0,24},{8,16},{16,8},{24,0},{1,25},{9,17},{17,9},{25,1},{2,26},{10... | collective-permute-start | bytes 1327112 | tf_op jit(solution)/shard_map/ppermute | solution.py:999
  220.4 5.6 %collective-permute-start.51 = (f32[16,768]{1,0:T(8,128)S(1)}, f32[16,768]{1,0:T(8,128)S(1)}, u32[]{:S(2)}, u32[]{:S(2)}) collective-permute-start(f32[16,768]{1,0:T(8,128)S(1)} %get-tuple-element.343), channel_id=1, source_target_pairs={{0,2},{1,3},{2,0},{3,1},{4,6},{5,7},{6,4},{7,5},{8,10},{9,11},{10,... | collective-permute-start | bytes 147464 | tf_op jit(solution)/shard_map/ppermute | solution.py:1185
  223.9 4.1 %collective-permute-start.52 = (f32[16,768]{1,0:T(8,128)S(1)}, f32[16,768]{1,0:T(8,128)S(1)}, u32[]{:S(2)}, u32[]{:S(2)}) collective-permute-start(f32[16,768]{1,0:T(8,128)S(1)} %get-tuple-element.343), channel_id=1, source_target_pairs={{0,3},{1,0},{2,1},{3,2},{4,7},{5,4},{6,5},{7,6},{8,11},{9,8},{10,9... | collective-permute-start | bytes 147464 | tf_op jit(solution)/shard_map/ppermute | solution.py:1185
  236.7 3.5 %collective-permute-start.53 = (bf16[3,96,768]{2,1,0:T(8,128)(2,1)S(1)}, bf16[3,96,768]{2,1,0:T(8,128)(2,1)S(1)}, u32[]{:S(2)}, u32[]{:S(2)}) collective-permute-start(bf16[3,96,768]{2,1,0:T(8,128)(2,1)S(1)} %get-tuple-element.346.refs_0_), channel_id=1, source_target_pairs={{0,4},{4,0},{1,5},{5,1},{2,6},{6,2},{3,7},{7,3},{8,12},{12,8},{9,1... | collective-permute-start | bytes 1327112 | tf_op jit(solution)/shard_map/ppermute | solution.py:1197
  236.7 3.5 %collective-permute-start.54 = (bf16[3,96,768]{2,1,0:T(8,128)(2,1)S(1)}, bf16[3,96,768]{2,1,0:T(8,128)(2,1)S(1)}, u32[]{:S(2)}, u32[]{:S(2)}) collective-permute-start(bf16[3,96,768]{2,1,0:T(8,128)(2,1)S(1)} %collective-permute-done.47.refs_1_), channel_id=1, source_target_pairs={{0,4},{4,0},{1,5},{5,1},{2,6},{6,2},{3,7},{7,3},{8,12},{12,8},{9,1... | collective-permute-start | bytes 1327112 | tf_op jit(solution)/shard_map/ppermute | solution.py:1197
  237.2 3.0 %collective-permute-start.55 = (bf16[3,96,768]{2,1,0:T(8,128)(2,1)S(1)}, bf16[3,96,768]{2,1,0:T(8,128)(2,1)S(1)}, u32[]{:S(2)}, u32[]{:S(2)}) collective-permute-start(bf16[3,96,768]{2,1,0:T(8,128)(2,1)S(1)} %collective-permute-done.48.refs_2_), channel_id=1, source_target_pairs={{0,4},{4,0},{1,5},{5,1},{2,6},{6,2},{3,7},{7,3},{8,12},{12,8},{9,1... | collective-permute-start | bytes 1327112 | tf_op jit(solution)/shard_map/ppermute | solution.py:1197
  237.2 3.2 %collective-permute-start.56 = (bf16[3,96,768]{2,1,0:T(8,128)(2,1)S(1)}, bf16[3,96,768]{2,1,0:T(8,128)(2,1)S(1)}, u32[]{:S(2)}, u32[]{:S(2)}) collective-permute-start(bf16[3,96,768]{2,1,0:T(8,128)(2,1)S(1)} %collective-permute-done.49.refs_3_), channel_id=1, source_target_pairs={{0,4},{4,0},{1,5},{5,1},{2,6},{6,2},{3,7},{7,3},{8,12},{12,8},{9,1... | collective-permute-start | bytes 1327112 | tf_op jit(solution)/shard_map/ppermute | solution.py:1197
  (17 other events, 144.1 us)

commit v3 on v2

--- a/solution.py
+++ b/solution.py
@@ -111,7 +111,7 @@
 
 
 def norm_two_kernel(tokens, mine, received, bias, gain, shift, first_sum, normed):
-    total = tokens[...].astype(F32) + (mine[...] + received[...].astype(F32)) + bias[...]
+    total = tokens[...].astype(F32) + (mine[...].astype(F32) + received[...].astype(F32)) + bias[...]
     first_sum[...] = total
     center, rstd = centred(total)
     normed[...] = (center * rstd * gain[...] + shift[...]).astype(BF16)
@@ -270,8 +270,8 @@
     both = bias[...].astype(F32)
     rows = jnp.where(row == 0, both[0:1, :], jnp.where(row == 1, both[1:2, :], 0.0))
     row_all = lax.broadcasted_iota(jnp.int32, (16, out.shape[1]), 0)
-    out[size:, :] = jnp.where(row_all == 2, up_bias[...].astype(F32), 0.0).astype(BF16)
-    row_two = jnp.where(row == 2, up_bias[:, 0:columns].astype(F32), rows)
+    out[size:, :] = jnp.where(row_all == 2, up_bias[...].astype(F32).reshape(1, -1), 0.0).astype(BF16)
+    row_two = jnp.where(row == 2, up_bias[...].astype(F32).reshape(1, -1)[:, 0:columns], rows)
     out[size:, 0:columns] = row_two.astype(BF16)
     tail[size:, :] = out[size:, :]
     tail_copy.wait()
@@ -1033,7 +1033,7 @@
         norm_one_shift,
     )
     piece_one, tail_one = pack_attention(
-        place, projection, mixer_weight, after(input_bias, normed_one), one_row(up_bias)
+        place, projection, mixer_weight, after(input_bias, normed_one), up_bias
     )
     depth_near_one = lax.ppermute(piece_one, ("c", "t"), to_near)
     normed_other = lax.ppermute(normed_one, "c", swap)
@@ -1057,7 +1057,7 @@
     near_y = lax.ppermute(near_two, "a", swap)
     far_two = lax.ppermute(after(both_two, near_two), ("c", "t"), to_far)
     saved, soft, part = attention(
-        place, own_one, near_one, far_one, normed_one, (saved, soft), F32
+        place, own_one, near_one, far_one, normed_one, (saved, soft), BF16
     )
     part, part_received, near_x, near_y, grad_other = together(
         part, part_received, near_x, near_y, grad_other

time: 244 us -> 243 us (level)
  transfers between devices with their start and end apart: 57 -> 57, of which waited for: 21 -> 22; matrix products, arithmetic and copies ran while one was open for 2% -> 1% of each run, Pallas kernels for 40% -> 40%
where the time goes in v3:
time: 243 us
  Pallas kernels  105 us (43%)
  starting transfers between devices  79.3 us (33%)
  waiting for transfers between devices  52.3 us (22%)
  local copies, waits for them, and re-layouts  3.1 us (1%)
    pallas_call x2, Pallas kernels, hidden_block(): pl.pallas_call(functools.partial(hidden_kernel, last), out_shape=(*grad_s...  30.3 us
    pallas_call x2, Pallas kernels, attention_back(): pl.pallas_call(functools.partial(attention_back_kernel, heads, far), grid...  24.6 us
    pallas_call x2, Pallas kernels, attention(): pl.pallas_call(functools.partial(attention_kernel, heads), grid=(tiles,),...  20.4 us
    ppermute x3, waiting for transfers between devices, spread(): lax.ppermute(piece, 'a', swap)  12.7 us
    ppermute x1, starting transfers between devices, local(): grad_other = lax.ppermute(after(output_grad, part), 'c', swap)  11.3 us
    ppermute x1, waiting for transfers between devices, local(): depth_near_one = lax.ppermute(piece_one, ('c', 't'), to_near)  8.53 us
    ppermute x1, starting transfers between devices, local(): received_far = lax.ppermute(send_far, 'c', swap)  5.92 us
    ppermute x3, starting transfers between devices, direct(): lax.ppermute(send_y, 'a', swap)  5.32 us
  transfers between devices with their start and end apart: 57, of which 22 were waited for; matrix products, arithmetic and copies ran while one was open for 1% of the time, Pallas kernels for 40%

profile of v3, /device:TPU:0, one launch (start us, length us, event | category | flops | bytes accessed | tf_op | source)
XLA Modules:
  0.0 242.5 jit_solution(1204308424080220585)
XLA Ops:
  1.4 2.9 %shard_map.254.normed.counts.rest_4_ = bf16[656,768]{1,0:T(8,128)(2,1)S(1)} custom-call(s32[3]{0:T(128)S(1)} %pad_add_fusion.place, s32[32]{0:T(128)S(1)} %copy-done.7, bf16[640,768]{1,0:T(8,128)(2,1)} %tokens.5, f32[768]{0:T(1024)} %gain.1, f32[768]{0:T(1024)} %shift.1), custom_call_target="tpu_custom_call" | custom-call | flops 4915200 | bytes 1966080 | tf_op jit(solution)/shard_map/pallas_call | solution.py:103
  4.8 1.9 shard_map.255
  6.8 2.7 %collective-permute-start = (bf16[208,768]{1,0:T(8,128)(2,1)S(1)}, bf16[208,768]{1,0:T(8,128)(2,1)S(1)}, u32[]{:S(2)}, u32[]{:S(2)}) collective-permute-start(bf16[208,768]{1,0:T(8,128)(2,1)S(1)} %get-tuple-element.194), channel_id=1, source_target_pairs={{0,1},{1,2},{2,3},{3,0},{4,6},{5,7},{6,4},{7,5},{8,9},{9,10},{10,1... | collective-permute-start | bytes 958472 | tf_op jit(solution)/shard_map/ppermute | solution.py:1038
  9.4 1.6 shard_map.256
  11.3 8.5 %collective-permute-done.near0.rest_5_.rest_0_ = bf16[208,768]{1,0:T(8,128)(2,1)S(1)} collective-permute-done((bf16[208,768]{1,0:T(8,128)(2,1)S(1)}, bf16[208,768]{1,0:T(8,128)(2,1)S(1)}, u32[]{:S(2)}, u32[]{:S(2)}) %collective-permute-start) | collective-permute-done | bytes 319520 | tf_op jit(solution)/shard_map/ppermute | solution.py:1038
  20.5 0.8 collective-permute-start.6
  21.3 1.6 collective-permute-start.2
  22.9 1.5 collective-permute-start.3
  24.9 3.5 %collective-permute-done.2.near1.rest_1_ = bf16[208,768]{1,0:T(8,128)(2,1)S(1)} collective-permute-done((bf16[208,768]{1,0:T(8,128)(2,1)S(1)}, bf16[208,768]{1,0:T(8,128)(2,1)S(1)}, u32[]{:S(2)}, u32[]{:S(2)}) %collective-permute-start.2) | collective-permute-done | bytes 319520 | tf_op jit(solution)/shard_map/ppermute | solution.py:997
  28.4 5.2 %collective-permute-done.3.near2.rest_2_ = bf16[208,768]{1,0:T(8,128)(2,1)S(1)} collective-permute-done((bf16[208,768]{1,0:T(8,128)(2,1)S(1)}, bf16[208,768]{1,0:T(8,128)(2,1)S(1)}, u32[]{:S(2)}, u32[]{:S(2)}) %collective-permute-start.3) | collective-permute-done | bytes 319520 | tf_op jit(solution)/shard_map/ppermute | solution.py:998
  33.6 2.2 collective-permute-start.7
  35.8 10.2 %shard_map.257 = (bf16[8,1280,192]{2,1,0:T(8,128)(2,1)}, bf16[1280,768]{1,0:T(8,128)(2,1)}, bf16[640,768]{1,0:T(8,128)(2,1)S(1)}) custom-call(s32[3]{0:T(128)S(1)} %pad_add_fusion.place, bf16[576,768]{1,0:T(8,128)(2,1)S(1)} %bitcast.11, bf16[208,768]{1,0:T(8,128)(2,1)S(1)} %get-tuple-element.199.tail.rest_1_, ...), custom_call_target="tpu_custom_call" | custom-call | flops 1765949440 | bytes 9915200 | tf_op jit(solution)/shard_map/pallas_call | solution.py:488
  46.0 2.2 collective-permute-done.7.rest_0_
  48.2 11.3 %collective-permute-start.11 = (bf16[640,768]{1,0:T(8,128)(2,1)S(1)}, bf16[640,768]{1,0:T(8,128)(2,1)S(1)}, u32[]{:S(2)}, u32[]{:S(2)}) collective-permute-start(bf16[640,768]{1,0:T(8,128)(2,1)S(1)} %copy-done.12), channel_id=1, source_target_pairs={{0,4},{4,0},{1,5},{5,1},{2,6},{6,2},{3,7},{7,3},{8,12},{12,8},{9,1... | collective-permute-start | bytes 2949128 | tf_op jit(solution)/shard_map/ppermute | solution.py:1054
  59.6 1.5 collective-permute-start.10
  61.1 2.0 collective-permute-start.9
  63.1 1.0 collective-permute-start.15
  64.1 10.2 %shard_map.258 = (bf16[8,1280,192]{2,1,0:T(8,128)(2,1)}, bf16[1280,768]{1,0:T(8,128)(2,1)}, bf16[640,768]{1,0:T(8,128)(2,1)S(1)}) custom-call(s32[3]{0:T(128)S(1)} %pad_add_fusion.place, bf16[576,768]{1,0:T(8,128)(2,1)S(1)} %bitcast.12, bf16[208,768]{1,0:T(8,128)(2,1)S(1)} %get-tuple-element.199.tail.rest_1_, ...), custom_call_target="tpu_custom_call", output_to_operand_aliasing={{0}: (11, {}), {1}: (12, {})} | custom-call | flops 1765949440 | bytes 9915200 | tf_op jit(solution)/shard_map/pallas_call | solution.py:488
  74.3 0.9 collective-permute-done.10.rest_2_
  75.3 1.5 collective-permute-done.9.rest_1_
  76.8 1.8 collective-permute-start.12
  79.0 3.8 %shard_map.259 = (f32[640,768]{1,0:T(8,128)}, bf16[640,768]{1,0:T(8,128)(2,1)S(1)}) custom-call(bf16[640,768]{1,0:T(8,128)(2,1)} %tokens.5, bf16[640,768]{1,0:T(8,128)(2,1)S(1)} %get-tuple-element.213.mine, bf16[640,768]{1,0:T(8,128)(2,1)S(1)} %collective-permute-done.8.received, f32[1,768]{1,0:T(1,128)S(1)} %reshape.51.bias, f32[1,768]{1,0:T(1,128)S(1)} %reshape.52.gain, ...), custom_call_target="tpu_custom_call" | custom-call | flops 5898240 | bytes 6881280 | tf_op jit(solution)/shard_map/pallas_call | solution.py:133
  82.9 2.0 collective-permute-done.12.rest_3_
  84.9 2.9 %collective-permute-done.13.rest_4_ = bf16[192,768]{1,0:T(8,128)(2,1)S(1)} collective-permute-done((bf16[192,768]{1,0:T(8,128)(2,1)S(1)}, bf16[192,768]{1,0:T(8,128)(2,1)S(1)}, u32[]{:S(2)}, u32[]{:S(2)}) %collective-permute-start.13) | collective-permute-done | bytes 294944 | tf_op jit(solution)/shard_map/ppermute | solution.py:1067
  88.4 2.2 collective-permute-done.14.rest_7_.rest_5_
  90.6 0.9 copy-done.22
  91.6 15.2 %shard_map.260 = (bf16[2,2,96,768]{3,2,1,0:T(8,128)(2,1)}, bf16[2,2,96,768]{3,2,1,0:T(8,128)(2,1)}, bf16[2,2,96,768]{3,2,1,0:T(8,128)(2,1)}, bf16[2,2,96,768]{3,...) custom-call(s32[3]{0:T(128)S(1)} %pad_add_fusion.place, ...), custom_call_target="tpu_custom_call" | custom-call | flops 9059696640 | bytes 19796480 | tf_op jit(solution)/shard_map/pallas_call | solution.py:762
  107.9 15.1 %shard_map.261 = (bf16[2,4,2,96,768]{4,3,2,1,0:T(8,128)(2,1)}, f32[8,768]{1,0:T(8,128)S(1)}, bf16[640,768]{1,0:T(8,128)(2,1)}, bf16[640,768]{1,0:T(8,128)(2,1)},...) custom-call(s32[3]{0:T(128)S(1)} %pad_add_fusion.place, bf16[1536,768]{1,0:T(8,128)(2,1)S(1)} %pad_maximum_fusion.rest_0_, ...), custom_call_target="tpu_custom_call" | custom-call | flops 9059696640 | bytes 19796480 | tf_op jit(solution)/shard_map/pallas_call | solution.py:762
  123.2 0.9 collective-permute-start.24
  125.0 1.0 collective-permute-done.20.part3
  126.0 4.2 %shard_map.263 = (bf16[640,768]{1,0:T(8,128)(2,1)S(1)}, f32[8,768]{1,0:T(8,128)S(1)}) custom-call(bf16[640,768]{1,0:T(8,128)(2,1)S(1)} %copy-done.3, bf16[640,768]{1,0:T(8,128)(2,1)S(1)} %collective-permute-done.18.part1, bf16[640,768]{1,0:T(8,128)(2,1)S(1)} %copy-done.4, bf16[640,768]{1,0:T(8,128)(2,1)S(1)} %collective-permute-done.20.part3, ...), custom_call_target="tpu_custom_call" | custom-call | flops 12288000 | bytes 8847360 | tf_op jit(solution)/shard_map/pallas_call | solution.py:174
  130.2 2.1 collective-permute-start.21
  132.3 2.2 collective-permute-done.21.rest_7_
  134.8 1.6 collective-permute-start.22
  136.4 1.4 collective-permute-start.23
  137.8 12.4 %shard_map.264 = (bf16[2,1,96,768]{3,2,1,0:T(8,128)(2,1)S(1)}, bf16[2,1,96,768]{3,2,1,0:T(8,128)(2,1)S(1)}, bf16[2,1,96,768]{3,2,1,0:T(8,128)(2,1)S(1)}, bf16[2,...) custom-call(s32[3]{0:T(128)S(1)} %pad_add_fusion.place, ...), custom_call_target="tpu_custom_call" | custom-call | flops 3215155200 | bytes 13830400 | tf_op jit(solution)/shard_map/pallas_call | solution.py:619
  151.0 5.9 %collective-permute-start.26 = (bf16[4,2,96,768]{3,2,1,0:T(8,128)(2,1)S(1)}, bf16[4,2,96,768]{3,2,1,0:T(8,128)(2,1)S(1)}, u32[]{:S(2)}, u32[]{:S(2)}) collective-permute-start(bf16[4,2,96,768]{3,2,1,0:T(8,128)(2,1)S(1)} %get-tuple-element.276), channel_id=1, source_target_pairs={{0,4},{4,0},{1,5},{5,1},{2,6},{6,2},{3,7},{7,3},{8,12},{12,8},{9,1... | collective-permute-start | bytes 3538952 | tf_op jit(solution)/shard_map/ppermute | solution.py:1124
  157.0 1.7 collective-permute-start.31
  158.7 1.6 collective-permute-start.28
  160.3 1.4 collective-permute-start.29
  162.2 12.2 %shard_map.266 = (bf16[2,1,96,768]{3,2,1,0:T(8,128)(2,1)S(1)}, bf16[2,1,96,768]{3,2,1,0:T(8,128)(2,1)S(1)}, bf16[2,1,96,768]{3,2,1,0:T(8,128)(2,1)S(1)}, bf16[2,...) custom-call(s32[3]{0:T(128)S(1)} %pad_add_fusion.place, ...), custom_call_target="tpu_custom_call" | custom-call | flops 3215155200 | bytes 13830400 | tf_op jit(solution)/shard_map/pallas_call | solution.py:619
  174.5 3.5 %collective-permute-start.32 = (bf16[640,768]{1,0:T(8,128)(2,1)S(1)}, bf16[640,768]{1,0:T(8,128)(2,1)S(1)}, u32[]{:S(2)}, u32[]{:S(2)}) collective-permute-start(bf16[640,768]{1,0:T(8,128)(2,1)S(1)} %get-tuple-element.291), channel_id=1, source_target_pairs={{0,4},{4,0},{1,5},{5,1},{2,6},{6,2},{3,7},{7,3},{8,12},{12,8},{9,1... | collective-permute-start | bytes 2949128 | tf_op jit(solution)/shard_map/ppermute | solution.py:1136
  178.0 1.1 shard_map.268
  179.6 1.6 collective-permute-start.34
  181.2 1.4 collective-permute-start.35
  183.2 5.0 %shard_map.267 = (f32[640,768]{1,0:T(8,128)}, f32[16,768]{1,0:T(8,128)S(1)}) custom-call(s32[3]{0:T(128)S(1)} %pad_add_fusion.place, bf16[640,768]{1,0:T(8,128)(2,1)S(1)} %get-tuple-element.270.part0, bf16[640,768]{1,0:T(8,128)(2,1)S(1)} %collective-permute-done.27.part1, bf16[640,768]{1,0:T(8,128)(2,1)S(1)} %get-tuple-element.290.part2, ...), custom_call_target="tpu_custom_call" | custom-call | flops 12288000 | bytes 7864320 | tf_op jit(solution)/shard_map/pallas_call | solution.py:233
  188.2 2.8 %collective-permute-start.39 = (bf16[2,1,96,768]{3,2,1,0:T(8,128)(2,1)S(1)}, bf16[2,1,96,768]{3,2,1,0:T(8,128)(2,1)S(1)}, u32[]{:S(2)}, u32[]{:S(2)}) collective-permute-start(bf16[2,1,96,768]{3,2,1,0:T(8,128)(2,1)S(1)} %get-tuple-element.315), channel_id=1, source_target_pairs={{1,0},{2,1},{3,2},{0,3},{6,4},{7,5},{4,6},{5,7},{9,8},{10,9},{11,1... | collective-permute-start | bytes 884744 | tf_op jit(solution)/shard_map/ppermute | solution.py:1143
  191.1 1.6 collective-permute-start.44
  192.6 3.6 %collective-permute-done.35.refs_2_ = bf16[2,1,96,768]{3,2,1,0:T(8,128)(2,1)S(1)} collective-permute-done((bf16[2,1,96,768]{3,2,1,0:T(8,128)(2,1)S(1)}, bf16[2,1,96,768]{3,2,1,0:T(8,128)(2,1)S(1)}, u32[]{:S(2)}, u32[]{:S(2)}) %collective-permute-start.35) | collective-permute-done | bytes 294944 | tf_op jit(solution)/shard_map/ppermute | solution.py:1020
  196.2 2.5 %collective-permute-start.45 = (bf16[2,96,768]{2,1,0:T(8,128)(2,1)S(1)}, bf16[2,96,768]{2,1,0:T(8,128)(2,1)S(1)}, u32[]{:S(2)}, u32[]{:S(2)}) collective-permute-start(bf16[2,96,768]{2,1,0:T(8,128)(2,1)S(1)} %get-tuple-element.329), channel_id=1, source_target_pairs={{0,16},{16,0},{1,17},{17,1},{2,18},{18,2},{3,19},{19,3},{4,20},{20... | collective-permute-start | bytes 884744 | tf_op jit(solution)/shard_map/ppermute | solution.py:1020
  200.2 1.6 add_convert_fusion
  202.5 4.6 %collective-permute-start.40 = (bf16[1,96,768]{2,1,0:T(8,128)(2,1)S(1)}, bf16[1,96,768]{2,1,0:T(8,128)(2,1)S(1)}, u32[]{:S(2)}, u32[]{:S(2)}) collective-permute-start(bf16[1,96,768]{2,1,0:T(8,128)(2,1)S(1)} %get-tuple-element.325), channel_id=1, source_target_pairs={{0,4},{4,0},{1,5},{5,1},{2,6},{6,2},{3,7},{7,3},{8,12},{12,8},{9,1... | collective-permute-start | bytes 442376 | tf_op jit(solution)/shard_map/ppermute | solution.py:1175
  207.6 1.6 collective-permute-start.42
  209.7 0.9 collective-permute-start.43
  211.7 3.1 %collective-permute-done.43.refs_11_ = f32[16,768]{1,0:T(8,128)S(1)} collective-permute-done((f32[16,768]{1,0:T(8,128)S(1)}, f32[16,768]{1,0:T(8,128)S(1)}, u32[]{:S(2)}, u32[]{:S(2)}) %collective-permute-start.43) | collective-permute-done | bytes 49184 | tf_op jit(solution)/shard_map/ppermute | solution.py:999
  216.0 1.0 collective-permute-start.47
  217.0 1.5 collective-permute-start.48
  218.4 1.5 collective-permute-start.49
  219.9 3.4 %collective-permute-start.51 = (f32[16,768]{1,0:T(8,128)S(1)}, f32[16,768]{1,0:T(8,128)S(1)}, u32[]{:S(2)}, u32[]{:S(2)}) collective-permute-start(f32[16,768]{1,0:T(8,128)S(1)} %get-tuple-element.343), channel_id=1, source_target_pairs={{0,2},{1,3},{2,0},{3,1},{4,6},{5,7},{6,4},{7,5},{8,10},{9,11},{10,... | collective-permute-start | bytes 147464 | tf_op jit(solution)/shard_map/ppermute | solution.py:1185
  223.3 2.2 collective-permute-done.51
  225.5 1.9 collective-permute-done.52
  229.1 7.1 %collective-permute-done.48.refs_2_ = bf16[3,96,768]{2,1,0:T(8,128)(2,1)S(1)} collective-permute-done((bf16[3,96,768]{2,1,0:T(8,128)(2,1)S(1)}, bf16[3,96,768]{2,1,0:T(8,128)(2,1)S(1)}, u32[]{:S(2)}, u32[]{:S(2)}) %collective-permute-start.48) | collective-permute-done | bytes 442400 | tf_op jit(solution)/shard_map/ppermute | solution.py:998
  237.2 2.5 %shard_map.272 = (f32[576,768]{1,0:T(8,128)}, f32[192,768]{1,0:T(8,128)}, f32[768,768]{1,0:T(8,128)}, f32[768,768]{1,0:T(8,128)}) custom-call(s32[3]{0:T(128)S(1)} %pad_add_fusion.place, bf16[3,96,768]{2,1,0:T(8,128)(2,1)S(1)} %get-tuple-element.346.refs_0_, bf16[3,96,768]{2,1,0:T(8,128)(2,1)S(1)} %collective-permute-done.47.refs_1_, ...), custom_call_target="tpu_custom_call" | custom-call | bytes 5308416 | tf_op jit(solution)/shard_map/pallas_call | solution.py:943
  239.8 2.5 %shard_map.273 = (f32[576,768]{1,0:T(8,128)}, f32[192,768]{1,0:T(8,128)}, f32[768,768]{1,0:T(8,128)}, f32[768,768]{1,0:T(8,128)}) custom-call(s32[3]{0:T(128)S(1)} %pad_add_fusion.place, bf16[3,96,768]{2,1,0:T(8,128)(2,1)S(1)} %collective-permute-done.53.refs_0_, ...), custom_call_target="tpu_custom_call", output_to_operand_aliasing={{0}: (5, {}), {1}: (6, {}), {2}: (7, {}), {3}: (8, {})} | custom-call | bytes 5308416 | tf_op jit(solution)/shard_map/pallas_call | solution.py:943
  (129 shorter events, 17.1 us)
Async XLA Ops:
  4.3 15.5 %collective-permute-start.1 = (bf16[656,768]{1,0:T(8,128)(2,1)S(1)}, bf16[656,768]{1,0:T(8,128)(2,1)S(1)}, u32[]{:S(2)}, u32[]{:S(2)}) collective-permute-start(bf16[656,768]{1,0:T(8,128)(2,1)S(1)} %shard_map.254.normed.counts.rest_4_), channel_id=1, source_target_pairs={{0,4},{4,0},{1,5},{5,1},{2,6},{6,2},{3,7},{7,3},{8,12},{12,8},{9,1... | collective-permute-start | bytes 3022856 | tf_op jit(solution)/shard_map/ppermute | solution.py:1039
  6.8 13.0 %collective-permute-start = (bf16[208,768]{1,0:T(8,128)(2,1)S(1)}, bf16[208,768]{1,0:T(8,128)(2,1)S(1)}, u32[]{:S(2)}, u32[]{:S(2)}) collective-permute-start(bf16[208,768]{1,0:T(8,128)(2,1)S(1)} %get-tuple-element.194), channel_id=1, source_target_pairs={{0,1},{1,2},{2,3},{3,0},{4,6},{5,7},{6,4},{7,5},{8,9},{9,10},{10,1... | collective-permute-start | bytes 958472 | tf_op jit(solution)/shard_map/ppermute | solution.py:1038
  19.8 16.0 %collective-permute-start.5 = (bf16[576,768]{1,0:T(8,128)(2,1)S(1)}, bf16[576,768]{1,0:T(8,128)(2,1)S(1)}, u32[]{:S(2)}, u32[]{:S(2)}) collective-permute-start(bf16[576,768]{1,0:T(8,128)(2,1)S(1)} %bitcast.10), channel_id=1, source_target_pairs={{4,7},{5,4},{6,5},{7,6},{12,15},{13,12},{14,13},{15,14},{20,23},{2... | collective-permute-start | bytes 2654216 | tf_op jit(solution)/shard_map/ppermute | solution.py:1046
  20.5 27.7 %copy-start.12 = (bf16[640,768]{1,0:T(8,128)(2,1)S(1)}, bf16[640,768]{1,0:T(8,128)(2,1)}, u32[]{:S(2)}) copy-start(bf16[640,768]{1,0:T(8,128)(2,1)} %output_grad.1) | copy-start | bytes 2949124
  20.5 4.4 %collective-permute-start.6 = (bf16[208,768]{1,0:T(8,128)(2,1)S(1)}, bf16[208,768]{1,0:T(8,128)(2,1)S(1)}, u32[]{:S(2)}, u32[]{:S(2)}) collective-permute-start(bf16[208,768]{1,0:T(8,128)(2,1)S(1)} %get-tuple-element.199.tail.rest_1_), channel_id=1, source_target_pairs={{4,7},{5,4},{6,5},{7,6},{12,15},{13,12},{14,13},{15,14},{20,23},{2... | collective-permute-start | bytes 958472 | tf_op jit(solution)/shard_map/ppermute | solution.py:1047
  21.3 7.1 %collective-permute-start.2 = (bf16[208,768]{1,0:T(8,128)(2,1)S(1)}, bf16[208,768]{1,0:T(8,128)(2,1)S(1)}, u32[]{:S(2)}, u32[]{:S(2)}) collective-permute-start(bf16[208,768]{1,0:T(8,128)(2,1)S(1)} %collective-permute-done.near0.rest_5_.rest_0_), channel_id=1, source_target_pairs={{0,8},{8,0},{1,9},{9,1},{2,10},{10,2},{3,11},{11,3},{4,12},{12,4},... | collective-permute-start | bytes 958472 | tf_op jit(solution)/shard_map/ppermute | solution.py:997
  22.9 10.7 %collective-permute-start.3 = (bf16[208,768]{1,0:T(8,128)(2,1)S(1)}, bf16[208,768]{1,0:T(8,128)(2,1)S(1)}, u32[]{:S(2)}, u32[]{:S(2)}) collective-permute-start(bf16[208,768]{1,0:T(8,128)(2,1)S(1)} %collective-permute-done.near0.rest_5_.rest_0_), channel_id=1, source_target_pairs={{0,16},{16,0},{1,17},{17,1},{2,18},{18,2},{3,19},{19,3},{4,20},{20... | collective-permute-start | bytes 958472 | tf_op jit(solution)/shard_map/ppermute | solution.py:998
  24.4 9.2 %collective-permute-start.4 = (bf16[208,768]{1,0:T(8,128)(2,1)S(1)}, bf16[208,768]{1,0:T(8,128)(2,1)S(1)}, u32[]{:S(2)}, u32[]{:S(2)}) collective-permute-start(bf16[208,768]{1,0:T(8,128)(2,1)S(1)} %collective-permute-done.near0.rest_5_.rest_0_), channel_id=1, source_target_pairs={{0,24},{8,16},{16,8},{24,0},{1,25},{9,17},{17,9},{25,1},{2,26},{10... | collective-permute-start | bytes 958472 | tf_op jit(solution)/shard_map/ppermute | solution.py:999
  33.6 14.6 %collective-permute-start.7 = (bf16[384,768]{1,0:T(8,128)(2,1)S(1)}, bf16[384,768]{1,0:T(8,128)(2,1)S(1)}, u32[]{:S(2)}, u32[]{:S(2)}) collective-permute-start(bf16[384,768]{1,0:T(8,128)(2,1)S(1)} %shard_map.256), channel_id=1, source_target_pairs={{0,1},{1,2},{2,3},{3,0},{4,6},{5,7},{6,4},{7,5},{8,9},{9,10},{10,1... | collective-permute-start | bytes 1769480 | tf_op jit(solution)/shard_map/ppermute | solution.py:1048
  48.2 30.8 %copy-start.17 = (f32[768]{0:T(1024)S(1)}, f32[768]{0:T(1024)}, u32[]{:S(2)}) copy-start(f32[768]{0:T(1024)} %param.23) | copy-start | bytes 9220
  48.2 30.8 %copy-start.18 = (f32[768]{0:T(1024)S(1)}, f32[768]{0:T(1024)}, u32[]{:S(2)}) copy-start(f32[768]{0:T(1024)} %param.22) | copy-start | bytes 9220
  48.2 30.8 %copy-start.19 = (f32[768]{0:T(1024)S(1)}, f32[768]{0:T(1024)}, u32[]{:S(2)}) copy-start(f32[768]{0:T(1024)} %param.24) | copy-start | bytes 9220
  48.2 28.5 %collective-permute-start.11 = (bf16[640,768]{1,0:T(8,128)(2,1)S(1)}, bf16[640,768]{1,0:T(8,128)(2,1)S(1)}, u32[]{:S(2)}, u32[]{:S(2)}) collective-permute-start(bf16[640,768]{1,0:T(8,128)(2,1)S(1)} %copy-done.12), channel_id=1, source_target_pairs={{0,4},{4,0},{1,5},{5,1},{2,6},{6,2},{3,7},{7,3},{8,12},{12,8},{9,1... | collective-permute-start | bytes 2949128 | tf_op jit(solution)/shard_map/ppermute | solution.py:1054
  59.5 17.3 %collective-permute-start.8 = (bf16[640,768]{1,0:T(8,128)(2,1)S(1)}, bf16[640,768]{1,0:T(8,128)(2,1)S(1)}, u32[]{:S(2)}, u32[]{:S(2)}) collective-permute-start(bf16[640,768]{1,0:T(8,128)(2,1)S(1)} %get-tuple-element.209), channel_id=1, source_target_pairs={{0,4},{4,0},{1,5},{5,1},{2,6},{6,2},{3,7},{7,3},{8,12},{12,8},{9,1... | collective-permute-start | bytes 2949128 | tf_op jit(solution)/shard_map/ppermute | solution.py:1055
  59.6 15.7 %collective-permute-start.10 = (bf16[384,768]{1,0:T(8,128)(2,1)S(1)}, bf16[384,768]{1,0:T(8,128)(2,1)S(1)}, u32[]{:S(2)}, u32[]{:S(2)}) collective-permute-start(bf16[384,768]{1,0:T(8,128)(2,1)S(1)} %collective-permute-done.7.rest_0_), channel_id=1, source_target_pairs={{0,16},{16,0},{1,17},{17,1},{2,18},{18,2},{3,19},{19,3},{4,20},{20... | collective-permute-start | bytes 1769480 | tf_op jit(solution)/shard_map/ppermute | solution.py:1057
  61.1 15.7 %collective-permute-start.9 = (bf16[384,768]{1,0:T(8,128)(2,1)S(1)}, bf16[384,768]{1,0:T(8,128)(2,1)S(1)}, u32[]{:S(2)}, u32[]{:S(2)}) collective-permute-start(bf16[384,768]{1,0:T(8,128)(2,1)S(1)} %collective-permute-done.7.rest_0_), channel_id=1, source_target_pairs={{0,8},{8,0},{1,9},{9,1},{2,10},{10,2},{3,11},{11,3},{4,12},{12,4},... | collective-permute-start | bytes 1769480 | tf_op jit(solution)/shard_map/ppermute | solution.py:1056
  63.1 43.6 %collective-permute-start.15 = (bf16[1536,768]{1,0:T(8,128)(2,1)S(1)}, bf16[1536,768]{1,0:T(8,128)(2,1)S(1)}, u32[]{:S(2)}, u32[]{:S(2)}) collective-permute-start(bf16[1536,768]{1,0:T(8,128)(2,1)S(1)} %pad_maximum_fusion.rest_0_), channel_id=1, source_target_pairs={{4,7},{5,4},{6,5},{7,6},{12,15},{13,12},{14,13},{15,14},{20,23},{2... | collective-permute-start | bytes 7077896 | tf_op jit(solution)/shard_map/ppermute | solution.py:1058
  76.8 8.1 %collective-permute-start.12 = (bf16[192,768]{1,0:T(8,128)(2,1)S(1)}, bf16[192,768]{1,0:T(8,128)(2,1)S(1)}, u32[]{:S(2)}, u32[]{:S(2)}) collective-permute-start(bf16[192,768]{1,0:T(8,128)(2,1)S(1)} %slice.30), channel_id=1, source_target_pairs={{0,8},{8,0},{1,9},{9,1},{2,10},{10,2},{3,11},{11,3},{4,12},{12,4},... | collective-permute-start | bytes 884744 | tf_op jit(solution)/shard_map/ppermute | solution.py:1066
  78.6 9.1 %collective-permute-start.13 = (bf16[192,768]{1,0:T(8,128)(2,1)S(1)}, bf16[192,768]{1,0:T(8,128)(2,1)S(1)}, u32[]{:S(2)}, u32[]{:S(2)}) collective-permute-start(bf16[192,768]{1,0:T(8,128)(2,1)S(1)} %slice.31), channel_id=1, source_target_pairs={{0,16},{16,0},{1,17},{17,1},{2,18},{18,2},{3,19},{19,3},{4,20},{20... | collective-permute-start | bytes 884744 | tf_op jit(solution)/shard_map/ppermute | solution.py:1067
  87.7 2.9 %collective-permute-start.14 = (bf16[640,768]{1,0:T(8,128)(2,1)S(1)}, bf16[640,768]{1,0:T(8,128)(2,1)S(1)}, u32[]{:S(2)}, u32[]{:S(2)}) collective-permute-start(bf16[640,768]{1,0:T(8,128)(2,1)S(1)} %get-tuple-element.219.rest_6_.rest_4_), channel_id=1, source_target_pairs={{0,4},{4,0},{1,5},{5,1},{2,6},{6,2},{3,7},{7,3},{8,12},{12,8},{9,1... | collective-permute-start | bytes 2949128 | tf_op jit(solution)/shard_map/ppermute | solution.py:1079
  106.7 17.5 %copy-start.5 = (bf16[2,2,96,768]{3,2,1,0:T(8,128)(2,1)S(1)}, bf16[2,2,96,768]{3,2,1,0:T(8,128)(2,1)}, u32[]{:S(2)}) copy-start(bf16[2,2,96,768]{3,2,1,0:T(8,128)(2,1)} %get-tuple-element.249.refs_0_) | copy-start | bytes 1769476
  106.7 17.5 %copy-start.6 = (bf16[2,2,96,768]{3,2,1,0:T(8,128)(2,1)S(1)}, bf16[2,2,96,768]{3,2,1,0:T(8,128)(2,1)}, u32[]{:S(2)}) copy-start(bf16[2,2,96,768]{3,2,1,0:T(8,128)(2,1)} %get-tuple-element.250.refs_1_) | copy-start | bytes 1769476
  106.8 16.4 %collective-permute-start.18 = (bf16[640,768]{1,0:T(8,128)(2,1)}, bf16[640,768]{1,0:T(8,128)(2,1)S(1)}, u32[]{:S(2)}, u32[]{:S(2)}) collective-permute-start(bf16[640,768]{1,0:T(8,128)(2,1)} %get-tuple-element.244), channel_id=1, source_target_pairs={{0,4},{4,0},{1,5},{5,1},{2,6},{6,2},{3,7},{7,3},{8,12},{12,8},{9,1... | collective-permute-start | bytes 2949128 | tf_op jit(solution)/shard_map/ppermute | solution.py:1088
  107.2 16.0 %collective-permute-start.19 = (bf16[640,768]{1,0:T(8,128)(2,1)}, bf16[640,768]{1,0:T(8,128)(2,1)S(1)}, u32[]{:S(2)}, u32[]{:S(2)}) collective-permute-start(bf16[640,768]{1,0:T(8,128)(2,1)} %get-tuple-element.245), channel_id=1, source_target_pairs={{0,4},{4,0},{1,5},{5,1},{2,6},{6,2},{3,7},{7,3},{8,12},{12,8},{9,1... | collective-permute-start | bytes 2949128 | tf_op jit(solution)/shard_map/ppermute | solution.py:1089
  107.3 15.8 %collective-permute-start.16 = (bf16[2,2,96,768]{3,2,1,0:T(8,128)(2,1)}, bf16[2,2,96,768]{3,2,1,0:T(8,128)(2,1)S(1)}, u32[]{:S(2)}, u32[]{:S(2)}) collective-permute-start(bf16[2,2,96,768]{3,2,1,0:T(8,128)(2,1)} %get-tuple-element.242), channel_id=1, source_target_pairs={{0,8},{8,0},{1,9},{9,1},{2,10},{10,2},{3,11},{11,3},{4,12},{12,4},... | collective-permute-start | bytes 1769480 | tf_op jit(solution)/shard_map/ppermute | solution.py:1009
  107.6 15.5 %collective-permute-start.17 = (bf16[2,2,96,768]{3,2,1,0:T(8,128)(2,1)}, bf16[2,2,96,768]{3,2,1,0:T(8,128)(2,1)S(1)}, u32[]{:S(2)}, u32[]{:S(2)}) collective-permute-start(bf16[2,2,96,768]{3,2,1,0:T(8,128)(2,1)} %get-tuple-element.243), channel_id=1, source_target_pairs={{0,16},{16,0},{1,17},{17,1},{2,18},{18,2},{3,19},{19,3},{4,20},{20... | collective-permute-start | bytes 1769480 | tf_op jit(solution)/shard_map/ppermute | solution.py:1010
  123.2 2.8 %collective-permute-start.20 = (bf16[640,768]{1,0:T(8,128)(2,1)}, bf16[640,768]{1,0:T(8,128)(2,1)S(1)}, u32[]{:S(2)}, u32[]{:S(2)}) collective-permute-start(bf16[640,768]{1,0:T(8,128)(2,1)} %get-tuple-element.248), channel_id=1, source_target_pairs={{0,4},{4,0},{1,5},{5,1},{2,6},{6,2},{3,7},{7,3},{8,12},{12,8},{9,1... | collective-permute-start | bytes 2949128 | tf_op jit(solution)/shard_map/ppermute | solution.py:1098
  123.2 27.0 %collective-permute-start.24 = (bf16[2,4,2,96,768]{4,3,2,1,0:T(8,128)(2,1)}, bf16[2,4,2,96,768]{4,3,2,1,0:T(8,128)(2,1)S(1)}, u32[]{:S(2)}, u32[]{:S(2)}) collective-permute-start(bf16[2,4,2,96,768]{4,3,2,1,0:T(8,128)(2,1)} %get-tuple-element.267.refs_3_.refs_4_), channel_id=1, source_target_pairs={{7,4},{4,5},{5,6},{6,7},{15,12},{12,13},{13,14},{14,15},{23,20},{2... | collective-permute-start | bytes 7077896 | tf_op jit(solution)/shard_map/ppermute | solution.py:1097
  130.2 32.0 %copy-start.1 = (bf16[640,768]{1,0:T(8,128)(2,1)}, bf16[640,768]{1,0:T(8,128)(2,1)S(1)}, u32[]{:S(2)}) copy-start(bf16[640,768]{1,0:T(8,128)(2,1)S(1)} %get-tuple-element.279.rest_6_.grad_first) | copy-start | bytes 2949124
  130.2 4.3 %collective-permute-start.21 = (bf16[640,768]{1,0:T(8,128)(2,1)S(1)}, bf16[640,768]{1,0:T(8,128)(2,1)S(1)}, u32[]{:S(2)}, u32[]{:S(2)}) collective-permute-start(bf16[640,768]{1,0:T(8,128)(2,1)S(1)} %get-tuple-element.279.rest_6_.grad_first), channel_id=1, source_target_pairs={{0,4},{4,0},{1,5},{5,1},{2,6},{6,2},{3,7},{7,3},{8,12},{12,8},{9,1... | collective-permute-start | bytes 2949128 | tf_op jit(solution)/shard_map/ppermute | solution.py:1108
  134.5 15.8 %collective-permute-start.25 = (bf16[640,768]{1,0:T(8,128)(2,1)S(1)}, bf16[640,768]{1,0:T(8,128)(2,1)S(1)}, u32[]{:S(2)}, u32[]{:S(2)}) collective-permute-start(bf16[640,768]{1,0:T(8,128)(2,1)S(1)} %copy-done.21), channel_id=1, source_target_pairs={{0,4},{4,0},{1,5},{5,1},{2,6},{6,2},{3,7},{7,3},{8,12},{12,8},{9,1... | collective-permute-start | bytes 2949128 | tf_op jit(solution)/shard_map/ppermute | solution.py:1109
  134.8 15.4 %collective-permute-start.22 = (bf16[2,96,768]{2,1,0:T(8,128)(2,1)S(1)}, bf16[2,96,768]{2,1,0:T(8,128)(2,1)S(1)}, u32[]{:S(2)}, u32[]{:S(2)}) collective-permute-start(bf16[2,96,768]{2,1,0:T(8,128)(2,1)S(1)} %get-tuple-element.253), channel_id=1, source_target_pairs={{0,16},{16,0},{1,17},{17,1},{2,18},{18,2},{3,19},{19,3},{4,20},{20... | collective-permute-start | bytes 884744 | tf_op jit(solution)/shard_map/ppermute | solution.py:1014
  136.4 13.8 %collective-permute-start.23 = (bf16[2,96,768]{2,1,0:T(8,128)(2,1)S(1)}, bf16[2,96,768]{2,1,0:T(8,128)(2,1)S(1)}, u32[]{:S(2)}, u32[]{:S(2)}) collective-permute-start(bf16[2,96,768]{2,1,0:T(8,128)(2,1)S(1)} %get-tuple-element.254), channel_id=1, source_target_pairs={{0,8},{8,0},{1,9},{9,1},{2,10},{10,2},{3,11},{11,3},{4,12},{12,4},... | collective-permute-start | bytes 884744 | tf_op jit(solution)/shard_map/ppermute | solution.py:1014
  151.0 23.4 %collective-permute-start.26 = (bf16[4,2,96,768]{3,2,1,0:T(8,128)(2,1)S(1)}, bf16[4,2,96,768]{3,2,1,0:T(8,128)(2,1)S(1)}, u32[]{:S(2)}, u32[]{:S(2)}) collective-permute-start(bf16[4,2,96,768]{3,2,1,0:T(8,128)(2,1)S(1)} %get-tuple-element.276), channel_id=1, source_target_pairs={{0,4},{4,0},{1,5},{5,1},{2,6},{6,2},{3,7},{7,3},{8,12},{12,8},{9,1... | collective-permute-start | bytes 3538952 | tf_op jit(solution)/shard_map/ppermute | solution.py:1124
  157.0 17.5 %collective-permute-start.31 = (bf16[2,2,96,768]{3,2,1,0:T(8,128)(2,1)S(1)}, bf16[2,2,96,768]{3,2,1,0:T(8,128)(2,1)S(1)}, u32[]{:S(2)}, u32[]{:S(2)}) collective-permute-start(bf16[2,2,96,768]{3,2,1,0:T(8,128)(2,1)S(1)} %get-tuple-element.278), channel_id=1, source_target_pairs={{1,0},{2,1},{3,2},{0,3},{6,4},{7,5},{4,6},{5,7},{9,8},{10,9},{11,1... | collective-permute-start | bytes 1769480 | tf_op jit(solution)/shard_map/ppermute | solution.py:1123
  158.7 15.7 %collective-permute-start.28 = (bf16[2,1,96,768]{3,2,1,0:T(8,128)(2,1)S(1)}, bf16[2,1,96,768]{3,2,1,0:T(8,128)(2,1)S(1)}, u32[]{:S(2)}, u32[]{:S(2)}) collective-permute-start(bf16[2,1,96,768]{3,2,1,0:T(8,128)(2,1)S(1)} %get-tuple-element.287), channel_id=1, source_target_pairs={{0,8},{8,0},{1,9},{9,1},{2,10},{10,2},{3,11},{11,3},{4,12},{12,4},... | collective-permute-start | bytes 884744 | tf_op jit(solution)/shard_map/ppermute | solution.py:1019
  160.3 14.2 %collective-permute-start.29 = (bf16[2,1,96,768]{3,2,1,0:T(8,128)(2,1)S(1)}, bf16[2,1,96,768]{3,2,1,0:T(8,128)(2,1)S(1)}, u32[]{:S(2)}, u32[]{:S(2)}) collective-permute-start(bf16[2,1,96,768]{3,2,1,0:T(8,128)(2,1)S(1)} %get-tuple-element.288), channel_id=1, source_target_pairs={{0,16},{16,0},{1,17},{17,1},{2,18},{18,2},{3,19},{19,3},{4,20},{20... | collective-permute-start | bytes 884744 | tf_op jit(solution)/shard_map/ppermute | solution.py:1020
  161.7 12.8 %collective-permute-start.30 = (bf16[2,1,96,768]{3,2,1,0:T(8,128)(2,1)S(1)}, bf16[2,1,96,768]{3,2,1,0:T(8,128)(2,1)S(1)}, u32[]{:S(2)}, u32[]{:S(2)}) collective-permute-start(bf16[2,1,96,768]{3,2,1,0:T(8,128)(2,1)S(1)} %get-tuple-element.289), channel_id=1, source_target_pairs={{0,24},{8,16},{16,8},{24,0},{1,25},{9,17},{17,9},{25,1},{2,26},{10... | collective-permute-start | bytes 884744 | tf_op jit(solution)/shard_map/ppermute | solution.py:1021
  174.5 8.1 %collective-permute-start.32 = (bf16[640,768]{1,0:T(8,128)(2,1)S(1)}, bf16[640,768]{1,0:T(8,128)(2,1)S(1)}, u32[]{:S(2)}, u32[]{:S(2)}) collective-permute-start(bf16[640,768]{1,0:T(8,128)(2,1)S(1)} %get-tuple-element.291), channel_id=1, source_target_pairs={{0,4},{4,0},{1,5},{5,1},{2,6},{6,2},{3,7},{7,3},{8,12},{12,8},{9,1... | collective-permute-start | bytes 2949128 | tf_op jit(solution)/shard_map/ppermute | solution.py:1136
  178.0 5.2 %collective-permute-start.27 = (bf16[640,768]{1,0:T(8,128)(2,1)S(1)}, bf16[640,768]{1,0:T(8,128)(2,1)S(1)}, u32[]{:S(2)}, u32[]{:S(2)}) collective-permute-start(bf16[640,768]{1,0:T(8,128)(2,1)S(1)} %get-tuple-element.277), channel_id=1, source_target_pairs={{0,4},{4,0},{1,5},{5,1},{2,6},{6,2},{3,7},{7,3},{8,12},{12,8},{9,1... | collective-permute-start | bytes 2949128 | tf_op jit(solution)/shard_map/ppermute | solution.py:1133
  179.1 9.1 %collective-permute-start.37 = (bf16[2,96,768]{2,1,0:T(8,128)(2,1)S(1)}, bf16[2,96,768]{2,1,0:T(8,128)(2,1)S(1)}, u32[]{:S(2)}, u32[]{:S(2)}) collective-permute-start(bf16[2,96,768]{2,1,0:T(8,128)(2,1)S(1)} %get-tuple-element.308), channel_id=1, source_target_pairs={{0,4},{4,0},{1,5},{5,1},{2,6},{6,2},{3,7},{7,3},{8,12},{12,8},{9,1... | collective-permute-start | bytes 884744 | tf_op jit(solution)/shard_map/ppermute | solution.py:1144
  179.6 11.5 %collective-permute-start.34 = (bf16[2,1,96,768]{3,2,1,0:T(8,128)(2,1)S(1)}, bf16[2,1,96,768]{3,2,1,0:T(8,128)(2,1)S(1)}, u32[]{:S(2)}, u32[]{:S(2)}) collective-permute-start(bf16[2,1,96,768]{3,2,1,0:T(8,128)(2,1)S(1)} %get-tuple-element.299), channel_id=1, source_target_pairs={{0,8},{8,0},{1,9},{9,1},{2,10},{10,2},{3,11},{11,3},{4,12},{12,4},... | collective-permute-start | bytes 884744 | tf_op jit(solution)/shard_map/ppermute | solution.py:1019
  181.2 15.0 %collective-permute-start.35 = (bf16[2,1,96,768]{3,2,1,0:T(8,128)(2,1)S(1)}, bf16[2,1,96,768]{3,2,1,0:T(8,128)(2,1)S(1)}, u32[]{:S(2)}, u32[]{:S(2)}) collective-permute-start(bf16[2,1,96,768]{3,2,1,0:T(8,128)(2,1)S(1)} %get-tuple-element.300), channel_id=1, source_target_pairs={{0,16},{16,0},{1,17},{17,1},{2,18},{18,2},{3,19},{19,3},{4,20},{20... | collective-permute-start | bytes 884744 | tf_op jit(solution)/shard_map/ppermute | solution.py:1020
  182.6 16.1 %collective-permute-start.36 = (bf16[2,1,96,768]{3,2,1,0:T(8,128)(2,1)S(1)}, bf16[2,1,96,768]{3,2,1,0:T(8,128)(2,1)S(1)}, u32[]{:S(2)}, u32[]{:S(2)}) collective-permute-start(bf16[2,1,96,768]{3,2,1,0:T(8,128)(2,1)S(1)} %get-tuple-element.301), channel_id=1, source_target_pairs={{0,24},{8,16},{16,8},{24,0},{1,25},{9,17},{17,9},{25,1},{2,26},{10... | collective-permute-start | bytes 884744 | tf_op jit(solution)/shard_map/ppermute | solution.py:1021
  188.2 10.5 %collective-permute-start.33 = (f32[16,768]{1,0:T(8,128)S(1)}, f32[16,768]{1,0:T(8,128)S(1)}, u32[]{:S(2)}, u32[]{:S(2)}) collective-permute-start(f32[16,768]{1,0:T(8,128)S(1)} %get-tuple-element.297.refs_4_), channel_id=1, source_target_pairs={{0,4},{4,0},{1,5},{5,1},{2,6},{6,2},{3,7},{7,3},{8,12},{12,8},{9,1... | collective-permute-start | bytes 147464 | tf_op jit(solution)/shard_map/ppermute | solution.py:1158
  188.2 13.6 %collective-permute-start.39 = (bf16[2,1,96,768]{3,2,1,0:T(8,128)(2,1)S(1)}, bf16[2,1,96,768]{3,2,1,0:T(8,128)(2,1)S(1)}, u32[]{:S(2)}, u32[]{:S(2)}) collective-permute-start(bf16[2,1,96,768]{3,2,1,0:T(8,128)(2,1)S(1)} %get-tuple-element.315), channel_id=1, source_target_pairs={{1,0},{2,1},{3,2},{0,3},{6,4},{7,5},{4,6},{5,7},{9,8},{10,9},{11,1... | collective-permute-start | bytes 884744 | tf_op jit(solution)/shard_map/ppermute | solution.py:1143
  191.1 16.5 %collective-permute-start.44 = (bf16[2,96,768]{2,1,0:T(8,128)(2,1)S(1)}, bf16[2,96,768]{2,1,0:T(8,128)(2,1)S(1)}, u32[]{:S(2)}, u32[]{:S(2)}) collective-permute-start(bf16[2,96,768]{2,1,0:T(8,128)(2,1)S(1)} %get-tuple-element.328), channel_id=1, source_target_pairs={{0,8},{8,0},{1,9},{9,1},{2,10},{10,2},{3,11},{11,3},{4,12},{12,4},... | collective-permute-start | bytes 884744 | tf_op jit(solution)/shard_map/ppermute | solution.py:1019
  196.2 13.5 %collective-permute-start.45 = (bf16[2,96,768]{2,1,0:T(8,128)(2,1)S(1)}, bf16[2,96,768]{2,1,0:T(8,128)(2,1)S(1)}, u32[]{:S(2)}, u32[]{:S(2)}) collective-permute-start(bf16[2,96,768]{2,1,0:T(8,128)(2,1)S(1)} %get-tuple-element.329), channel_id=1, source_target_pairs={{0,16},{16,0},{1,17},{17,1},{2,18},{18,2},{3,19},{19,3},{4,20},{20... | collective-permute-start | bytes 884744 | tf_op jit(solution)/shard_map/ppermute | solution.py:1020
  198.7 11.9 %collective-permute-start.46 = (bf16[2,96,768]{2,1,0:T(8,128)(2,1)S(1)}, bf16[2,96,768]{2,1,0:T(8,128)(2,1)S(1)}, u32[]{:S(2)}, u32[]{:S(2)}) collective-permute-start(bf16[2,96,768]{2,1,0:T(8,128)(2,1)S(1)} %get-tuple-element.330), channel_id=1, source_target_pairs={{0,24},{8,16},{16,8},{24,0},{1,25},{9,17},{17,9},{25,1},{2,26},{10... | collective-permute-start | bytes 884744 | tf_op jit(solution)/shard_map/ppermute | solution.py:1021
  199.4 2.4 collective-permute-start.38
  202.5 12.3 %collective-permute-start.40 = (bf16[1,96,768]{2,1,0:T(8,128)(2,1)S(1)}, bf16[1,96,768]{2,1,0:T(8,128)(2,1)S(1)}, u32[]{:S(2)}, u32[]{:S(2)}) collective-permute-start(bf16[1,96,768]{2,1,0:T(8,128)(2,1)S(1)} %get-tuple-element.325), channel_id=1, source_target_pairs={{0,4},{4,0},{1,5},{5,1},{2,6},{6,2},{3,7},{7,3},{8,12},{12,8},{9,1... | collective-permute-start | bytes 442376 | tf_op jit(solution)/shard_map/ppermute | solution.py:1175
  207.1 4.2 %collective-permute-start.41 = (f32[16,768]{1,0:T(8,128)S(1)}, f32[16,768]{1,0:T(8,128)S(1)}, u32[]{:S(2)}, u32[]{:S(2)}) collective-permute-start(f32[16,768]{1,0:T(8,128)S(1)} %get-tuple-element.338.refs_8_), channel_id=1, source_target_pairs={{0,8},{8,0},{1,9},{9,1},{2,10},{10,2},{3,11},{11,3},{4,12},{12,4},... | collective-permute-start | bytes 147464 | tf_op jit(solution)/shard_map/ppermute | solution.py:997
  207.6 4.1 %collective-permute-start.42 = (f32[16,768]{1,0:T(8,128)S(1)}, f32[16,768]{1,0:T(8,128)S(1)}, u32[]{:S(2)}, u32[]{:S(2)}) collective-permute-start(f32[16,768]{1,0:T(8,128)S(1)} %get-tuple-element.338.refs_8_), channel_id=1, source_target_pairs={{0,16},{16,0},{1,17},{17,1},{2,18},{18,2},{3,19},{19,3},{4,20},{20... | collective-permute-start | bytes 147464 | tf_op jit(solution)/shard_map/ppermute | solution.py:998
  209.7 5.0 %collective-permute-start.43 = (f32[16,768]{1,0:T(8,128)S(1)}, f32[16,768]{1,0:T(8,128)S(1)}, u32[]{:S(2)}, u32[]{:S(2)}) collective-permute-start(f32[16,768]{1,0:T(8,128)S(1)} %get-tuple-element.338.refs_8_), channel_id=1, source_target_pairs={{0,24},{8,16},{16,8},{24,0},{1,25},{9,17},{17,9},{25,1},{2,26},{10... | collective-permute-start | bytes 147464 | tf_op jit(solution)/shard_map/ppermute | solution.py:999
  215.5 7.8 %collective-permute-start.50 = (f32[16,768]{1,0:T(8,128)S(1)}, f32[16,768]{1,0:T(8,128)S(1)}, u32[]{:S(2)}, u32[]{:S(2)}) collective-permute-start(f32[16,768]{1,0:T(8,128)S(1)} %get-tuple-element.343), channel_id=1, source_target_pairs={{0,1},{1,2},{2,3},{3,0},{4,5},{5,6},{6,7},{7,4},{8,9},{9,10},{10,1... | collective-permute-start | bytes 147464 | tf_op jit(solution)/shard_map/ppermute | solution.py:1185
  216.0 13.1 %collective-permute-start.47 = (bf16[3,96,768]{2,1,0:T(8,128)(2,1)S(1)}, bf16[3,96,768]{2,1,0:T(8,128)(2,1)S(1)}, u32[]{:S(2)}, u32[]{:S(2)}) collective-permute-start(bf16[3,96,768]{2,1,0:T(8,128)(2,1)S(1)} %get-tuple-element.346.refs_0_), channel_id=1, source_target_pairs={{0,8},{8,0},{1,9},{9,1},{2,10},{10,2},{3,11},{11,3},{4,12},{12,4},... | collective-permute-start | bytes 1327112 | tf_op jit(solution)/shard_map/ppermute | solution.py:997
  217.0 19.2 %collective-permute-start.48 = (bf16[3,96,768]{2,1,0:T(8,128)(2,1)S(1)}, bf16[3,96,768]{2,1,0:T(8,128)(2,1)S(1)}, u32[]{:S(2)}, u32[]{:S(2)}) collective-permute-start(bf16[3,96,768]{2,1,0:T(8,128)(2,1)S(1)} %get-tuple-element.346.refs_0_), channel_id=1, source_target_pairs={{0,16},{16,0},{1,17},{17,1},{2,18},{18,2},{3,19},{19,3},{4,20},{20... | collective-permute-start | bytes 1327112 | tf_op jit(solution)/shard_map/ppermute | solution.py:998
  218.4 17.7 %collective-permute-start.49 = (bf16[3,96,768]{2,1,0:T(8,128)(2,1)S(1)}, bf16[3,96,768]{2,1,0:T(8,128)(2,1)S(1)}, u32[]{:S(2)}, u32[]{:S(2)}) collective-permute-start(bf16[3,96,768]{2,1,0:T(8,128)(2,1)S(1)} %get-tuple-element.346.refs_0_), channel_id=1, source_target_pairs={{0,24},{8,16},{16,8},{24,0},{1,25},{9,17},{17,9},{25,1},{2,26},{10... | collective-permute-start | bytes 1327112 | tf_op jit(solution)/shard_map/ppermute | solution.py:999
  219.9 5.6 %collective-permute-start.51 = (f32[16,768]{1,0:T(8,128)S(1)}, f32[16,768]{1,0:T(8,128)S(1)}, u32[]{:S(2)}, u32[]{:S(2)}) collective-permute-start(f32[16,768]{1,0:T(8,128)S(1)} %get-tuple-element.343), channel_id=1, source_target_pairs={{0,2},{1,3},{2,0},{3,1},{4,6},{5,7},{6,4},{7,5},{8,10},{9,11},{10,... | collective-permute-start | bytes 147464 | tf_op jit(solution)/shard_map/ppermute | solution.py:1185
  223.3 4.1 %collective-permute-start.52 = (f32[16,768]{1,0:T(8,128)S(1)}, f32[16,768]{1,0:T(8,128)S(1)}, u32[]{:S(2)}, u32[]{:S(2)}) collective-permute-start(f32[16,768]{1,0:T(8,128)S(1)} %get-tuple-element.343), channel_id=1, source_target_pairs={{0,3},{1,0},{2,1},{3,2},{4,7},{5,4},{6,5},{7,6},{8,11},{9,8},{10,9... | collective-permute-start | bytes 147464 | tf_op jit(solution)/shard_map/ppermute | solution.py:1185
  236.1 3.5 %collective-permute-start.53 = (bf16[3,96,768]{2,1,0:T(8,128)(2,1)S(1)}, bf16[3,96,768]{2,1,0:T(8,128)(2,1)S(1)}, u32[]{:S(2)}, u32[]{:S(2)}) collective-permute-start(bf16[3,96,768]{2,1,0:T(8,128)(2,1)S(1)} %get-tuple-element.346.refs_0_), channel_id=1, source_target_pairs={{0,4},{4,0},{1,5},{5,1},{2,6},{6,2},{3,7},{7,3},{8,12},{12,8},{9,1... | collective-permute-start | bytes 1327112 | tf_op jit(solution)/shard_map/ppermute | solution.py:1197
  236.1 3.5 %collective-permute-start.54 = (bf16[3,96,768]{2,1,0:T(8,128)(2,1)S(1)}, bf16[3,96,768]{2,1,0:T(8,128)(2,1)S(1)}, u32[]{:S(2)}, u32[]{:S(2)}) collective-permute-start(bf16[3,96,768]{2,1,0:T(8,128)(2,1)S(1)} %collective-permute-done.47.refs_1_), channel_id=1, source_target_pairs={{0,4},{4,0},{1,5},{5,1},{2,6},{6,2},{3,7},{7,3},{8,12},{12,8},{9,1... | collective-permute-start | bytes 1327112 | tf_op jit(solution)/shard_map/ppermute | solution.py:1197
  236.7 3.0 %collective-permute-start.55 = (bf16[3,96,768]{2,1,0:T(8,128)(2,1)S(1)}, bf16[3,96,768]{2,1,0:T(8,128)(2,1)S(1)}, u32[]{:S(2)}, u32[]{:S(2)}) collective-permute-start(bf16[3,96,768]{2,1,0:T(8,128)(2,1)S(1)} %collective-permute-done.48.refs_2_), channel_id=1, source_target_pairs={{0,4},{4,0},{1,5},{5,1},{2,6},{6,2},{3,7},{7,3},{8,12},{12,8},{9,1... | collective-permute-start | bytes 1327112 | tf_op jit(solution)/shard_map/ppermute | solution.py:1197
  236.7 3.2 %collective-permute-start.56 = (bf16[3,96,768]{2,1,0:T(8,128)(2,1)S(1)}, bf16[3,96,768]{2,1,0:T(8,128)(2,1)S(1)}, u32[]{:S(2)}, u32[]{:S(2)}) collective-permute-start(bf16[3,96,768]{2,1,0:T(8,128)(2,1)S(1)} %collective-permute-done.49.refs_3_), channel_id=1, source_target_pairs={{0,4},{4,0},{1,5},{5,1},{2,6},{6,2},{3,7},{7,3},{8,12},{12,8},{9,1... | collective-permute-start | bytes 1327112 | tf_op jit(solution)/shard_map/ppermute | solution.py:1197
  (16 other events, 140.1 us)
